TPU v7x, 128 devices: a whole 4x4x4 slice. The times are simulated.
128 devices in a mesh: depth: 8 (over z, core), row: 16 (over x, y).
Axes of the slice: x: 4, y: 4, z: 4, core: 2. Of those that a mesh axis runs over, the one named last changes fastest.
Arguments:
- volume: float32 [256, 512, 4096], P('depth', 'row'), may hold values from 0.02 to 0.52
- palette: float32 [3, 8], replicated, may hold values from 0.15 to 4
Outputs:
- image: float32 [4, 512, 4096], P(None, 'row', 'depth')
All inputs are finite; a program needn't handle non-finite values.
Results may differ from a plain program's by a relative error of at most 0.0003.
Values sent between devices are 32-bit elements; how exact they have to be, the bound alone decides.
No kernel may reach another device: no remote copies, remote signals or barrier semaphores. Data moves between devices by JAX's collectives and lax.ppermute only.
A program may use at most 192 MiB of HBM per device.

v0:
```python
import jax
import jax.numpy as jnp
from jax import lax
from jax.sharding import PartitionSpec as P


def padded_2(cells, sides, width):
    for axis, dim in sides:
        count = lax.axis_size(axis)
        ends = count - 1
        head = lax.slice_in_dim(cells, 0, width, axis=dim)
        tail = lax.slice_in_dim(cells, cells.shape[dim] - width, cells.shape[dim], axis=dim)
        cells = jnp.concatenate(
            [
                lax.ppermute(tail, axis, [(i, (i + 1) % count) for i in range(ends)]),
                cells,
                lax.ppermute(head, axis, [((i + 1) % count, i) for i in range(ends)]),
            ],
            axis=dim,
        )
    return cells


def swapped(value, axis, stride):
    mask = 2**stride
    pairs = [(source, source ^ mask) for source in range(lax.axis_size(axis))]
    return lax.ppermute(value, axis, pairs)


def sample_terms(field, grad_z, grad_y, grad_x, palette, scale):
    along = 0.36 * grad_z + 0.48 * grad_y + 0.8 * grad_x
    square = grad_z * grad_z + grad_y * grad_y + grad_x * grad_x
    shade = 0.25 + 0.75 * jnp.abs(along) / jnp.sqrt(square + 0.04)
    bumps = palette.shape[1]
    colors = [jnp.zeros_like(field) for k in range(3)]
    for j in range(bumps):
        bump = jnp.exp(-jnp.square((bumps - 1) * field - j))
        for k in range(3):
            colors[k] = colors[k] + palette[k, j] * bump
    colors = [shade * c for c in colors]
    return (field * scale, colors)


def over_blend(front, back):
    color = front[:3] + front[3:4] * back[:3]
    passed = front[3:4] * back[3:4]
    return jnp.concatenate([color, passed], axis=0)


def on_device(volume, palette):
    depth_cells, rows, columns = volume.shape
    groups = lax.axis_size("depth")
    scale = 4.0 / (depth_cells * groups)
    padded = padded_2(volume, (("depth", 0), ("row", 1)), 1)
    grad_z = (padded[2:, 1:-1, :] - padded[:-2, 1:-1, :]) * 0.5
    grad_y = (padded[1:-1, 2:, :] - padded[1:-1, :-2, :]) * 0.5
    side_pad = jnp.pad(volume, ((0, 0), (0, 0), (1, 1)))
    grad_x = (side_pad[:, :, 2:] - side_pad[:, :, :-2]) * 0.5
    tau, colors = sample_terms(volume, grad_z, grad_y, grad_x, palette, scale)
    before = jnp.cumsum(tau, axis=0) - tau
    weight = jnp.exp(-before) * (1.0 - jnp.exp(-tau))
    channels = [jnp.sum(weight * c, axis=0) for c in colors]
    channels.append(jnp.exp(-jnp.sum(tau, axis=0)))
    partial_image = jnp.stack(channels, axis=0)
    block_width = columns // groups
    piece = partial_image.reshape(4, rows, groups, block_width)
    index = lax.axis_index("depth")
    for bit in range(groups.bit_length() - 1):
        mine = index // 2**bit % 2
        paired = piece.reshape(4, rows, piece.shape[2] // 2, 2, block_width)
        first = paired[:, :, :, 0, :]
        second = paired[:, :, :, 1, :]
        keep = jnp.where(mine == 0, first, second)
        outgoing = jnp.where(mine == 0, second, first)
        arrived = swapped(outgoing, "depth", bit)
        front = jnp.where(mine == 0, keep, arrived)
        back = jnp.where(mine == 0, arrived, keep)
        piece = over_blend(front, back)
    final = piece[:, :, 0, :]
    return jnp.concatenate([final[:3], 1.0 - final[3:4]], axis=0)


def solution(mesh):
    return jax.shard_map(
        on_device,
        mesh=mesh,
        in_specs=(P("depth", "row", None), P()),
        out_specs=P(None, "row", "depth"),
        check_vma=False,
    )
```

profile of v0, /device:TPU:6, one launch (start us, length us, event | category | flops | bytes accessed | tf_op | source)
XLA Modules:
  0.0 206.1 jit_solution(18436206571184149113)
XLA Ops:
  0.0 1.3 fusion.18
  1.3 1.8 collective-permute-start.1
  3.1 1.3 collective-permute-start
  4.6 7.4 %constant_dynamic-update-slice_fusion.1 = f32[34,32,4096]{2,1,0:T(8,128)S(1)} fusion(f32[34,32,4096]{2,1,0:T(8,128)S(1)} %constant_dynamic-update-slice_fusion.2, f32[32,32,4096]{2,1,0:T(8,128)} %param.2), kind=kLoop, calls=%fused_computation.59 | loop fusion | bytes 33554432
  12.0 6.1 %copy-done = f32[34,32,4096]{2,1,0:T(8,128)} copy-done((f32[34,32,4096]{2,1,0:T(8,128)}, f32[34,32,4096]{2,1,0:T(8,128)S(1)}, u32[]{:S(2)}) %copy-start) | copy-done | bytes 17825816
  18.1 1.9 fusion.17
  20.0 5.2 %collective-permute-start.2 = (f32[34,1,4096]{2,1,0:T(1,128)}, f32[34,1,4096]{2,1,0:T(1,128)S(1)}, u32[]{:S(2)}, u32[]{:S(2)}) collective-permute-start(f32[34,1,4096]{2,1,0:T(1,128)} %get-tuple-element.9), channel_id=1, source_target_pairs={{1,0},{2,1},{3,2},{4,3},{5,4},{6,5},{7,6},{8,7},{9,8},{10,9},{11,1... | collective-permute-start | bytes 1671176 | tf_op jit(solution)/shard_map/ppermute | solution.py:17
  25.2 1.9 collective-permute-start.3
  28.5 4.2 %collective-permute-done.2 = f32[34,1,4096]{2,1,0:T(1,128)S(1)} collective-permute-done((f32[34,1,4096]{2,1,0:T(1,128)}, f32[34,1,4096]{2,1,0:T(1,128)S(1)}, u32[]{:S(2)}, u32[]{:S(2)}) %collective-permute-start.2) | collective-permute-done | bytes 557088 | tf_op jit(solution)/shard_map/ppermute | solution.py:17
  32.6 6.5 %collective-permute-done.3 = f32[34,1,4096]{2,1,0:T(1,128)S(1)} collective-permute-done((f32[34,1,4096]{2,1,0:T(1,128)S(1)}, f32[34,1,4096]{2,1,0:T(1,128)S(1)}, u32[]{:S(2)}, u32[]{:S(2)}) %collective-permute-start.3) | collective-permute-done | bytes 557088 | tf_op jit(solution)/shard_map/ppermute | solution.py:15
  39.9 79.6 %multiply_reduce_fusion = (f32[32,4096]{1,0:T(8,128)S(1)}, f32[32,4096]{1,0:T(8,128)S(1)}, f32[32,4096]{1,0:T(8,128)S(1)}, f32[32,32,4096]{2,1,0:T(8,128)}, f32[32,32,4096]{2,1,0:T(8,128)}) fusion(f32[32,32,4096]{2,1,0:T(8,128)} %param.2, f32[]{:T(128)} %bitcast.23, f32[]{:T(128)} %bitcast.22, f32[]{:T(128)} %bitcast.21, f32[]{:T(128)} %bitcast.20, ...), kind=kOutput, calls=%fused_computation.6 | output fusion | flops 519700480 | bytes 88678400 | tf_op jit(solution)/shard_map/jit(cumsum)/reduce_window_sum | solution.py:60
  119.5 35.1 %multiply_reduce_fusion.2 = f32[32,4096]{1,0:T(8,128)S(1)} fusion(f32[32,32,4096]{2,1,0:T(8,128)} %get-tuple-element.52, f32[32,32,4096]{2,1,0:T(8,128)} %get-tuple-element.8, f32[32,32,4096]{2,1,0:T(8,128)} %param.2, f32[]{:T(128)} %bitcast.7, f32[]{:T(128)} %bitcast.6, f32[]{:T(128)} %bitcast.5, f32[]{:T(128)} %bitcast.4, f32[]{:T(128)} %bitcast.3, ...), kind=kLoop, calls=%fused_computation.8 | loop fusion | flops 176029696 | bytes 50855968 | tf_op jit(solution)/shard_map/reduce_sum | solution.py:62
  155.1 0.8 constant_dynamic-update-slice_fusion.6
  157.3 0.8 constant_dynamic-update-slice_fusion.5
  158.2 0.8 constant_dynamic-update-slice_fusion.4
  159.0 0.8 constant_dynamic-update-slice_fusion.3
  159.8 4.4 %fusion.19 = (f32[4,32,4,1,512]{4,3,2,1,0:T(1,128)S(1)}, f32[4,32,4,1,512]{4,3,2,1,0:T(1,128)S(1)}, f32[4,32,4,1,512]{4,3,2,1,0:T(1,128)S(1)}) fusion(f32[4,32,4,2,512]{4,3,2,1,0:T(2,128)} %constant_dynamic-update-slice_fusion.3, pred[]{:T(512)S(6)} %eq.12), kind=kLoop, calls=%fused_computation.68 | loop fusion | flops 262144 | bytes 5242881 | tf_op jit(solution)/shard_map/slice | solution.py:71
  164.5 5.4 %collective-permute-start.4 = (f32[4,32,4,512]{3,2,1,0:T(4,128)S(1)}, f32[4,32,4,512]{3,2,1,0:T(4,128)}, u32[]{:S(2)}, u32[]{:S(2)}) collective-permute-start(f32[4,32,4,512]{3,2,1,0:T(4,128)S(1)} %bitcast.100), channel_id=1, source_target_pairs={{0,16},{16,0},{32,48},{48,32},{64,80},{80,64},{96,112},{112,96},{1... | collective-permute-start | bytes 3145736 | tf_op jit(solution)/shard_map/ppermute | solution.py:27
  170.0 2.4 %collective-permute-done.4 = f32[4,32,4,512]{3,2,1,0:T(4,128)} collective-permute-done((f32[4,32,4,512]{3,2,1,0:T(4,128)S(1)}, f32[4,32,4,512]{3,2,1,0:T(4,128)}, u32[]{:S(2)}, u32[]{:S(2)}) %collective-permute-start.4) | collective-permute-done | bytes 1048608 | tf_op jit(solution)/shard_map/ppermute | solution.py:27
  172.4 1.8 broadcast_select_fusion.2
  175.2 8.1 %collective-permute-start.5 = (f32[4,32,2,512]{3,1,2,0:T(8,128)S(1)}, f32[4,32,2,512]{3,1,2,0:T(8,128)S(1)}, u32[]{:S(2)}, u32[]{:S(2)}) collective-permute-start(f32[4,32,2,512]{3,1,2,0:T(8,128)S(1)} %select_bitcast_fusion), channel_id=1, source_target_pairs={{0,32},{16,48},{32,0},{48,16},{64,96},{80,112},{96,64},{112,80},{1... | collective-permute-start | bytes 1572872 | tf_op jit(solution)/shard_map/ppermute | solution.py:27
  183.3 12.2 %collective-permute-done.5 = f32[4,32,2,512]{3,1,2,0:T(8,128)S(1)} collective-permute-done((f32[4,32,2,512]{3,1,2,0:T(8,128)S(1)}, f32[4,32,2,512]{3,1,2,0:T(8,128)S(1)}, u32[]{:S(2)}, u32[]{:S(2)}) %collective-permute-start.5) | collective-permute-done | bytes 524320 | tf_op jit(solution)/shard_map/ppermute | solution.py:27
  195.9 3.5 %collective-permute-start.6 = (f32[4,32,1,512]{3,1,0,2:T(8,128)S(1)}, f32[4,32,1,512]{3,1,0,2:T(8,128)S(1)}, u32[]{:S(2)}, u32[]{:S(2)}) collective-permute-start(f32[4,32,1,512]{3,1,0,2:T(8,128)S(1)} %select_bitcast_fusion.1), channel_id=1, source_target_pairs={{0,64},{16,80},{32,96},{48,112},{64,0},{80,16},{96,32},{112,48},{1... | collective-permute-start | bytes 786440 | tf_op jit(solution)/shard_map/ppermute | solution.py:27
  199.4 5.9 %collective-permute-done.6 = f32[4,32,1,512]{3,1,0,2:T(8,128)S(1)} collective-permute-done((f32[4,32,1,512]{3,1,0,2:T(8,128)S(1)}, f32[4,32,1,512]{3,1,0,2:T(8,128)S(1)}, u32[]{:S(2)}, u32[]{:S(2)}) %collective-permute-start.6) | collective-permute-done | bytes 262176 | tf_op jit(solution)/shard_map/ppermute | solution.py:27
  (31 shorter events, 6.7 us)
Async XLA Ops:
  1.3 3.3 %collective-permute-start.1 = (f32[1,32,4096]{2,1,0:T(8,128)S(1)}, f32[1,32,4096]{2,1,0:T(8,128)S(1)}, u32[]{:S(2)}, u32[]{:S(2)}) collective-permute-start(f32[1,32,4096]{2,1,0:T(8,128)S(1)} %get-tuple-element.12), channel_id=1, source_target_pairs={{0,16},{16,32},{32,48},{48,64},{64,80},{80,96},{96,112},{1,17},{17... | collective-permute-start | bytes 1572872 | tf_op jit(solution)/shard_map/ppermute | solution.py:15
  3.1 8.9 %collective-permute-start = (f32[1,32,4096]{2,1,0:T(8,128)S(1)}, f32[1,32,4096]{2,1,0:T(8,128)S(1)}, u32[]{:S(2)}, u32[]{:S(2)}) collective-permute-start(f32[1,32,4096]{2,1,0:T(8,128)S(1)} %get-tuple-element.11), channel_id=1, source_target_pairs={{16,0},{32,16},{48,32},{64,48},{80,64},{96,80},{112,96},{17,1},{33... | collective-permute-start | bytes 1572872 | tf_op jit(solution)/shard_map/ppermute | solution.py:17
  4.6 22.5 %copy-start.2 = (f32[3,8]{1,0:T(4,128)S(1)}, f32[3,8]{1,0:T(4,128)}, u32[]{:S(2)}) copy-start(f32[3,8]{1,0:T(4,128)} %param.3) | copy-start | bytes 292
  12.0 6.1 %copy-start = (f32[34,32,4096]{2,1,0:T(8,128)}, f32[34,32,4096]{2,1,0:T(8,128)S(1)}, u32[]{:S(2)}) copy-start(f32[34,32,4096]{2,1,0:T(8,128)S(1)} %constant_dynamic-update-slice_fusion) | copy-start | bytes 53477380
  20.0 12.7 %collective-permute-start.2 = (f32[34,1,4096]{2,1,0:T(1,128)}, f32[34,1,4096]{2,1,0:T(1,128)S(1)}, u32[]{:S(2)}, u32[]{:S(2)}) collective-permute-start(f32[34,1,4096]{2,1,0:T(1,128)} %get-tuple-element.9), channel_id=1, source_target_pairs={{1,0},{2,1},{3,2},{4,3},{5,4},{6,5},{7,6},{8,7},{9,8},{10,9},{11,1... | collective-permute-start | bytes 1671176 | tf_op jit(solution)/shard_map/ppermute | solution.py:17
  25.2 14.0 %collective-permute-start.3 = (f32[34,1,4096]{2,1,0:T(1,128)S(1)}, f32[34,1,4096]{2,1,0:T(1,128)S(1)}, u32[]{:S(2)}, u32[]{:S(2)}) collective-permute-start(f32[34,1,4096]{2,1,0:T(1,128)S(1)} %get-tuple-element.10), channel_id=1, source_target_pairs={{0,1},{1,2},{2,3},{3,4},{4,5},{5,6},{6,7},{7,8},{8,9},{9,10},{10,1... | collective-permute-start | bytes 1671176 | tf_op jit(solution)/shard_map/ppermute | solution.py:15
  39.1 0.8 copy-start.1
  164.5 7.9 %collective-permute-start.4 = (f32[4,32,4,512]{3,2,1,0:T(4,128)S(1)}, f32[4,32,4,512]{3,2,1,0:T(4,128)}, u32[]{:S(2)}, u32[]{:S(2)}) collective-permute-start(f32[4,32,4,512]{3,2,1,0:T(4,128)S(1)} %bitcast.100), channel_id=1, source_target_pairs={{0,16},{16,0},{32,48},{48,32},{64,80},{80,64},{96,112},{112,96},{1... | collective-permute-start | bytes 3145736 | tf_op jit(solution)/shard_map/ppermute | solution.py:27
  175.2 20.3 %collective-permute-start.5 = (f32[4,32,2,512]{3,1,2,0:T(8,128)S(1)}, f32[4,32,2,512]{3,1,2,0:T(8,128)S(1)}, u32[]{:S(2)}, u32[]{:S(2)}) collective-permute-start(f32[4,32,2,512]{3,1,2,0:T(8,128)S(1)} %select_bitcast_fusion), channel_id=1, source_target_pairs={{0,32},{16,48},{32,0},{48,16},{64,96},{80,112},{96,64},{112,80},{1... | collective-permute-start | bytes 1572872 | tf_op jit(solution)/shard_map/ppermute | solution.py:27
  195.9 9.4 %collective-permute-start.6 = (f32[4,32,1,512]{3,1,0,2:T(8,128)S(1)}, f32[4,32,1,512]{3,1,0,2:T(8,128)S(1)}, u32[]{:S(2)}, u32[]{:S(2)}) collective-permute-start(f32[4,32,1,512]{3,1,0,2:T(8,128)S(1)} %select_bitcast_fusion.1), channel_id=1, source_target_pairs={{0,64},{16,80},{32,96},{48,112},{64,0},{80,16},{96,32},{112,48},{1... | collective-permute-start | bytes 786440 | tf_op jit(solution)/shard_map/ppermute | solution.py:27
where the time goes:
time: 207 us; the launch traced here: 206 us
  other arithmetic  123 us (59%)
  waiting for transfers between devices  31.3 us (15%)
  starting transfers between devices  27.2 us (13%)
  local copies, waits for them, and re-layouts  24.5 us (12%)
    another operation x1, other arithmetic, on_device(): before = jnp.cumsum(tau, axis=0) - tau  79.6 us
    reduce_sum x1, other arithmetic, on_device(): channels = [jnp.sum(weight * c, axis=0) for c in colors]  35.1 us
    ppermute x3, waiting for transfers between devices, swapped(): return lax.ppermute(value, axis, pairs)  20.5 us
    unnamed x12, local copies, waits for them, and re-layouts  17.1 us
    ppermute x3, starting transfers between devices, swapped(): return lax.ppermute(value, axis, pairs)  17 us
    ppermute x2, waiting for transfers between devices, padded_2(): lax.ppermute(tail, axis, [(i, (i + 1) % count) for i in range(ends)])  6.66 us
    ppermute x2, starting transfers between devices, padded_2(): lax.ppermute(head, axis, [((i + 1) % count, i) for i in range(ends)])  6.47 us
    slice x1, other arithmetic, on_device(): first = paired[:, :, :, 0, :]  4.4 us
  transfers between devices with their start and end apart: 7, of which 6 were waited for; matrix products, arithmetic and copies ran while one was open for 4% of the time, Pallas kernels for 0%

commit v1 on v0

v1 whole, which is shorter than its diff:
```python
import functools
import math

import jax
import jax.numpy as jnp
from jax import lax
from jax.experimental import pallas as pl
from jax.experimental.pallas import tpu as pltpu
from jax.sharding import PartitionSpec as P

LANES = 128
SUBLANES = 8
LOG2E = math.log2(math.e)
TO_Y = 4.0 / 3.0
TO_X = 20.0 / 9.0
AMBIENT = 0.25 / 0.27
VMEM_BYTES = 58 * 2**20


def lane_masks():
    lane = lax.broadcasted_iota(jnp.int32, (SUBLANES, LANES), 1)
    return lane == 0, lane == LANES - 1


def shade_of(dz, dy, dx):
    along = jnp.abs(dz + TO_Y * dy + TO_X * dx)
    square = (dz * dz + 0.16) + (dy * dy + dx * dx)
    return along * lax.rsqrt(square) + AMBIENT


def across(left, here, right, first, last):
    after = pltpu.roll(jnp.where(first, right, here), LANES - 1, 1)
    before = pltpu.roll(jnp.where(last, left, here), 1, 1)
    return after - before


def add_bumps(moments, amount, field):
    ratio = jnp.exp2(field * (14 * LOG2E))
    amount = amount * jnp.exp2(field * field * (-49 * LOG2E))
    out = []
    for j, moment in enumerate(moments):
        out.append(amount if moment is None else moment + amount)
        if j + 1 < len(moments):
            amount = amount * ratio
    return out


def coefficients(palette_ref):
    bumps = palette_ref.shape[1]
    return [[palette_ref[k, j] * jnp.float32(0.27 * math.exp(-j * j)) for j in range(bumps)] for k in range(3)]


def contracted(coef, moments):
    out = []
    for k in range(3):
        total = moments[0] * coef[k][0]
        for j in range(1, len(moments)):
            total = total + moments[j] * coef[k][j]
        out.append(total)
    return out


def sample_kernel(volume_ref, prev_ref, next_ref, edge_ref, early_ref, palette_ref, *refs, mode, scale, depth):
    planes, rows, columns = volume_ref.shape
    tiles = columns // LANES
    if mode == "A":
        out_ref, vb, sem = refs
    elif mode == "B":
        keep_ref, send_ref, vb, vs, sem, sem_s = refs
    else:
        keep_ref, send_ref, vb, sem = refs
    first_row, count, at = {"A": (0, 24, 0), "B": (8, 24, 0), "C": (0, 16, 8), "D": (16, 16, 0)}[mode]
    mid = pl.ds(SUBLANES, SUBLANES)

    def tile_lanes(c):
        return pl.ds(pl.multiple_of(c * LANES, LANES), LANES)

    def copies(c):
        out = [
            pltpu.make_async_copy(
                volume_ref.at[:, pl.ds(first_row, count), tile_lanes(c)],
                vb.at[c + 1, :, pl.ds(at, count), :],
                sem.at[c],
            )
        ]
        if mode == "B":
            for i, z in enumerate((0, planes - 1)):
                out.append(
                    pltpu.make_async_copy(
                        volume_ref.at[z, pl.ds(0, 24), tile_lanes(c)],
                        vs.at[c + 1, i],
                        sem_s.at[c, i],
                    )
                )
        return out

    def begin(c, _):
        for copy in copies(c):
            copy.start()
        return 0

    lax.fori_loop(0, tiles, begin, 0)
    zero = jnp.zeros((planes, SUBLANES, LANES), jnp.float32)
    for c in (0, tiles + 1):
        vb[c, :, 8:16, :] = zero
        if mode == "B":
            vs[c, :, 8:16, :] = zero[:2]
    if mode in "CD":
        row = 7 if mode == "C" else 16

        def place(c, _):
            for z in range(planes):
                vb[c + 1, z, row : row + 1, :] = edge_ref[z : z + 1, tile_lanes(c)]
            return 0

        lax.fori_loop(0, tiles, place, 0)
    first, last = lane_masks()
    coef = coefficients(palette_ref)
    core = lax.axis_index(depth) % 2
    for copy in copies(0):
        copy.wait()

    def store(c, values, where):
        block = c // (tiles // 8)
        at_lane = pl.ds(pl.multiple_of((block // 2) * (columns // 8) + (c % (tiles // 8)) * LANES, LANES), LANES)

        @pl.when(block % 2 == core)
        def _():
            for k, value in enumerate(values):
                keep_ref[k, where, at_lane] = value

        @pl.when(block % 2 != core)
        def _():
            for k, value in enumerate(values):
                send_ref[k, where, at_lane] = value

    main_row = {"A": 8, "B": 16, "C": 0, "D": 24}[mode]
    inner = mode == "A"

    def body(c, _):
        @pl.when(c < tiles - 1)
        def _():
            for copy in copies(c + 1):
                copy.wait()

        moments = [None] * 8
        total = jnp.zeros((SUBLANES, LANES), jnp.float32)
        passed = jnp.ones((SUBLANES, LANES), jnp.float32)
        for z in range(planes):
            here = vb[c + 1, z, mid, :]
            total = total + here
            after = jnp.exp2(total * (-scale * LOG2E))
            if not (inner and z in (0, planes - 1)):
                up = vb[c + 1, z + 1, mid, :] if z < planes - 1 else next_ref[pl.ds(main_row, 8), tile_lanes(c)]
                down = vb[c + 1, z - 1, mid, :] if z > 0 else prev_ref[pl.ds(main_row, 8), tile_lanes(c)]
                dy = vb[c + 1, z, pl.ds(9, 8), :] - vb[c + 1, z, pl.ds(7, 8), :]
                dx = across(vb[c, z, mid, :], here, vb[c + 2, z, mid, :], first, last)
                moments = add_bumps(moments, (passed - after) * shade_of(up - down, dy, dx), here)
            passed = after
        colors = contracted(coef, moments)
        if mode == "A":
            for k in range(3):
                out_ref[k, :, tile_lanes(c)] = colors[k]
            out_ref[3, :, tile_lanes(c)] = passed
            return 0
        if mode == "B":
            store(c, colors + [passed], pl.ds(8, 8))
            moments = [None] * 8
            passed = early_ref[3, :, tile_lanes(c)]
            for i, z in enumerate((0, planes - 1)):
                here = vs[c + 1, i, mid, :]
                up = vb[c + 1, 1, pl.ds(0, 8), :] if i == 0 else next_ref[pl.ds(8, 8), tile_lanes(c)]
                down = prev_ref[pl.ds(8, 8), tile_lanes(c)] if i == 0 else vb[c + 1, planes - 2, pl.ds(0, 8), :]
                dy = vs[c + 1, i, pl.ds(9, 8), :] - vs[c + 1, i, pl.ds(7, 8), :]
                dx = across(vs[c, i, mid, :], here, vs[c + 2, i, mid, :], first, last)
                if i == 0:
                    amount = 1.0 - jnp.exp2(here * (-scale * LOG2E))
                else:
                    amount = passed * (jnp.exp2(here * (scale * LOG2E)) - 1.0)
                moments = add_bumps(moments, amount * shade_of(up - down, dy, dx), here)
            colors = contracted(coef, moments)
            colors = [early_ref[k, :, tile_lanes(c)] + colors[k] for k in range(3)]
            store(c, colors + [passed], pl.ds(0, 8))
            return 0
        store(c, colors + [passed], pl.ds(0, 8))
        return 0

    lax.fori_loop(0, tiles, body, 0)


def sample(mode, volume, before, after, edge, early, palette, scale, depth):
    planes, rows, columns = volume.shape
    tiles = columns // LANES
    vmem = pl.BlockSpec(memory_space=pltpu.VMEM)
    scratch = [pltpu.VMEM((tiles + 2, planes, 24, LANES), jnp.float32)]
    if mode == "B":
        scratch.append(pltpu.VMEM((tiles + 2, 2, 24, LANES), jnp.float32))
    scratch.append(pltpu.SemaphoreType.DMA((tiles,)))
    if mode == "B":
        scratch.append(pltpu.SemaphoreType.DMA((tiles, 2)))
    if mode == "A":
        out_shape = jax.ShapeDtypeStruct((4, 8, columns), jnp.float32)
        out_specs = vmem
    else:
        half = jax.ShapeDtypeStruct((4, 16 if mode == "B" else 8, columns // 2), jnp.float32)
        out_shape = (half, half)
        out_specs = (vmem, vmem)
    given = [volume, before, after, edge, early, palette]
    specs = [pl.BlockSpec(memory_space=pl.ANY)] + [vmem] * 4 + [pl.BlockSpec(memory_space=pltpu.SMEM)]
    used = [value is not None for value in given]

    def kernel(*refs):
        refs = list(refs)
        full = [refs.pop(0) if there else None for there in used]
        sample_kernel(*full, *refs, mode=mode, scale=scale, depth=depth)

    return pl.pallas_call(
        kernel,
        out_shape=out_shape,
        in_specs=[spec for spec, there in zip(specs, used) if there],
        out_specs=out_specs,
        scratch_shapes=scratch,
        compiler_params=pltpu.CompilerParams(vmem_limit_bytes=VMEM_BYTES),
        name="sample_" + mode,
    )(*[value for value in given if value is not None])


def merge_kernel(keep_ref, arrived_ref, *out_refs, depth):
    index = lax.axis_index(depth)
    chip = index // 2
    width = out_refs[0].shape[2]
    for core in range(2):
        front, back = (keep_ref, arrived_ref) if core == 0 else (arrived_ref, keep_ref)

        @pl.when(index % 2 == core)
        def _():
            for step, out_ref in enumerate(out_refs):
                lanes = pl.ds(pl.multiple_of(((chip + step) % 4) * width, width), width)
                passed = front[3, :, lanes]
                for k in range(3):
                    out_ref[k] = front[k, :, lanes] + passed * back[k, :, lanes]
                out_ref[3] = passed * back[3, :, lanes]


def merge(keep, arrived, depth):
    channels, rows, columns = keep.shape
    piece = jax.ShapeDtypeStruct((channels, rows, columns // 4), jnp.float32)
    return pl.pallas_call(
        functools.partial(merge_kernel, depth=depth),
        out_shape=(piece,) * 4,
        name="merge",
    )(keep, arrived)


def final_kernel(*refs, spans, depth):
    out_ref = refs[-1]
    chip = lax.axis_index(depth) // 2
    for mine in range(4):

        @pl.when(chip == mine)
        def _():
            for i, (row, count) in enumerate(spans):
                pieces = [refs[4 * i + (mine - z) % 4] for z in range(4)]
                passed = pieces[0][3]
                colors = [pieces[0][k] for k in range(3)]
                for piece in pieces[1:]:
                    for k in range(3):
                        colors[k] = colors[k] + passed * piece[k]
                    passed = passed * piece[3]
                for k in range(3):
                    out_ref[k, row : row + count, :] = colors[k]
                out_ref[3, row : row + count, :] = 1.0 - passed


def on_device(volume, palette):
    planes, rows, columns = volume.shape
    groups = lax.axis_size("depth")
    stacks = lax.axis_size("row")
    scale = 4.0 / (planes * groups)

    def shifted(value, axis, count, step):
        pairs = [(i, i + step) for i in range(count) if 0 <= i + step < count]
        return lax.ppermute(value, axis, pairs)

    before = shifted(volume[-1], "depth", groups, 1)
    after = shifted(volume[0], "depth", groups, -1)
    above = shifted(volume[:, -1, :], "row", stacks, 1)
    below = shifted(volume[:, 0, :], "row", stacks, -1)

    run = functools.partial(sample, scale=scale, depth="depth", palette=palette)
    early = run("A", volume, None, None, None, None)
    chunks = [
        (8, 16, run("B", volume, before, after, None, early)),
        (0, 8, run("C", volume, before, after, above, None)),
        (24, 8, run("D", volume, before, after, below, None)),
    ]
    pieces = []
    for _, _, (keep, send) in chunks:
        arrived = lax.ppermute(send, "depth", [(i, i ^ 1) for i in range(groups)])
        parts = merge(keep, arrived, "depth")
        for step in range(4):
            if step == 0:
                pieces.append(parts[0])
            else:
                pairs = [(i, (i + 2 * step) % groups) for i in range(groups)]
                pieces.append(lax.ppermute(parts[step], "depth", pairs))
    spans = [(row, count) for row, count, _ in chunks]
    return pl.pallas_call(
        functools.partial(final_kernel, spans=spans, depth="depth"),
        out_shape=jax.ShapeDtypeStruct((4, rows, columns // groups), jnp.float32),
        name="final",
    )(*pieces)


def solution(mesh):
    return jax.shard_map(
        on_device,
        mesh=mesh,
        in_specs=(P("depth", "row", None), P()),
        out_specs=P(None, "row", "depth"),
        check_vma=False,
    )
```

time: 207 us -> 102 us (0.49)
  other arithmetic: 123 us -> 0 us
  Pallas kernels: 0 us -> 56.1 us
  waiting for transfers between devices: 31.3 us -> 4.66 us
  local copies, waits for them, and re-layouts: 24.5 us -> 12.4 us
    another operation x1 -> x0, other arithmetic: 79.6 us -> none  [on_device(): before = jnp.cumsum(tau, axis=0) - tau]
    pallas_call x0 -> x8, Pallas kernels: none -> 56.1 us  [the longest x4 48.5 us: sample(): pl.pallas_call(kernel, out_shape=out_shape, in_specs=[spec for spec, ther...]
    reduce_sum x1 -> x0, other arithmetic: 35.1 us -> none  [on_device(): channels = [jnp.sum(weight * c, axis=0) for c in colors]]
    ppermute x7 -> x16, waiting for transfers between devices: 31.3 us -> 4.66 us  [the longest x9 4.65 us: on_device(): pieces.append(lax.ppermute(parts[step], 'depth', pairs))]
    unnamed x12 -> x34, local copies, waits for them, and re-layouts: 17.1 us -> 6.72 us
    slice x2 -> x0, other arithmetic: 4.44 us -> none  [the longest x1 4.4 us: on_device(): first = paired[:, :, :, 0, :]]
    select_n x5 -> x0, other arithmetic: 2.16 us -> none  [the longest x3 2.04 us: on_device(): front = jnp.where(mine == 0, keep, arrived)]
    another operation x4 -> x0, local copies, waits for them, and re-layouts: 2.15 us -> none  [on_device(): partial_image = jnp.stack(channels, axis=0)]
  transfers between devices with their start and end apart: 7 -> 16, of which waited for: 6 -> 1; matrix products, arithmetic and copies ran while one was open for 4% -> 5% of each run, Pallas kernels for 0% -> 54%
where the time goes in v1:
time: 102 us; the launch traced here: 101 us
  Pallas kernels  56.1 us (55%)
  starting transfers between devices  27.5 us (27%)
  local copies, waits for them, and re-layouts  12.4 us (12%)
  waiting for transfers between devices  4.66 us (5%)
    pallas_call x4, Pallas kernels, sample(): pl.pallas_call(kernel, out_shape=out_shape, in_specs=[spec for spec, ther...  48.5 us
    ppermute x9, starting transfers between devices, on_device(): pieces.append(lax.ppermute(parts[step], 'depth', pairs))  14.1 us
    ppermute x4, starting transfers between devices, shifted(): return lax.ppermute(value, axis, pairs)  10.2 us
    unnamed x34, local copies, waits for them, and re-layouts  6.72 us
    pallas_call x3, Pallas kernels, merge(): pl.pallas_call(functools.partial(merge_kernel, depth=depth), out_shape=(p...  5.58 us
    ppermute x9, waiting for transfers between devices, on_device(): pieces.append(lax.ppermute(parts[step], 'depth', pairs))  4.65 us
    slice x1, local copies, waits for them, and re-layouts, on_device(): below = shifted(volume[:, 0, :], 'row', stacks, -1)  4.41 us
    ppermute x3, starting transfers between devices, on_device(): arrived = lax.ppermute(send, 'depth', [(i, i ^ 1) for i in range(groups)])  3.27 us
  transfers between devices with their start and end apart: 16, of which 1 were waited for; matrix products, arithmetic and copies ran while one was open for 5% of the time, Pallas kernels for 54%

profile of v1, /device:TPU:6, one launch (start us, length us, event | category | flops | bytes accessed | tf_op | source)
XLA Modules:
  0.0 100.9 jit_solution(12797349299357882024)
XLA Ops:
  0.0 1.3 %slice_bitcast_fusion = (f32[32,4096]{1,0:T(8,128)S(1)}, f32[32,4096]{1,0:T(8,128)S(1)}) fusion(f32[32,32,4096]{2,1,0:T(8,128)} %refs_0_.7), kind=kLoop, calls=%fused_computation.2 | loop fusion | bytes 2097152 | tf_op jit(solution)/shard_map/squeeze | solution.py:286
  1.3 1.8 %collective-permute-start = (f32[32,4096]{1,0:T(8,128)S(1)}, f32[32,4096]{1,0:T(8,128)S(1)}, u32[]{:S(2)}, u32[]{:S(2)}) collective-permute-start(f32[32,4096]{1,0:T(8,128)S(1)} %get-tuple-element.44), channel_id=1, source_target_pairs={{0,16},{16,32},{32,48},{48,64},{64,80},{80,96},{96,112},{1,17},{17... | collective-permute-start | bytes 1572872 | tf_op jit(solution)/shard_map/ppermute | solution.py:283
  3.1 1.3 %collective-permute-start.1 = (f32[32,4096]{1,0:T(8,128)S(1)}, f32[32,4096]{1,0:T(8,128)S(1)}, u32[]{:S(2)}, u32[]{:S(2)}) collective-permute-start(f32[32,4096]{1,0:T(8,128)S(1)} %get-tuple-element.43), channel_id=1, source_target_pairs={{16,0},{32,16},{48,32},{64,48},{80,64},{96,80},{112,96},{17,1},{33... | collective-permute-start | bytes 1572872 | tf_op jit(solution)/shard_map/ppermute | solution.py:283
  4.4 4.4 %fusion = (f32[32,1,4096]{2,1,0:T(1,128)S(1)}, f32[32,1,4096]{2,1,0:T(1,128)S(1)}) fusion(f32[32,32,4096]{2,1,0:T(8,128)} %refs_0_.7), kind=kLoop, calls=%fused_computation.4 | loop fusion | bytes 2097152 | tf_op jit(solution)/shard_map/slice | solution.py:288
  9.1 5.2 %collective-permute-start.11 = (f32[32,4096]{1,0:T(8,128)S(1)}, f32[32,4096]{1,0:T(8,128)S(1)}, u32[]{:S(2)}, u32[]{:S(2)}) collective-permute-start(f32[32,4096]{1,0:T(8,128)S(1)} %bitcast.11), channel_id=1, source_target_pairs={{1,0},{2,1},{3,2},{4,3},{5,4},{6,5},{7,6},{8,7},{9,8},{10,9},{11,1... | collective-permute-start | bytes 1572872 | tf_op jit(solution)/shard_map/ppermute | solution.py:283
  14.6 1.9 %collective-permute-start.6 = (f32[32,4096]{1,0:T(8,128)S(1)}, f32[32,4096]{1,0:T(8,128)S(1)}, u32[]{:S(2)}, u32[]{:S(2)}) collective-permute-start(f32[32,4096]{1,0:T(8,128)S(1)} %bitcast.10), channel_id=1, source_target_pairs={{0,1},{1,2},{2,3},{3,4},{4,5},{5,6},{6,7},{7,8},{8,9},{9,10},{10,1... | collective-permute-start | bytes 1572872 | tf_op jit(solution)/shard_map/ppermute | solution.py:283
  16.5 10.0 %sample_A.1.refs_3_ = f32[4,8,4096]{2,1,0:T(8,128)} custom-call(f32[32,32,4096]{2,1,0:T(8,128)} %refs_0_.7, f32[3,8]{1,0:T(4,128)} %refs_4_.5), custom_call_target="tpu_custom_call" | custom-call | tf_op jit(solution)/shard_map/sample_A/pallas_call | solution.py:217
  28.1 15.7 %sample_B.1 = (f32[4,16,2048]{2,1,0:T(8,128)}, f32[4,16,2048]{2,1,0:T(8,128)}) custom-call(f32[32,32,4096]{2,1,0:T(8,128)} %refs_0_.7, f32[32,4096]{1,0:T(8,128)} %copy-done, f32[32,4096]{1,0:T(8,128)} %copy-done.1, f32[4,8,4096]{2,1,0:T(8,128)} %sample_A.1.refs_3_, f32[3,8]{1,0:T(4,128)} %refs_4_.5), custom_call_target="tpu_custom_call" | custom-call | tf_op jit(solution)/shard_map/sample_B/pallas_call | solution.py:217
  43.9 2.6 %collective-permute-start.2 = (f32[4,16,2048]{2,1,0:T(8,128)}, f32[4,16,2048]{2,1,0:T(8,128)S(1)}, u32[]{:S(2)}, u32[]{:S(2)}) collective-permute-start(f32[4,16,2048]{2,1,0:T(8,128)} %get-tuple-element.24), channel_id=1, source_target_pairs={{0,16},{16,0},{32,48},{48,32},{64,80},{80,64},{96,112},{112,96},{1... | collective-permute-start | bytes 1572872 | tf_op jit(solution)/shard_map/ppermute | solution.py:299
  46.5 0.8 copy-done.3
  47.3 11.4 %sample_D.1 = (f32[4,8,2048]{2,1,0:T(8,128)}, f32[4,8,2048]{2,1,0:T(8,128)}) custom-call(f32[32,32,4096]{2,1,0:T(8,128)} %refs_0_.7, f32[32,4096]{1,0:T(8,128)} %copy-done, f32[32,4096]{1,0:T(8,128)} %copy-done.1, f32[32,4096]{1,0:T(8,128)} %copy-done.3, f32[3,8]{1,0:T(4,128)} %refs_4_.5), custom_call_target="tpu_custom_call" | custom-call | tf_op jit(solution)/shard_map/sample_D/pallas_call | solution.py:217
  59.6 11.4 %sample_C.1 = (f32[4,8,2048]{2,1,0:T(8,128)}, f32[4,8,2048]{2,1,0:T(8,128)}) custom-call(f32[32,32,4096]{2,1,0:T(8,128)} %refs_0_.7, f32[32,4096]{1,0:T(8,128)} %copy-done, f32[32,4096]{1,0:T(8,128)} %copy-done.1, f32[32,4096]{1,0:T(8,128)} %copy-done.2, f32[3,8]{1,0:T(4,128)} %refs_4_.5), custom_call_target="tpu_custom_call" | custom-call | tf_op jit(solution)/shard_map/sample_C/pallas_call | solution.py:217
  72.3 1.8 %merge.5 = (f32[4,8,512]{2,1,0:T(8,128)}, f32[4,8,512]{2,1,0:T(8,128)}, f32[4,8,512]{2,1,0:T(8,128)}, f32[4,8,512]{2,1,0:T(8,128)}) custom-call(f32[4,8,2048]{2,1,0:T(8,128)} %get-tuple-element.35.keep_ref, f32[4,8,2048]{2,1,0:T(8,128)} %copy-done.6), custom_call_target="tpu_custom_call" | custom-call | tf_op jit(solution)/shard_map/merge/pallas_call | solution.py:248
  74.1 1.9 %collective-permute-start.13 = (f32[4,8,512]{2,1,0:T(8,128)}, f32[4,8,512]{2,1,0:T(8,128)S(1)}, u32[]{:S(2)}, u32[]{:S(2)}) collective-permute-start(f32[4,8,512]{2,1,0:T(8,128)} %get-tuple-element.38), channel_id=1, source_target_pairs={{0,32},{16,48},{32,64},{48,80},{64,96},{80,112},{96,0},{112,16},{1... | collective-permute-start | bytes 196616 | tf_op jit(solution)/shard_map/ppermute | solution.py:306
  76.0 3.6 %collective-permute-start.14 = (f32[4,8,512]{2,1,0:T(8,128)}, f32[4,8,512]{2,1,0:T(8,128)S(1)}, u32[]{:S(2)}, u32[]{:S(2)}) collective-permute-start(f32[4,8,512]{2,1,0:T(8,128)} %get-tuple-element.39), channel_id=1, source_target_pairs={{0,64},{16,80},{32,96},{48,112},{64,0},{80,16},{96,32},{112,48},{1... | collective-permute-start | bytes 196616 | tf_op jit(solution)/shard_map/ppermute | solution.py:306
  79.6 1.0 collective-permute-start.15
  81.3 1.8 %merge.4 = (f32[4,8,512]{2,1,0:T(8,128)}, f32[4,8,512]{2,1,0:T(8,128)}, f32[4,8,512]{2,1,0:T(8,128)}, f32[4,8,512]{2,1,0:T(8,128)}) custom-call(f32[4,8,2048]{2,1,0:T(8,128)} %get-tuple-element.29.keep_ref, f32[4,8,2048]{2,1,0:T(8,128)} %copy-done.5), custom_call_target="tpu_custom_call" | custom-call | tf_op jit(solution)/shard_map/merge/pallas_call | solution.py:248
  83.9 2.0 %merge.3 = (f32[4,16,512]{2,1,0:T(8,128)}, f32[4,16,512]{2,1,0:T(8,128)}, f32[4,16,512]{2,1,0:T(8,128)}, f32[4,16,512]{2,1,0:T(8,128)}) custom-call(f32[4,16,2048]{2,1,0:T(8,128)} %get-tuple-element.23.keep_ref, f32[4,16,2048]{2,1,0:T(8,128)} %copy-done.4), custom_call_target="tpu_custom_call" | custom-call | tf_op jit(solution)/shard_map/merge/pallas_call | solution.py:248
  85.9 2.0 %collective-permute-start.3 = (f32[4,16,512]{2,1,0:T(8,128)}, f32[4,16,512]{2,1,0:T(8,128)S(1)}, u32[]{:S(2)}, u32[]{:S(2)}) collective-permute-start(f32[4,16,512]{2,1,0:T(8,128)} %get-tuple-element.26), channel_id=1, source_target_pairs={{0,32},{16,48},{32,64},{48,80},{64,96},{80,112},{96,0},{112,16},{1... | collective-permute-start | bytes 393224 | tf_op jit(solution)/shard_map/ppermute | solution.py:306
  87.9 1.2 %collective-permute-start.4 = (f32[4,16,512]{2,1,0:T(8,128)}, f32[4,16,512]{2,1,0:T(8,128)S(1)}, u32[]{:S(2)}, u32[]{:S(2)}) collective-permute-start(f32[4,16,512]{2,1,0:T(8,128)} %get-tuple-element.27), channel_id=1, source_target_pairs={{0,64},{16,80},{32,96},{48,112},{64,0},{80,16},{96,32},{112,48},{1... | collective-permute-start | bytes 393224 | tf_op jit(solution)/shard_map/ppermute | solution.py:306
  89.1 2.5 %collective-permute-start.5 = (f32[4,16,512]{2,1,0:T(8,128)}, f32[4,16,512]{2,1,0:T(8,128)S(1)}, u32[]{:S(2)}, u32[]{:S(2)}) collective-permute-start(f32[4,16,512]{2,1,0:T(8,128)} %get-tuple-element.28), channel_id=1, source_target_pairs={{0,96},{16,112},{32,0},{48,16},{64,32},{80,48},{96,64},{112,80},{1... | collective-permute-start | bytes 393224 | tf_op jit(solution)/shard_map/ppermute | solution.py:306
  91.6 1.8 %collective-permute-start.9 = (f32[4,8,512]{2,1,0:T(8,128)}, f32[4,8,512]{2,1,0:T(8,128)S(1)}, u32[]{:S(2)}, u32[]{:S(2)}) collective-permute-start(f32[4,8,512]{2,1,0:T(8,128)} %get-tuple-element.33), channel_id=1, source_target_pairs={{0,64},{16,80},{32,96},{48,112},{64,0},{80,16},{96,32},{112,48},{1... | collective-permute-start | bytes 196616 | tf_op jit(solution)/shard_map/ppermute | solution.py:306
  93.5 4.6 %collective-permute-done.8.refs_5_ = f32[4,8,512]{2,1,0:T(8,128)S(1)} collective-permute-done((f32[4,8,512]{2,1,0:T(8,128)}, f32[4,8,512]{2,1,0:T(8,128)S(1)}, u32[]{:S(2)}, u32[]{:S(2)}) %collective-permute-start.8) | collective-permute-done | bytes 65568 | tf_op jit(solution)/shard_map/ppermute | solution.py:306
  98.9 2.0 %final.1 = f32[4,32,512]{2,1,0:T(8,128)} custom-call(f32[4,16,512]{2,1,0:T(8,128)} %get-tuple-element.25.refs_0_, f32[4,16,512]{2,1,0:T(8,128)} %copy-done.7, f32[4,16,512]{2,1,0:T(8,128)} %copy-done.8, f32[4,16,512]{2,1,0:T(8,128)} %copy-done.9, f32[4,8,512]{2,1,0:T(8,128)} %get-tuple-element.31.refs_4_, f32[4,8,512]{2,1,0:T(8,128)} %copy-done.14, ...), custom_call_target="tpu_custom_call" | custom-call | tf_op jit(solution)/shard_map/final/pallas_call | solution.py:308
  (52 shorter events, 6.6 us)
Async XLA Ops:
  1.3 25.3 %collective-permute-start = (f32[32,4096]{1,0:T(8,128)S(1)}, f32[32,4096]{1,0:T(8,128)S(1)}, u32[]{:S(2)}, u32[]{:S(2)}) collective-permute-start(f32[32,4096]{1,0:T(8,128)S(1)} %get-tuple-element.44), channel_id=1, source_target_pairs={{0,16},{16,32},{32,48},{48,64},{64,80},{80,96},{96,112},{1,17},{17... | collective-permute-start | bytes 1572872 | tf_op jit(solution)/shard_map/ppermute | solution.py:283
  3.1 23.5 %collective-permute-start.1 = (f32[32,4096]{1,0:T(8,128)S(1)}, f32[32,4096]{1,0:T(8,128)S(1)}, u32[]{:S(2)}, u32[]{:S(2)}) collective-permute-start(f32[32,4096]{1,0:T(8,128)S(1)} %get-tuple-element.43), channel_id=1, source_target_pairs={{16,0},{32,16},{48,32},{64,48},{80,64},{96,80},{112,96},{17,1},{33... | collective-permute-start | bytes 1572872 | tf_op jit(solution)/shard_map/ppermute | solution.py:283
  9.1 37.4 %collective-permute-start.11 = (f32[32,4096]{1,0:T(8,128)S(1)}, f32[32,4096]{1,0:T(8,128)S(1)}, u32[]{:S(2)}, u32[]{:S(2)}) collective-permute-start(f32[32,4096]{1,0:T(8,128)S(1)} %bitcast.11), channel_id=1, source_target_pairs={{1,0},{2,1},{3,2},{4,3},{5,4},{6,5},{7,6},{8,7},{9,8},{10,9},{11,1... | collective-permute-start | bytes 1572872 | tf_op jit(solution)/shard_map/ppermute | solution.py:283
  14.6 44.2 %collective-permute-start.6 = (f32[32,4096]{1,0:T(8,128)S(1)}, f32[32,4096]{1,0:T(8,128)S(1)}, u32[]{:S(2)}, u32[]{:S(2)}) collective-permute-start(f32[32,4096]{1,0:T(8,128)S(1)} %bitcast.10), channel_id=1, source_target_pairs={{0,1},{1,2},{2,3},{3,4},{4,5},{5,6},{6,7},{7,8},{8,9},{9,10},{10,1... | collective-permute-start | bytes 1572872 | tf_op jit(solution)/shard_map/ppermute | solution.py:283
  27.4 0.8 copy-start.1
  43.9 39.2 %collective-permute-start.2 = (f32[4,16,2048]{2,1,0:T(8,128)}, f32[4,16,2048]{2,1,0:T(8,128)S(1)}, u32[]{:S(2)}, u32[]{:S(2)}) collective-permute-start(f32[4,16,2048]{2,1,0:T(8,128)} %get-tuple-element.24), channel_id=1, source_target_pairs={{0,16},{16,0},{32,48},{48,32},{64,80},{80,64},{96,112},{112,96},{1... | collective-permute-start | bytes 1572872 | tf_op jit(solution)/shard_map/ppermute | solution.py:299
  46.5 0.8 copy-start.3
  58.7 12.9 %collective-permute-start.12 = (f32[4,8,2048]{2,1,0:T(8,128)}, f32[4,8,2048]{2,1,0:T(8,128)S(1)}, u32[]{:S(2)}, u32[]{:S(2)}) collective-permute-start(f32[4,8,2048]{2,1,0:T(8,128)} %get-tuple-element.36), channel_id=1, source_target_pairs={{0,16},{16,0},{32,48},{48,32},{64,80},{80,64},{96,112},{112,96},{1... | collective-permute-start | bytes 786440 | tf_op jit(solution)/shard_map/ppermute | solution.py:299
  58.8 0.8 copy-start.2
  71.0 9.6 %collective-permute-start.7 = (f32[4,8,2048]{2,1,0:T(8,128)}, f32[4,8,2048]{2,1,0:T(8,128)S(1)}, u32[]{:S(2)}, u32[]{:S(2)}) collective-permute-start(f32[4,8,2048]{2,1,0:T(8,128)} %get-tuple-element.30), channel_id=1, source_target_pairs={{0,16},{16,0},{32,48},{48,32},{64,80},{80,64},{96,112},{112,96},{1... | collective-permute-start | bytes 786440 | tf_op jit(solution)/shard_map/ppermute | solution.py:299
  74.1 13.9 %collective-permute-start.13 = (f32[4,8,512]{2,1,0:T(8,128)}, f32[4,8,512]{2,1,0:T(8,128)S(1)}, u32[]{:S(2)}, u32[]{:S(2)}) collective-permute-start(f32[4,8,512]{2,1,0:T(8,128)} %get-tuple-element.38), channel_id=1, source_target_pairs={{0,32},{16,48},{32,64},{48,80},{64,96},{80,112},{96,0},{112,16},{1... | collective-permute-start | bytes 196616 | tf_op jit(solution)/shard_map/ppermute | solution.py:306
  76.0 13.1 %collective-permute-start.14 = (f32[4,8,512]{2,1,0:T(8,128)}, f32[4,8,512]{2,1,0:T(8,128)S(1)}, u32[]{:S(2)}, u32[]{:S(2)}) collective-permute-start(f32[4,8,512]{2,1,0:T(8,128)} %get-tuple-element.39), channel_id=1, source_target_pairs={{0,64},{16,80},{32,96},{48,112},{64,0},{80,16},{96,32},{112,48},{1... | collective-permute-start | bytes 196616 | tf_op jit(solution)/shard_map/ppermute | solution.py:306
  79.6 12.1 %collective-permute-start.15 = (f32[4,8,512]{2,1,0:T(8,128)}, f32[4,8,512]{2,1,0:T(8,128)S(1)}, u32[]{:S(2)}, u32[]{:S(2)}) collective-permute-start(f32[4,8,512]{2,1,0:T(8,128)} %get-tuple-element.40), channel_id=1, source_target_pairs={{0,96},{16,112},{32,0},{48,16},{64,32},{80,48},{96,64},{112,80},{1... | collective-permute-start | bytes 196616 | tf_op jit(solution)/shard_map/ppermute | solution.py:306
  83.0 8.6 %collective-permute-start.10 = (f32[4,8,512]{2,1,0:T(8,128)}, f32[4,8,512]{2,1,0:T(8,128)S(1)}, u32[]{:S(2)}, u32[]{:S(2)}) collective-permute-start(f32[4,8,512]{2,1,0:T(8,128)} %get-tuple-element.34), channel_id=1, source_target_pairs={{0,96},{16,112},{32,0},{48,16},{64,32},{80,48},{96,64},{112,80},{1... | collective-permute-start | bytes 196616 | tf_op jit(solution)/shard_map/ppermute | solution.py:306
  83.0 0.8 copy-start.4
  85.9 12.2 %collective-permute-start.3 = (f32[4,16,512]{2,1,0:T(8,128)}, f32[4,16,512]{2,1,0:T(8,128)S(1)}, u32[]{:S(2)}, u32[]{:S(2)}) collective-permute-start(f32[4,16,512]{2,1,0:T(8,128)} %get-tuple-element.26), channel_id=1, source_target_pairs={{0,32},{16,48},{32,64},{48,80},{64,96},{80,112},{96,0},{112,16},{1... | collective-permute-start | bytes 393224 | tf_op jit(solution)/shard_map/ppermute | solution.py:306
  87.9 10.3 %copy-start.10 = (f32[4,8,512]{2,1,0:T(8,128)}, f32[4,8,512]{2,1,0:T(8,128)S(1)}, u32[]{:S(2)}) copy-start(f32[4,8,512]{2,1,0:T(8,128)S(1)} %collective-permute-done.13.refs_9_) | copy-start | bytes 196612
  87.9 10.2 %collective-permute-start.4 = (f32[4,16,512]{2,1,0:T(8,128)}, f32[4,16,512]{2,1,0:T(8,128)S(1)}, u32[]{:S(2)}, u32[]{:S(2)}) collective-permute-start(f32[4,16,512]{2,1,0:T(8,128)} %get-tuple-element.27), channel_id=1, source_target_pairs={{0,64},{16,80},{32,96},{48,112},{64,0},{80,16},{96,32},{112,48},{1... | collective-permute-start | bytes 393224 | tf_op jit(solution)/shard_map/ppermute | solution.py:306
  89.1 9.1 %copy-start.11 = (f32[4,8,512]{2,1,0:T(8,128)}, f32[4,8,512]{2,1,0:T(8,128)S(1)}, u32[]{:S(2)}) copy-start(f32[4,8,512]{2,1,0:T(8,128)S(1)} %collective-permute-done.14.refs_10_) | copy-start | bytes 196612
  89.1 9.1 %collective-permute-start.5 = (f32[4,16,512]{2,1,0:T(8,128)}, f32[4,16,512]{2,1,0:T(8,128)S(1)}, u32[]{:S(2)}, u32[]{:S(2)}) collective-permute-start(f32[4,16,512]{2,1,0:T(8,128)} %get-tuple-element.28), channel_id=1, source_target_pairs={{0,96},{16,112},{32,0},{48,16},{64,32},{80,48},{96,64},{112,80},{1... | collective-permute-start | bytes 393224 | tf_op jit(solution)/shard_map/ppermute | solution.py:306
  91.6 6.6 %copy-start.12 = (f32[4,8,512]{2,1,0:T(8,128)}, f32[4,8,512]{2,1,0:T(8,128)S(1)}, u32[]{:S(2)}) copy-start(f32[4,8,512]{2,1,0:T(8,128)S(1)} %collective-permute-done.15.refs_11_) | copy-start | bytes 196612
  91.6 6.5 %collective-permute-start.8 = (f32[4,8,512]{2,1,0:T(8,128)}, f32[4,8,512]{2,1,0:T(8,128)S(1)}, u32[]{:S(2)}, u32[]{:S(2)}) collective-permute-start(f32[4,8,512]{2,1,0:T(8,128)} %get-tuple-element.32), channel_id=1, source_target_pairs={{0,32},{16,48},{32,64},{48,80},{64,96},{80,112},{96,0},{112,16},{1... | collective-permute-start | bytes 196616 | tf_op jit(solution)/shard_map/ppermute | solution.py:306
  91.6 6.6 %copy-start.13 = (f32[4,8,512]{2,1,0:T(8,128)}, f32[4,8,512]{2,1,0:T(8,128)S(1)}, u32[]{:S(2)}) copy-start(f32[4,8,512]{2,1,0:T(8,128)S(1)} %collective-permute-done.10.refs_7_) | copy-start | bytes 196612
  91.6 6.5 %collective-permute-start.9 = (f32[4,8,512]{2,1,0:T(8,128)}, f32[4,8,512]{2,1,0:T(8,128)S(1)}, u32[]{:S(2)}, u32[]{:S(2)}) collective-permute-start(f32[4,8,512]{2,1,0:T(8,128)} %get-tuple-element.33), channel_id=1, source_target_pairs={{0,64},{16,80},{32,96},{48,112},{64,0},{80,16},{96,32},{112,48},{1... | collective-permute-start | bytes 196616 | tf_op jit(solution)/shard_map/ppermute | solution.py:306
  (8 other events, 5.6 us)

commit v2 on v0

v2 whole, which is shorter than its diff:
```python
import functools
import math

import jax
import jax.numpy as jnp
from jax import lax
from jax.experimental import pallas as pl
from jax.experimental.pallas import tpu as pltpu
from jax.sharding import PartitionSpec as P


LANES = 128
SUBLANES = 8
BELOW = 8
STAGED = 48
LOG2E = math.log2(math.e)
TO_Y = 4.0 / 3.0
TO_X = 20.0 / 9.0
AMBIENT = 0.25 / 0.27
AHEAD = 4
SPLIT = 20
VMEM = pl.BlockSpec(memory_space=pltpu.VMEM)
ANY = pl.BlockSpec(memory_space=pl.ANY)
HBM = pl.BlockSpec(memory_space=pltpu.HBM)
SMEM = pl.BlockSpec(memory_space=pltpu.SMEM)


def in_vmem(value):
    return pltpu.with_memory_space_constraint(value, pltpu.VMEM)


def vmem_shape(*shape):
    return pltpu.VMEM(shape, jnp.float32)


def shade_of(dz, dy, dx):
    along = jnp.abs(dz + TO_Y * dy + TO_X * dx)
    square = (dz * dz + 0.16) + (dy * dy + dx * dx)
    return along * lax.rsqrt(square) + AMBIENT


def across(left, here, right):
    lane = lax.broadcasted_iota(jnp.int32, (SUBLANES, LANES), 1)
    after = pltpu.roll(jnp.where(lane == 0, right, here), LANES - 1, 1)
    before = pltpu.roll(jnp.where(lane == LANES - 1, left, here), 1, 1)
    return after - before


def add_bumps(moments, amount, field):
    ratio = jnp.exp2(field * (14 * LOG2E))
    amount = amount * jnp.exp2(field * field * (-49 * LOG2E))
    out = []
    for j, moment in enumerate(moments):
        out.append(amount if moment is None else moment + amount)
        if j + 1 < len(moments):
            amount = amount * ratio
    return out


def coefficients(palette_ref):
    bumps = palette_ref.shape[1]
    return [[palette_ref[k, j] * jnp.float32(0.27 * math.exp(-j * j)) for j in range(bumps)] for k in range(3)]


def contracted(coef, moments):
    out = []
    for k in range(3):
        total = moments[0] * coef[k][0]
        for j in range(1, len(moments)):
            total = total + moments[j] * coef[k][j]
        out.append(total)
    return out


def tile_lanes(c):
    return pl.ds(pl.multiple_of(c * LANES, LANES), LANES)


def gradients(vb, c, z, row, up, down):
    here = vb[c + 1, z, pl.ds(row, 8), :]
    dy = vb[c + 1, z, pl.ds(row + 1, 8), :] - vb[c + 1, z, pl.ds(row - 1, 8), :]
    dx = across(vb[c, z, pl.ds(row, 8), :], here, vb[c + 2, z, pl.ds(row, 8), :])
    if up is None:
        up = vb[c + 1, z + 1, pl.ds(row, 8), :]
    if down is None:
        down = vb[c + 1, z - 1, pl.ds(row, 8), :]
    return here, up - down, dy, dx


def march(vb, c, group, planes, scale, ends=None):
    row = BELOW + group * SUBLANES
    moments = [None] * 8
    total = jnp.zeros((SUBLANES, LANES), jnp.float32)
    passed = jnp.ones((SUBLANES, LANES), jnp.float32)
    for z in range(planes):
        outer = z in (0, planes - 1)
        total = total + vb[c + 1, z, pl.ds(row, 8), :]
        after = jnp.exp2(total * (-scale * LOG2E))
        if not outer or ends is not None:
            down = ends[0] if z == 0 else None
            up = ends[1] if z == planes - 1 else None
            here, dz, dy, dx = gradients(vb, c, z, row, up, down)
            moments = add_bumps(moments, (passed - after) * shade_of(dz, dy, dx), here)
        passed = after
    return moments, passed


def march_ends(vb, c, group, planes, scale, ends, passed):
    row = BELOW + group * SUBLANES
    here, dz, dy, dx = gradients(vb, c, 0, row, None, ends[0])
    amount = 1.0 - jnp.exp2(here * (-scale * LOG2E))
    moments = add_bumps([None] * 8, amount * shade_of(dz, dy, dx), here)
    here, dz, dy, dx = gradients(vb, c, planes - 1, row, ends[1], None)
    amount = passed * (jnp.exp2(here * (scale * LOG2E)) - 1.0)
    return add_bumps(moments, amount * shade_of(dz, dy, dx), here)


def stage_kernel(volume_ref, palette_ref, vb, early_ref, top_ref, bottom_ref, sem, *, scale):
    planes, rows, columns = volume_ref.shape
    tiles = columns // LANES

    def copy(c):
        return pltpu.make_async_copy(
            volume_ref.at[:, :, tile_lanes(c)], vb.at[c + 1, :, pl.ds(BELOW, rows), :], sem.at[c]
        )

    for c in range(AHEAD):
        copy(c).start()
    zero = jnp.zeros((planes, rows, LANES), jnp.float32)
    vb[0, :, BELOW : BELOW + rows, :] = zero
    vb[tiles + 1, :, BELOW : BELOW + rows, :] = zero
    coef = coefficients(palette_ref)

    def arrive(c):
        copy(c).wait()

        @pl.when(c + AHEAD < tiles)
        def _():
            copy(c + AHEAD).start()

        flat = vb.reshape(tiles + 2, planes * STAGED, LANES)
        for z in range(0, planes, 8):
            for out, row in ((top_ref, BELOW), (bottom_ref, BELOW + rows - 1)):
                out[z : z + 8, tile_lanes(c)] = flat[c + 1, pl.ds(z * STAGED + row, 8, stride=STAGED), :]

    arrive(0)

    def body(c, _):
        arrive(c + 1)
        moments, passed = march(vb, c, 1, planes, scale)
        for k, value in enumerate(contracted(coef, moments) + [passed]):
            early_ref[k, :, tile_lanes(c)] = value
        return 0

    lax.fori_loop(0, SPLIT, body, 0)

    def rest(c, _):
        arrive(c)
        return 0

    lax.fori_loop(SPLIT + 1, tiles, rest, 0)


def early_kernel(vb, palette_ref, early_ref, *, scale, planes):
    tiles = vb.shape[0] - 2
    coef = coefficients(palette_ref)

    def body(c, _):
        moments, passed = march(vb, c, 1, planes, scale)
        for k, value in enumerate(contracted(coef, moments) + [passed]):
            early_ref[k, :, tile_lanes(c)] = value
        return 0

    lax.fori_loop(SPLIT, tiles, body, 0)


def place_of(block):
    chip = block // 2
    return 2 * ((chip ^ (chip // 2)) % 2) + chip // 2


def store_halves(keep_ref, send_ref, c, tiles, index, values, rows):
    per_block = tiles // 8
    block = c // per_block
    lanes = tile_lanes(place_of(block) * per_block + c % per_block)

    @pl.when(block % 2 == index % 2)
    def _():
        for k, value in enumerate(values):
            keep_ref[k, rows, lanes] = value

    @pl.when(block % 2 != index % 2)
    def _():
        for k, value in enumerate(values):
            send_ref[k, rows, lanes] = value


def depth_ends(prev_ref, next_ref, index, groups):
    inside_prev = jnp.where(index == 0, 0.0, 1.0)
    inside_next = jnp.where(index == groups - 1, 0.0, 1.0)

    def ends(c, group):
        rows = pl.ds(group * SUBLANES, SUBLANES)
        return prev_ref[rows, tile_lanes(c)] * inside_prev, next_ref[rows, tile_lanes(c)] * inside_next

    return ends


def middle_kernel(vb, prev_ref, next_ref, first_ref, second_ref, palette_ref, keep_ref, send_ref, *, scale, planes, depth, groups):
    tiles = vb.shape[0] - 2
    coef = coefficients(palette_ref)
    index = lax.axis_index(depth)
    ends = depth_ends(prev_ref, next_ref, index, groups)

    def body(c, _):
        moments, passed = march(vb, c, 2, planes, scale, ends(c, 2))
        store_halves(keep_ref, send_ref, c, tiles, index, contracted(coef, moments) + [passed], pl.ds(8, 8))
        early = [jnp.where(c < SPLIT, first_ref[k, :, tile_lanes(c)], second_ref[k, :, tile_lanes(c)]) for k in range(4)]
        moments = march_ends(vb, c, 1, planes, scale, ends(c, 1), early[3])
        colors = [early[k] + color for k, color in enumerate(contracted(coef, moments))]
        store_halves(keep_ref, send_ref, c, tiles, index, colors + [early[3]], pl.ds(0, 8))
        return 0

    lax.fori_loop(0, tiles, body, 0)


def outer_kernel(vb_in, prev_ref, next_ref, edge_ref, after_ref, palette_ref, vb, keep_ref, send_ref, *, scale, planes, depth, groups, row, stacks, top):
    tiles = vb.shape[0] - 2
    coef = coefficients(palette_ref)
    index = lax.axis_index(depth)
    ends = depth_ends(prev_ref, next_ref, index, groups)
    at_end = lax.axis_index(row) == (0 if top else stacks - 1)
    inside = jnp.where(at_end, 0.0, 1.0)
    group = 0 if top else 3
    slot = BELOW - 1 if top else BELOW + 4 * SUBLANES
    flat = vb.reshape(tiles + 2, planes * STAGED, LANES)

    def place(c, _):
        for z in range(0, planes, 8):
            flat[c + 1, pl.ds(z * STAGED + slot, 8, stride=STAGED), :] = edge_ref[z : z + 8, tile_lanes(c)] * inside
        return 0

    lax.fori_loop(0, tiles, place, 0)

    def body(c, _):
        moments, passed = march(vb, c, group, planes, scale, ends(c, group))
        store_halves(keep_ref, send_ref, c, tiles, index, contracted(coef, moments) + [passed], pl.ds(0, 8))
        return 0

    lax.fori_loop(0, tiles, body, 0)


def blend(front, back, lanes):
    passed = front[3, :, lanes]
    out = [front[k, :, lanes] + passed * back[k, :, lanes] for k in range(3)]
    return out + [passed * back[3, :, lanes]]


def merge_kernel(mine_ref, theirs_ref, keep_ref, send_ref, *, depth, step):
    index = lax.axis_index(depth)
    chip = index // 2
    width = keep_ref.shape[2]
    if step == 0:
        in_front, half = index % 2 == 0, (chip ^ (chip // 2)) % 2
    else:
        in_front, half = chip % 2 == 0, chip // 2
    keep_lanes = pl.ds(pl.multiple_of(half * width, width), width)
    send_lanes = pl.ds(pl.multiple_of((1 - half) * width, width), width)
    for mine_first in (True, False):

        @pl.when(in_front == mine_first)
        def _():
            front, back = (mine_ref, theirs_ref) if mine_first else (theirs_ref, mine_ref)
            for out_ref, lanes in ((send_ref, send_lanes), (keep_ref, keep_lanes)):
                for k, value in enumerate(blend(front, back, lanes)):
                    out_ref[k] = value


def final_kernel(*refs, spans, depth):
    out_ref = refs[-1]
    chip = lax.axis_index(depth) // 2
    for mine_first in (True, False):

        @pl.when((chip < 2) == mine_first)
        def _():
            for i, (row, count) in enumerate(spans):
                front, back = (refs[2 * i], refs[2 * i + 1]) if mine_first else (refs[2 * i + 1], refs[2 * i])
                values = blend(front, back, slice(None))
                for k in range(3):
                    out_ref[k, row : row + count, :] = values[k]
                out_ref[3, row : row + count, :] = 1.0 - values[3]


def call(body, out_shape, in_specs, args, scratch=(), aliases=None, limit=4, **kwargs):
    single = not isinstance(out_shape, tuple)
    out_specs = VMEM if single else (VMEM,) * len(out_shape)
    return pl.pallas_call(
        functools.partial(body, **kwargs),
        out_shape=out_shape,
        in_specs=in_specs,
        out_specs=out_specs,
        scratch_shapes=scratch,
        input_output_aliases=aliases or {},
        compiler_params=pltpu.CompilerParams(vmem_limit_bytes=limit * 2**20),
    )(*args)


def on_device(volume, palette):
    planes, rows, columns = volume.shape
    groups = lax.axis_size("depth")
    stacks = lax.axis_size("row")
    tiles = columns // LANES
    scale = 4.0 / (planes * groups)

    def ring(value, axis, count, step):
        return lax.ppermute(value, axis, [(i, (i + step) % count) for i in range(count)])

    before = ring(volume[-1], "depth", groups, 1)
    after = ring(volume[0], "depth", groups, -1)
    staged = vmem_shape(tiles + 2, planes, STAGED, LANES)
    strip = vmem_shape(4, SUBLANES, columns)
    edge = vmem_shape(planes, columns)
    vb, first, top, bottom = call(
        stage_kernel,
        (staged, strip, edge, edge),
        [HBM, SMEM],
        (pltpu.with_memory_space_constraint(volume, pltpu.HBM), palette),
        scratch=[pltpu.SemaphoreType.DMA((tiles,))],
        scale=scale,
    )
    above = ring(bottom, "row", stacks, 1)
    below = ring(top, "row", stacks, -1)
    common = dict(scale=scale, planes=planes)
    second = call(early_kernel, strip, [VMEM, SMEM], (in_vmem(vb), palette), **common)
    common.update(depth="depth", groups=groups)
    before, after = in_vmem(before), in_vmem(after)
    half = lambda count: (vmem_shape(4, count, columns // 2),) * 2
    keep, send = call(
        middle_kernel,
        half(16),
        [VMEM] * 5 + [SMEM],
        (in_vmem(vb), before, after, in_vmem(first), in_vmem(second), palette),
        **common,
    )
    pairs = lambda other: [(i, other(i)) for i in range(groups)]
    partners = [pairs(lambda i: i ^ 1), pairs(lambda i: i ^ 2), pairs(lambda i: groups - 2 - i // 2 * 2 + i % 2)]

    def outer(vb, edge, behind, top):
        return call(
            outer_kernel,
            (staged,) + half(8),
            [VMEM] * 4 + [ANY, SMEM],
            (in_vmem(vb), before, after, in_vmem(edge), behind, palette),
            aliases={0: 0},
            row="row",
            stacks=stacks,
            top=top,
            **common,
        )

    def swap(value, step):
        return lax.ppermute(value, "depth", partners[step])

    def merged(keep, arrived, step):
        channels, count, width = keep.shape
        shape = (vmem_shape(channels, count, width // 2),) * 2
        return call(merge_kernel, shape, [VMEM, VMEM], (in_vmem(keep), in_vmem(arrived)), depth="depth", step=step)

    kept = [keep, None, None]
    arrived = [swap(send, 0), None, None]
    vb, kept[1], send = outer(vb, above, kept[0], True)
    arrived[1] = swap(send, 0)
    kept[0], send = merged(kept[0], arrived[0], 0)
    arrived[0] = swap(send, 1)
    vb, kept[2], send = outer(vb, below, kept[0], False)
    arrived[2] = swap(send, 0)
    kept[0], send = merged(kept[0], arrived[0], 1)
    arrived[0] = swap(send, 2)
    for i in (1, 2):
        kept[i], send = merged(kept[i], arrived[i], 0)
        arrived[i] = swap(send, 1)
    for i in (1, 2):
        kept[i], send = merged(kept[i], arrived[i], 1)
        arrived[i] = swap(send, 2)
    args = []
    for i in range(3):
        args += [in_vmem(kept[i]), in_vmem(arrived[i])]
    return call(
        final_kernel,
        jax.ShapeDtypeStruct((4, rows, columns // groups), jnp.float32),
        [VMEM] * 6,
        args,
        spans=((8, 16), (0, 8), (24, 8)),
        depth="depth",
    )


def solution(mesh):
    return jax.shard_map(
        on_device,
        mesh=mesh,
        in_specs=(P("depth", "row", None), P()),
        out_specs=P(None, "row", "depth"),
        check_vma=False,
    )
```

time: 207 us -> 80.3 us (0.39)
  the two profiles are of different devices: /device:TPU:6 before, /device:TPU:30 now
where the time goes in v2:
time: 80.3 us; the launch traced here: 80 us
  Pallas kernels  45.1 us (56%)
  waiting for transfers between devices  16.5 us (21%)
  starting transfers between devices  16.2 us (20%)
  local copies, waits for them, and re-layouts  1.96 us (2%)
    pallas_call x12, Pallas kernels, call(): pl.pallas_call(functools.partial(body, **kwargs), out_shape=out_shape, in...  45.1 us
    ppermute x9, starting transfers between devices, swap(): return lax.ppermute(value, 'depth', partners[step])  10.5 us
    ppermute x9, waiting for transfers between devices, swap(): return lax.ppermute(value, 'depth', partners[step])  10.2 us
    ppermute x4, waiting for transfers between devices, ring(): lax.ppermute(value, axis, [(i, (i + step) % count) for i in range(count)])  6.32 us
    ppermute x4, starting transfers between devices, ring(): lax.ppermute(value, axis, [(i, (i + step) % count) for i in range(count)])  5.66 us
  transfers between devices with their start and end apart: 13, of which 4 were waited for; matrix products, arithmetic and copies ran while one was open for 0% of the time, Pallas kernels for 56%

profile of v2, /device:TPU:30, one launch (start us, length us, event | category | flops | bytes accessed | tf_op | source)
XLA Modules:
  0.0 80.0 jit_solution(15821129297373661825)
XLA Ops:
  0.0 1.3 %slice_bitcast_fusion = (f32[32,4096]{1,0:T(8,128)S(1)}, f32[32,4096]{1,0:T(8,128)S(1)}) fusion(f32[32,32,4096]{2,1,0:T(8,128)} %volume_ref.1), kind=kLoop, calls=%fused_computation | loop fusion | bytes 2097152 | tf_op jit(solution)/shard_map/squeeze | solution.py:319
  1.3 3.5 %collective-permute-start.1 = (f32[32,4096]{1,0:T(8,128)S(1)}, f32[32,4096]{1,0:T(8,128)S(1)}, u32[]{:S(2)}, u32[]{:S(2)}) collective-permute-start(f32[32,4096]{1,0:T(8,128)S(1)} %get-tuple-element.51), channel_id=1, source_target_pairs={{0,112},{16,0},{32,16},{48,32},{64,48},{80,64},{96,80},{112,96},{1... | collective-permute-start | bytes 1572872 | tf_op jit(solution)/shard_map/ppermute | solution.py:316
  4.8 0.7 copy-done
  5.5 10.8 %shard_map.28 = (f32[34,32,48,128]{3,2,1,0:T(8,128)S(1)}, f32[4,8,4096]{2,1,0:T(8,128)S(1)}, f32[32,4096]{1,0:T(8,128)S(1)}, f32[32,4096]{1,0:T(8,128)S(1)}) custom-call(f32[32,32,4096]{2,1,0:T(8,128)} %volume_ref.1, f32[3,8]{1,0:T(4,128)S(1)} %copy-done), custom_call_target="tpu_custom_call" | custom-call | tf_op jit(solution)/shard_map/pallas_call | solution.py:297
  16.3 0.2 collective-permute-start.5
  16.5 3.3 %shard_map.29.second_ref = f32[4,8,4096]{2,1,0:T(8,128)S(1)} custom-call(f32[34,32,48,128]{3,2,1,0:T(8,128)S(1)} %get-tuple-element.28.vb.vb_in, f32[3,8]{1,0:T(4,128)S(1)} %copy-done), custom_call_target="tpu_custom_call" | custom-call | tf_op jit(solution)/shard_map/pallas_call | solution.py:297
  19.8 11.9 %shard_map.30 = (f32[4,16,2048]{2,1,0:T(8,128)S(1)}, f32[4,16,2048]{2,1,0:T(8,128)S(1)}) custom-call(f32[34,32,48,128]{3,2,1,0:T(8,128)S(1)} %get-tuple-element.28.vb.vb_in, f32[32,4096]{1,0:T(8,128)S(1)} %collective-permute-done.prev_ref, f32[32,4096]{1,0:T(8,128)S(1)} %collective-permute-done.1.next_ref, f32[4,8,4096]{2,1,0:T(8,128)S(1)} %get-tuple-element.29.first_ref, ...), custom_call_target="tpu_custom_call" | custom-call | tf_op jit(solution)/shard_map/pallas_call | solution.py:297
  31.7 0.1 collective-permute-start.2
  31.8 2.0 %collective-permute-start.9 = (f32[32,4096]{1,0:T(8,128)S(1)}, f32[32,4096]{1,0:T(8,128)S(1)}, u32[]{:S(2)}, u32[]{:S(2)}) collective-permute-start(f32[32,4096]{1,0:T(8,128)S(1)} %get-tuple-element.44), channel_id=1, source_target_pairs={{0,15},{1,0},{2,1},{3,2},{4,3},{5,4},{6,5},{7,6},{8,7},{9,8},{10,9... | collective-permute-start | bytes 1572872 | tf_op jit(solution)/shard_map/ppermute | solution.py:316
  33.8 9.1 %shard_map.33 = (f32[34,32,48,128]{3,2,1,0:T(8,128)S(1)}, f32[4,8,2048]{2,1,0:T(8,128)S(1)}, f32[4,8,2048]{2,1,0:T(8,128)S(1)}) custom-call(f32[34,32,48,128]{3,2,1,0:T(8,128)S(1)} %get-tuple-element.28.vb.vb_in, f32[32,4096]{1,0:T(8,128)S(1)} %collective-permute-done.prev_ref, ...), custom_call_target="tpu_custom_call", output_to_operand_aliasing={{0}: (0, {})} | custom-call | tf_op jit(solution)/shard_map/pallas_call | solution.py:297
  42.8 0.2 collective-permute-start.6
  43.1 6.3 %collective-permute-done.9.edge_ref = f32[32,4096]{1,0:T(8,128)S(1)} collective-permute-done((f32[32,4096]{1,0:T(8,128)S(1)}, f32[32,4096]{1,0:T(8,128)S(1)}, u32[]{:S(2)}, u32[]{:S(2)}) %collective-permute-start.9) | collective-permute-done | bytes 524320 | tf_op jit(solution)/shard_map/ppermute | solution.py:316
  49.5 9.1 %shard_map.36 = (f32[34,32,48,128]{3,2,1,0:T(8,128)S(1)}, f32[4,8,2048]{2,1,0:T(8,128)S(1)}, f32[4,8,2048]{2,1,0:T(8,128)S(1)}) custom-call(f32[34,32,48,128]{3,2,1,0:T(8,128)S(1)} %get-tuple-element.43.vb_in, f32[32,4096]{1,0:T(8,128)S(1)} %collective-permute-done.prev_ref, ...), custom_call_target="tpu_custom_call", output_to_operand_aliasing={{0}: (0, {})} | custom-call | tf_op jit(solution)/shard_map/pallas_call | solution.py:297
  58.6 0.1 collective-permute-start.10
  58.7 0.1 collective-permute-start.3
  58.9 2.1 %collective-permute-start.7 = (f32[4,8,1024]{2,1,0:T(8,128)S(1)}, f32[4,8,1024]{2,1,0:T(8,128)S(1)}, u32[]{:S(2)}, u32[]{:S(2)}) collective-permute-start(f32[4,8,1024]{2,1,0:T(8,128)S(1)} %get-tuple-element.40), channel_id=1, source_target_pairs={{0,32},{16,48},{32,0},{48,16},{64,96},{80,112},{96,64},{112,80},{1... | collective-permute-start | bytes 393224 | tf_op jit(solution)/shard_map/ppermute | solution.py:362
  60.9 0.1 collective-permute-start.11
  61.1 6.8 %collective-permute-done.3.theirs_ref = f32[4,16,1024]{2,1,0:T(8,128)S(1)} collective-permute-done((f32[4,16,1024]{2,1,0:T(8,128)S(1)}, f32[4,16,1024]{2,1,0:T(8,128)S(1)}, u32[]{:S(2)}, u32[]{:S(2)}) %collective-permute-start.3) | collective-permute-done | bytes 262176 | tf_op jit(solution)/shard_map/ppermute | solution.py:362
  68.0 2.9 %collective-permute-start.4 = (f32[4,16,512]{2,1,0:T(8,128)S(1)}, f32[4,16,512]{2,1,0:T(8,128)S(1)}, u32[]{:S(2)}, u32[]{:S(2)}) collective-permute-start(f32[4,16,512]{2,1,0:T(8,128)S(1)} %get-tuple-element.35), channel_id=1, source_target_pairs={{0,96},{16,112},{32,64},{48,80},{64,32},{80,48},{96,0},{112,16},{1... | collective-permute-start | bytes 393224 | tf_op jit(solution)/shard_map/ppermute | solution.py:362
  70.9 2.8 %collective-permute-start.8 = (f32[4,8,512]{2,1,0:T(8,128)S(1)}, f32[4,8,512]{2,1,0:T(8,128)S(1)}, u32[]{:S(2)}, u32[]{:S(2)}) collective-permute-start(f32[4,8,512]{2,1,0:T(8,128)S(1)} %get-tuple-element.42), channel_id=1, source_target_pairs={{0,96},{16,112},{32,64},{48,80},{64,32},{80,48},{96,0},{112,16},{1... | collective-permute-start | bytes 196616 | tf_op jit(solution)/shard_map/ppermute | solution.py:362
  73.7 2.2 %collective-permute-start.12 = (f32[4,8,512]{2,1,0:T(8,128)S(1)}, f32[4,8,512]{2,1,0:T(8,128)S(1)}, u32[]{:S(2)}, u32[]{:S(2)}) collective-permute-start(f32[4,8,512]{2,1,0:T(8,128)S(1)} %get-tuple-element.50), channel_id=1, source_target_pairs={{0,96},{16,112},{32,64},{48,80},{64,32},{80,48},{96,0},{112,16},{1... | collective-permute-start | bytes 196616 | tf_op jit(solution)/shard_map/ppermute | solution.py:362
  75.9 0.5 collective-permute-done.8.refs_3_
  76.4 2.8 %collective-permute-done.12.refs_5_ = f32[4,8,512]{2,1,0:T(8,128)S(1)} collective-permute-done((f32[4,8,512]{2,1,0:T(8,128)S(1)}, f32[4,8,512]{2,1,0:T(8,128)S(1)}, u32[]{:S(2)}, u32[]{:S(2)}) %collective-permute-start.12) | collective-permute-done | bytes 65568 | tf_op jit(solution)/shard_map/ppermute | solution.py:362
  79.2 0.7 shard_map.39
  (19 shorter events, 0.3 us)
Async XLA Ops:
  1.3 18.5 %collective-permute-start.1 = (f32[32,4096]{1,0:T(8,128)S(1)}, f32[32,4096]{1,0:T(8,128)S(1)}, u32[]{:S(2)}, u32[]{:S(2)}) collective-permute-start(f32[32,4096]{1,0:T(8,128)S(1)} %get-tuple-element.51), channel_id=1, source_target_pairs={{0,112},{16,0},{32,16},{48,32},{64,48},{80,64},{96,80},{112,96},{1... | collective-permute-start | bytes 1572872 | tf_op jit(solution)/shard_map/ppermute | solution.py:316
  4.8 15.0 %collective-permute-start = (f32[32,4096]{1,0:T(8,128)S(1)}, f32[32,4096]{1,0:T(8,128)S(1)}, u32[]{:S(2)}, u32[]{:S(2)}) collective-permute-start(f32[32,4096]{1,0:T(8,128)S(1)} %get-tuple-element.52), channel_id=1, source_target_pairs={{0,16},{16,32},{32,48},{48,64},{64,80},{80,96},{96,112},{112,0},{1... | collective-permute-start | bytes 1572872 | tf_op jit(solution)/shard_map/ppermute | solution.py:316
  4.8 0.7 copy-start
  16.3 17.5 %collective-permute-start.5 = (f32[32,4096]{1,0:T(8,128)S(1)}, f32[32,4096]{1,0:T(8,128)S(1)}, u32[]{:S(2)}, u32[]{:S(2)}) collective-permute-start(f32[32,4096]{1,0:T(8,128)S(1)} %get-tuple-element.36), channel_id=1, source_target_pairs={{0,1},{1,2},{2,3},{3,4},{4,5},{5,6},{6,7},{7,8},{8,9},{9,10},{10,1... | collective-permute-start | bytes 1572872 | tf_op jit(solution)/shard_map/ppermute | solution.py:316
  19.8 29.7 %copy-start.1 = (f32[3,8]{1,0:T(4,128)S(1)}, f32[3,8]{1,0:T(4,128)}, u32[]{:S(2)}) copy-start(f32[3,8]{1,0:T(4,128)} %palette_ref.9) | copy-start | bytes 292
  31.7 11.4 %collective-permute-start.2 = (f32[4,16,2048]{2,1,0:T(8,128)S(1)}, f32[4,16,2048]{2,1,0:T(8,128)S(1)}, u32[]{:S(2)}, u32[]{:S(2)}) collective-permute-start(f32[4,16,2048]{2,1,0:T(8,128)S(1)} %get-tuple-element.31), channel_id=1, source_target_pairs={{0,16},{16,0},{32,48},{48,32},{64,80},{80,64},{96,112},{112,96},{1... | collective-permute-start | bytes 1572872 | tf_op jit(solution)/shard_map/ppermute | solution.py:362
  31.8 17.6 %collective-permute-start.9 = (f32[32,4096]{1,0:T(8,128)S(1)}, f32[32,4096]{1,0:T(8,128)S(1)}, u32[]{:S(2)}, u32[]{:S(2)}) collective-permute-start(f32[32,4096]{1,0:T(8,128)S(1)} %get-tuple-element.44), channel_id=1, source_target_pairs={{0,15},{1,0},{2,1},{3,2},{4,3},{5,4},{6,5},{7,6},{8,7},{9,8},{10,9... | collective-permute-start | bytes 1572872 | tf_op jit(solution)/shard_map/ppermute | solution.py:316
  42.8 15.9 %collective-permute-start.6 = (f32[4,8,2048]{2,1,0:T(8,128)S(1)}, f32[4,8,2048]{2,1,0:T(8,128)S(1)}, u32[]{:S(2)}, u32[]{:S(2)}) collective-permute-start(f32[4,8,2048]{2,1,0:T(8,128)S(1)} %get-tuple-element.38), channel_id=1, source_target_pairs={{0,16},{16,0},{32,48},{48,32},{64,80},{80,64},{96,112},{112,96},{1... | collective-permute-start | bytes 786440 | tf_op jit(solution)/shard_map/ppermute | solution.py:362
  58.6 2.3 %collective-permute-start.10 = (f32[4,8,2048]{2,1,0:T(8,128)S(1)}, f32[4,8,2048]{2,1,0:T(8,128)S(1)}, u32[]{:S(2)}, u32[]{:S(2)}) collective-permute-start(f32[4,8,2048]{2,1,0:T(8,128)S(1)} %get-tuple-element.46), channel_id=1, source_target_pairs={{0,16},{16,0},{32,48},{48,32},{64,80},{80,64},{96,112},{112,96},{1... | collective-permute-start | bytes 786440 | tf_op jit(solution)/shard_map/ppermute | solution.py:362
  58.7 9.3 %collective-permute-start.3 = (f32[4,16,1024]{2,1,0:T(8,128)S(1)}, f32[4,16,1024]{2,1,0:T(8,128)S(1)}, u32[]{:S(2)}, u32[]{:S(2)}) collective-permute-start(f32[4,16,1024]{2,1,0:T(8,128)S(1)} %get-tuple-element.33), channel_id=1, source_target_pairs={{0,32},{16,48},{32,0},{48,16},{64,96},{80,112},{96,64},{112,80},{1... | collective-permute-start | bytes 786440 | tf_op jit(solution)/shard_map/ppermute | solution.py:362
  58.9 12.0 %collective-permute-start.7 = (f32[4,8,1024]{2,1,0:T(8,128)S(1)}, f32[4,8,1024]{2,1,0:T(8,128)S(1)}, u32[]{:S(2)}, u32[]{:S(2)}) collective-permute-start(f32[4,8,1024]{2,1,0:T(8,128)S(1)} %get-tuple-element.40), channel_id=1, source_target_pairs={{0,32},{16,48},{32,0},{48,16},{64,96},{80,112},{96,64},{112,80},{1... | collective-permute-start | bytes 393224 | tf_op jit(solution)/shard_map/ppermute | solution.py:362
  60.9 12.7 %collective-permute-start.11 = (f32[4,8,1024]{2,1,0:T(8,128)S(1)}, f32[4,8,1024]{2,1,0:T(8,128)S(1)}, u32[]{:S(2)}, u32[]{:S(2)}) collective-permute-start(f32[4,8,1024]{2,1,0:T(8,128)S(1)} %get-tuple-element.48), channel_id=1, source_target_pairs={{0,32},{16,48},{32,0},{48,16},{64,96},{80,112},{96,64},{112,80},{1... | collective-permute-start | bytes 393224 | tf_op jit(solution)/shard_map/ppermute | solution.py:362
  68.0 8.5 %collective-permute-start.4 = (f32[4,16,512]{2,1,0:T(8,128)S(1)}, f32[4,16,512]{2,1,0:T(8,128)S(1)}, u32[]{:S(2)}, u32[]{:S(2)}) collective-permute-start(f32[4,16,512]{2,1,0:T(8,128)S(1)} %get-tuple-element.35), channel_id=1, source_target_pairs={{0,96},{16,112},{32,64},{48,80},{64,32},{80,48},{96,0},{112,16},{1... | collective-permute-start | bytes 393224 | tf_op jit(solution)/shard_map/ppermute | solution.py:362
  70.9 5.6 %collective-permute-start.8 = (f32[4,8,512]{2,1,0:T(8,128)S(1)}, f32[4,8,512]{2,1,0:T(8,128)S(1)}, u32[]{:S(2)}, u32[]{:S(2)}) collective-permute-start(f32[4,8,512]{2,1,0:T(8,128)S(1)} %get-tuple-element.42), channel_id=1, source_target_pairs={{0,96},{16,112},{32,64},{48,80},{64,32},{80,48},{96,0},{112,16},{1... | collective-permute-start | bytes 196616 | tf_op jit(solution)/shard_map/ppermute | solution.py:362
  73.7 5.6 %collective-permute-start.12 = (f32[4,8,512]{2,1,0:T(8,128)S(1)}, f32[4,8,512]{2,1,0:T(8,128)S(1)}, u32[]{:S(2)}, u32[]{:S(2)}) collective-permute-start(f32[4,8,512]{2,1,0:T(8,128)S(1)} %get-tuple-element.50), channel_id=1, source_target_pairs={{0,96},{16,112},{32,64},{48,80},{64,32},{80,48},{96,0},{112,16},{1... | collective-permute-start | bytes 196616 | tf_op jit(solution)/shard_map/ppermute | solution.py:362

commit v3 on v2

v3 whole, which is shorter than its diff:
```python
import functools
import math

import jax
import jax.numpy as jnp
from jax import lax
from jax.experimental import pallas as pl
from jax.experimental.pallas import tpu as pltpu
from jax.sharding import PartitionSpec as P


LANES = 128
SUBLANES = 8
BELOW = 8
STAGED = 48
LOG2E = math.log2(math.e)
TO_Y = 4.0 / 3.0
TO_X = 20.0 / 9.0
AMBIENT = 0.25 / 0.27
AHEAD = 10
SPLIT = 20
VMEM = pl.BlockSpec(memory_space=pltpu.VMEM)
ANY = pl.BlockSpec(memory_space=pl.ANY)
HBM = pl.BlockSpec(memory_space=pltpu.HBM)
SMEM = pl.BlockSpec(memory_space=pltpu.SMEM)


def in_vmem(value):
    return pltpu.with_memory_space_constraint(value, pltpu.VMEM)


def vmem_shape(*shape):
    return pltpu.VMEM(shape, jnp.float32)


def shade_of(dz, dy, dx):
    along = jnp.abs(dz + TO_Y * dy + TO_X * dx)
    square = (dz * dz + 0.16) + (dy * dy + dx * dx)
    return along * lax.rsqrt(square) + AMBIENT


def across(left, here, right):
    lane = lax.broadcasted_iota(jnp.int32, (SUBLANES, LANES), 1)
    after = pltpu.roll(jnp.where(lane == 0, right, here), LANES - 1, 1)
    before = pltpu.roll(jnp.where(lane == LANES - 1, left, here), 1, 1)
    return after - before


def add_bumps(moments, amount, field):
    ratio = jnp.exp2(field * (14 * LOG2E))
    amount = amount * jnp.exp2(field * field * (-49 * LOG2E))
    out = []
    for j, moment in enumerate(moments):
        out.append(amount if moment is None else moment + amount)
        if j + 1 < len(moments):
            amount = amount * ratio
    return out


def contracted(coef_ref, moments):
    bumps = len(moments)
    out = []
    for k in range(3):
        total = moments[0] * coef_ref[k * bumps]
        for j in range(1, bumps):
            total = total + moments[j] * coef_ref[k * bumps + j]
        out.append(total)
    return out


def tile_lanes(c):
    return pl.ds(pl.multiple_of(c * LANES, LANES), LANES)


def gradients(vb, c, z, row, up, down):
    here = vb[c + 1, z, pl.ds(row, 8), :]
    dy = vb[c + 1, z, pl.ds(row + 1, 8), :] - vb[c + 1, z, pl.ds(row - 1, 8), :]
    dx = across(vb[c, z, pl.ds(row, 8), :], here, vb[c + 2, z, pl.ds(row, 8), :])
    if up is None:
        up = vb[c + 1, z + 1, pl.ds(row, 8), :]
    if down is None:
        down = vb[c + 1, z - 1, pl.ds(row, 8), :]
    return here, up - down, dy, dx


def march(vb, c, group, planes, scale, ends=None):
    row = BELOW + group * SUBLANES
    moments = [None] * 8
    total = jnp.zeros((SUBLANES, LANES), jnp.float32)
    passed = jnp.ones((SUBLANES, LANES), jnp.float32)
    for z in range(planes):
        outer = z in (0, planes - 1)
        total = total + vb[c + 1, z, pl.ds(row, 8), :]
        after = jnp.exp2(total * (-scale * LOG2E))
        if not outer or ends is not None:
            down = ends[0] if z == 0 else None
            up = ends[1] if z == planes - 1 else None
            here, dz, dy, dx = gradients(vb, c, z, row, up, down)
            moments = add_bumps(moments, (passed - after) * shade_of(dz, dy, dx), here)
        passed = after
    return moments, passed


def march_ends(vb, c, group, planes, scale, ends, passed):
    row = BELOW + group * SUBLANES
    here, dz, dy, dx = gradients(vb, c, 0, row, None, ends[0])
    amount = 1.0 - jnp.exp2(here * (-scale * LOG2E))
    moments = add_bumps([None] * 8, amount * shade_of(dz, dy, dx), here)
    here, dz, dy, dx = gradients(vb, c, planes - 1, row, ends[1], None)
    amount = passed * (jnp.exp2(here * (scale * LOG2E)) - 1.0)
    return add_bumps(moments, amount * shade_of(dz, dy, dx), here)


def march_early(vb, coef_ref, early_ref, c, planes, scale):
    moments, passed = march(vb, c, 1, planes, scale)
    for k, value in enumerate(contracted(coef_ref, moments) + [passed]):
        early_ref[k, :, tile_lanes(c)] = value


def stage_kernel(volume_ref, palette_ref, vb, coef_ref, early_ref, top_ref, bottom_ref, palette, sem, palette_sem, *, scale):
    planes, rows, columns = volume_ref.shape
    tiles = columns // LANES
    bumps = palette_ref.shape[1]
    flat = vb.reshape(tiles + 2, planes * STAGED, LANES)

    def copy(c):
        return pltpu.make_async_copy(
            volume_ref.at[:, :, tile_lanes(c)], vb.at[c + 1, :, pl.ds(BELOW, rows), :], sem.at[c]
        )

    weights = pltpu.make_async_copy(palette_ref, palette, palette_sem)
    weights.start()
    for c in range(AHEAD):
        copy(c).start()
    zero = jnp.zeros((planes, rows, LANES), jnp.float32)
    vb[0, :, BELOW : BELOW + rows, :] = zero
    vb[tiles + 1, :, BELOW : BELOW + rows, :] = zero
    weights.wait()
    for k in range(3):
        for j in range(bumps):
            weight = palette[k, j] * jnp.float32(0.27 * math.exp(-j * j))
            coef_ref[k * bumps + j] = jnp.full((SUBLANES, LANES), weight, jnp.float32)

    def arrive(c):
        copy(c).wait()

        @pl.when(c + AHEAD < tiles)
        def _():
            copy(c + AHEAD).start()

        for z in range(0, planes, 8):
            for out, row in ((top_ref, BELOW), (bottom_ref, BELOW + rows - 1)):
                out[z : z + 8, tile_lanes(c)] = flat[c + 1, pl.ds(z * STAGED + row, 8, stride=STAGED), :]

    arrive(0)

    def body(i, _):
        arrive(2 * i + 1)
        arrive(2 * i + 2)
        for c in (2 * i, 2 * i + 1):
            march_early(vb, coef_ref, early_ref, c, planes, scale)
        return 0

    lax.fori_loop(0, SPLIT // 2, body, 0)

    def rest(c, _):
        arrive(c)
        return 0

    lax.fori_loop(SPLIT + 1, tiles, rest, 0)


def early_kernel(vb, coef_ref, early_ref, *, scale, planes):
    tiles = vb.shape[0] - 2

    def body(i, _):
        for c in (2 * i, 2 * i + 1):
            march_early(vb, coef_ref, early_ref, c, planes, scale)
        return 0

    lax.fori_loop(SPLIT // 2, tiles // 2, body, 0)


def place_of(block):
    chip = block // 2
    return 2 * ((chip ^ (chip // 2)) % 2) + chip // 2


def half_tiles(m, tiles, parity, unroll):
    per_block = tiles // 8
    out = []
    for i in range(unroll):
        at = m * unroll + i
        block = 2 * (at // per_block) + parity
        out.append((block * per_block + at % per_block, place_of(block) * per_block + at % per_block))
    return out


def depth_ends(prev_ref, next_ref, index, groups):
    inside_prev = jnp.where(index == 0, 0.0, 1.0)
    inside_next = jnp.where(index == groups - 1, 0.0, 1.0)

    def ends(c, group):
        rows = pl.ds(group * SUBLANES, SUBLANES)
        return prev_ref[rows, tile_lanes(c)] * inside_prev, next_ref[rows, tile_lanes(c)] * inside_next

    return ends


def middle_kernel(vb, prev_ref, next_ref, first_ref, second_ref, coef_ref, out_ref, *, scale, planes, depth, groups, send):
    tiles = vb.shape[0] - 2
    index = lax.axis_index(depth)
    ends = depth_ends(prev_ref, next_ref, index, groups)
    parity = (index + send) % 2

    def body(m, _):
        for c, place in half_tiles(m, tiles, parity, 2):
            moments, passed = march(vb, c, 2, planes, scale, ends(c, 2))
            for k, value in enumerate(contracted(coef_ref, moments) + [passed]):
                out_ref[k, 8:16, tile_lanes(place)] = value
            early = [
                jnp.where(c < SPLIT, first_ref[k, :, tile_lanes(c)], second_ref[k, :, tile_lanes(c)]) for k in range(4)
            ]
            moments = march_ends(vb, c, 1, planes, scale, ends(c, 1), early[3])
            for k, color in enumerate(contracted(coef_ref, moments)):
                out_ref[k, 0:8, tile_lanes(place)] = early[k] + color
            out_ref[3, 0:8, tile_lanes(place)] = early[3]
        return 0

    lax.fori_loop(0, tiles // 4, body, 0)


def outer_tiles(vb, prev_ref, next_ref, coef_ref, out_ref, *, scale, planes, depth, groups, send, group):
    tiles = vb.shape[0] - 2
    index = lax.axis_index(depth)
    ends = depth_ends(prev_ref, next_ref, index, groups)
    parity = (index + send) % 2

    def body(m, _):
        for c, place in half_tiles(m, tiles, parity, 2):
            moments, passed = march(vb, c, group, planes, scale, ends(c, group))
            for k, value in enumerate(contracted(coef_ref, moments) + [passed]):
                out_ref[k, :, tile_lanes(place)] = value
        return 0

    lax.fori_loop(0, tiles // 4, body, 0)


def outer_kernel(vb_in, prev_ref, next_ref, edge_ref, behind_ref, coef_ref, vb, out_ref, *, row, stacks, group, **kwargs):
    tiles, planes = vb.shape[0] - 2, vb.shape[1]
    top = group == 0
    at_end = lax.axis_index(row) == (0 if top else stacks - 1)
    inside = jnp.where(at_end, 0.0, 1.0)
    slot = BELOW - 1 if top else BELOW + 4 * SUBLANES
    flat = vb.reshape(tiles + 2, planes * STAGED, LANES)

    def place(c, _):
        for z in range(0, planes, 8):
            flat[c + 1, pl.ds(z * STAGED + slot, 8, stride=STAGED), :] = edge_ref[z : z + 8, tile_lanes(c)] * inside
        return 0

    lax.fori_loop(0, tiles, place, 0)
    outer_tiles(vb, prev_ref, next_ref, coef_ref, out_ref, send=1, group=group, **kwargs)


def outer_rest_kernel(vb, prev_ref, next_ref, coef_ref, out_ref, **kwargs):
    outer_tiles(vb, prev_ref, next_ref, coef_ref, out_ref, send=0, **kwargs)


def blend(front, back, lanes):
    passed = front[3, :, lanes]
    out = [front[k, :, lanes] + passed * back[k, :, lanes] for k in range(3)]
    return out + [passed * back[3, :, lanes]]


def merge_kernel(*refs, depth, step):
    *given, keep_ref, send_ref = refs
    index = lax.axis_index(depth)
    chip = index // 2
    width = keep_ref.shape[2]
    if step == 0:
        in_front, half = index % 2 == 0, (chip ^ (chip // 2)) % 2
    else:
        in_front, half = chip % 2 == 0, chip // 2
    keep_lanes = pl.ds(pl.multiple_of(half * width, width), width)
    send_lanes = pl.ds(pl.multiple_of((1 - half) * width, width), width)
    for mine_first in (True, False):

        @pl.when(in_front == mine_first)
        def _():
            row = 0
            for mine_ref, theirs_ref in zip(given[::2], given[1::2]):
                count = mine_ref.shape[1]
                front, back = (mine_ref, theirs_ref) if mine_first else (theirs_ref, mine_ref)
                for out_ref, lanes in ((send_ref, send_lanes), (keep_ref, keep_lanes)):
                    for k, value in enumerate(blend(front, back, lanes)):
                        out_ref[k, row : row + count, :] = value
                row += count


def final_kernel(*refs, spans, depth):
    out_ref = refs[-1]
    chip = lax.axis_index(depth) // 2
    for mine_first in (True, False):

        @pl.when((chip < 2) == mine_first)
        def _():
            for i, parts in enumerate(spans):
                front, back = (refs[2 * i], refs[2 * i + 1]) if mine_first else (refs[2 * i + 1], refs[2 * i])
                values = blend(front, back, slice(None))
                values[3] = 1.0 - values[3]
                for at, row, count in parts:
                    for k, value in enumerate(values):
                        out_ref[k, row : row + count, :] = value[at : at + count]


def call(body, out_shape, in_specs, args, scratch=(), aliases=None, limit=4, **kwargs):
    single = not isinstance(out_shape, tuple)
    out_specs = VMEM if single else (VMEM,) * len(out_shape)
    return pl.pallas_call(
        functools.partial(body, **kwargs),
        out_shape=out_shape,
        in_specs=in_specs,
        out_specs=out_specs,
        scratch_shapes=scratch,
        input_output_aliases=aliases or {},
        compiler_params=pltpu.CompilerParams(vmem_limit_bytes=limit * 2**20),
    )(*args)


def on_device(volume, palette):
    planes, rows, columns = volume.shape
    groups = lax.axis_size("depth")
    stacks = lax.axis_size("row")
    tiles = columns // LANES
    scale = 4.0 / (planes * groups)

    def ring(value, axis, count, step):
        return lax.ppermute(value, axis, [(i, (i + step) % count) for i in range(count)])

    before = ring(volume[-1], "depth", groups, 1)
    after = ring(volume[0], "depth", groups, -1)
    staged = vmem_shape(tiles + 2, planes, STAGED, LANES)
    strip = vmem_shape(4, SUBLANES, columns)
    edge = vmem_shape(planes, columns)
    to_hbm = lambda value: pltpu.with_memory_space_constraint(value, pltpu.HBM)
    vb, coef, first, top, bottom = call(
        stage_kernel,
        (staged, vmem_shape(palette.size, SUBLANES, LANES), strip, edge, edge),
        [HBM, HBM],
        (to_hbm(volume), to_hbm(palette)),
        scratch=[
            pltpu.SMEM(palette.shape, jnp.float32),
            pltpu.SemaphoreType.DMA((tiles,)),
            pltpu.SemaphoreType.DMA(()),
        ],
        scale=scale,
    )
    above = in_vmem(ring(bottom, "row", stacks, 1))
    below = in_vmem(ring(top, "row", stacks, -1))
    common = dict(scale=scale, planes=planes)
    coef = in_vmem(coef)
    second = call(early_kernel, strip, [VMEM, VMEM], (in_vmem(vb), coef), **common)
    common.update(depth="depth", groups=groups)
    before, after = in_vmem(before), in_vmem(after)
    half = lambda count: vmem_shape(4, count, columns // 2)
    pairs = lambda other: [(i, other(i)) for i in range(groups)]
    partners = [pairs(lambda i: i ^ 1), pairs(lambda i: i ^ 2), pairs(lambda i: groups - 2 - i // 2 * 2 + i % 2)]

    def swap(value, step):
        return lax.ppermute(value, "depth", partners[step])

    def middle(send):
        return call(
            middle_kernel,
            half(16),
            [VMEM] * 6,
            (in_vmem(vb), before, after, in_vmem(first), in_vmem(second), coef),
            send=send,
            **common,
        )

    def outer(vb, edge, behind, group):
        return call(
            outer_kernel,
            (staged, half(8)),
            [VMEM] * 4 + [ANY, VMEM],
            (in_vmem(vb), before, after, edge, behind, coef),
            aliases={0: 0},
            row="row",
            stacks=stacks,
            group=group,
            **common,
        )

    def outer_rest(vb, group):
        return call(outer_rest_kernel, half(8), [VMEM] * 4, (in_vmem(vb), before, after, coef), group=group, **common)

    def merged(given, step):
        channels, _, width = given[0].shape
        shape = (vmem_shape(channels, sum(value.shape[1] for value in given[::2]), width // 2),) * 2
        return call(
            merge_kernel, shape, [VMEM] * len(given), [in_vmem(value) for value in given], depth="depth", step=step
        )

    arrived0 = swap(middle(1), 0)
    kept0 = middle(0)
    behind = kept0
    kept0, send = merged([kept0, arrived0], 0)
    arrived0 = swap(send, 1)
    vb, send = outer(vb, above, behind, 0)
    arrived1 = swap(send, 0)
    kept1 = outer_rest(vb, 0)
    behind = kept1
    kept1, send = merged([kept1, arrived1], 0)
    arrived1 = swap(send, 1)
    vb, send = outer(vb, below, behind, 3)
    arrived2 = swap(send, 0)
    kept01, send = merged([kept0, arrived0, kept1, arrived1], 1)
    arrived01 = swap(send, 2)
    kept2 = outer_rest(vb, 3)
    kept2, send = merged([kept2, arrived2], 0)
    arrived2 = swap(send, 1)
    kept2, send = merged([kept2, arrived2], 1)
    arrived2 = swap(send, 2)
    return call(
        final_kernel,
        jax.ShapeDtypeStruct((4, rows, columns // groups), jnp.float32),
        [VMEM] * 4,
        [in_vmem(value) for value in (kept01, arrived01, kept2, arrived2)],
        spans=(((0, 8, 16), (16, 0, 8)), ((0, 24, 8),)),
        depth="depth",
    )


def solution(mesh):
    return jax.shard_map(
        on_device,
        mesh=mesh,
        in_specs=(P("depth", "row", None), P()),
        out_specs=P(None, "row", "depth"),
        check_vma=False,
    )
```

time: 80.3 us -> 61.1 us (0.76)
  the two profiles are of different devices: /device:TPU:30 before, /device:TPU:0 now
where the time goes in v3:
time: 61.1 us; the launch traced here: 60.9 us
  Pallas kernels  32.2 us (53%)
  starting transfers between devices  17.5 us (29%)
  waiting for transfers between devices  9.71 us (16%)
  local copies, waits for them, and re-layouts  1.27 us (2%)
    pallas_call x14, Pallas kernels, call(): pl.pallas_call(functools.partial(body, **kwargs), out_shape=out_shape, in...  32.2 us
    ppermute x8, waiting for transfers between devices, swap(): return lax.ppermute(value, 'depth', partners[step])  9.1 us
    ppermute x4, starting transfers between devices, ring(): lax.ppermute(value, axis, [(i, (i + step) % count) for i in range(count)])  9.02 us
    ppermute x8, starting transfers between devices, swap(): return lax.ppermute(value, 'depth', partners[step])  8.52 us
    squeeze x1, local copies, waits for them, and re-layouts, on_device(): after = ring(volume[0], 'depth', groups, -1)  1.27 us
  transfers between devices with their start and end apart: 12, of which 3 were waited for; matrix products, arithmetic and copies ran while one was open for 0% of the time, Pallas kernels for 52%

profile of v3, /device:TPU:0, one launch (start us, length us, event | category | flops | bytes accessed | tf_op | source)
XLA Modules:
  0.0 60.9 jit_solution(15609526839817556200)
XLA Ops:
  0.0 1.3 %slice_bitcast_fusion = (f32[32,4096]{1,0:T(8,128)S(1)}, f32[32,4096]{1,0:T(8,128)S(1)}) fusion(f32[32,32,4096]{2,1,0:T(8,128)} %volume_ref.1), kind=kLoop, calls=%fused_computation | loop fusion | bytes 2097152 | tf_op jit(solution)/shard_map/squeeze | solution.py:342
  1.3 3.6 %collective-permute-start.1 = (f32[32,4096]{1,0:T(8,128)S(1)}, f32[32,4096]{1,0:T(8,128)S(1)}, u32[]{:S(2)}, u32[]{:S(2)}) collective-permute-start(f32[32,4096]{1,0:T(8,128)S(1)} %get-tuple-element.43), channel_id=1, source_target_pairs={{0,112},{16,0},{32,16},{48,32},{64,48},{80,64},{96,80},{112,96},{1... | collective-permute-start | bytes 1572872 | tf_op jit(solution)/shard_map/ppermute | solution.py:339
  4.9 7.1 %shard_map.28 = (f32[34,32,48,128]{3,2,1,0:T(8,128)S(1)}, f32[24,8,128]{2,1,0:T(8,128)S(1)}, f32[4,8,4096]{2,1,0:T(8,128)S(1)}, f32[32,4096]{1,0:T(8,128)S(1)}, f32[32,4096]{1,0:T(8,128)S(1)}) custom-call(f32[32,32,4096]{2,1,0:T(8,128)} %volume_ref.1, f32[3,8]{1,0:T(4,128)} %palette_ref.1), custom_call_target="tpu_custom_call" | custom-call | tf_op jit(solution)/shard_map/pallas_call | solution.py:320
  12.0 1.6 %collective-permute-start.4 = (f32[32,4096]{1,0:T(8,128)S(1)}, f32[32,4096]{1,0:T(8,128)S(1)}, u32[]{:S(2)}, u32[]{:S(2)}) collective-permute-start(f32[32,4096]{1,0:T(8,128)S(1)} %get-tuple-element.29), channel_id=1, source_target_pairs={{0,1},{1,2},{2,3},{3,4},{4,5},{5,6},{6,7},{7,8},{8,9},{9,10},{10,1... | collective-permute-start | bytes 1572872 | tf_op jit(solution)/shard_map/ppermute | solution.py:339
  13.7 3.8 %collective-permute-start.8 = (f32[32,4096]{1,0:T(8,128)S(1)}, f32[32,4096]{1,0:T(8,128)S(1)}, u32[]{:S(2)}, u32[]{:S(2)}) collective-permute-start(f32[32,4096]{1,0:T(8,128)S(1)} %get-tuple-element.36), channel_id=1, source_target_pairs={{0,15},{1,0},{2,1},{3,2},{4,3},{5,4},{6,5},{7,6},{8,7},{9,8},{10,9... | collective-permute-start | bytes 1572872 | tf_op jit(solution)/shard_map/ppermute | solution.py:339
  17.4 2.3 %shard_map.29.second_ref = f32[4,8,4096]{2,1,0:T(8,128)S(1)} custom-call(f32[34,32,48,128]{3,2,1,0:T(8,128)S(1)} %get-tuple-element.24.vb.vb_in, f32[24,8,128]{2,1,0:T(8,128)S(1)} %get-tuple-element.26.coef_ref), custom_call_target="tpu_custom_call" | custom-call | tf_op jit(solution)/shard_map/pallas_call | solution.py:320
  19.8 3.7 %shard_map.31 = f32[4,16,2048]{2,1,0:T(8,128)S(1)} custom-call(f32[34,32,48,128]{3,2,1,0:T(8,128)S(1)} %get-tuple-element.24.vb.vb_in, f32[32,4096]{1,0:T(8,128)S(1)} %collective-permute-done.prev_ref, f32[32,4096]{1,0:T(8,128)S(1)} %collective-permute-done.1.next_ref, f32[4,8,4096]{2,1,0:T(8,128)S(1)} %get-tuple-element.25.first_ref, ...), custom_call_target="tpu_custom_call" | custom-call | tf_op jit(solution)/shard_map/pallas_call | solution.py:320
  23.5 0.1 collective-permute-start.2
  23.6 3.7 %shard_map.30.refs_0_.behind_ref = f32[4,16,2048]{2,1,0:T(8,128)S(1)} custom-call(f32[34,32,48,128]{3,2,1,0:T(8,128)S(1)} %get-tuple-element.24.vb.vb_in, f32[32,4096]{1,0:T(8,128)S(1)} %collective-permute-done.prev_ref, f32[32,4096]{1,0:T(8,128)S(1)} %collective-permute-done.1.next_ref, f32[4,8,4096]{2,1,0:T(8,128)S(1)} %get-tuple-element.25.first_ref, ...), custom_call_target="tpu_custom_call" | custom-call | tf_op jit(solution)/shard_map/pallas_call | solution.py:320
  27.4 0.6 collective-permute-done.4.edge_ref
  28.0 3.8 %shard_map.33 = (f32[34,32,48,128]{3,2,1,0:T(8,128)S(1)}, f32[4,8,2048]{2,1,0:T(8,128)S(1)}) custom-call(f32[34,32,48,128]{3,2,1,0:T(8,128)S(1)} %get-tuple-element.24.vb.vb_in, f32[32,4096]{1,0:T(8,128)S(1)} %collective-permute-done.prev_ref, f32[32,4096]{1,0:T(8,128)S(1)} %collective-permute-done.1.next_ref, ...), custom_call_target="tpu_custom_call", output_to_operand_aliasing={{0}: (0, {})} | custom-call | tf_op jit(solution)/shard_map/pallas_call | solution.py:320
  31.8 0.1 collective-permute-start.5
  31.8 3.4 %shard_map.34.refs_0_.behind_ref = f32[4,8,2048]{2,1,0:T(8,128)S(1)} custom-call(f32[34,32,48,128]{3,2,1,0:T(8,128)S(1)} %get-tuple-element.30.vb.vb_in, f32[32,4096]{1,0:T(8,128)S(1)} %collective-permute-done.prev_ref, f32[32,4096]{1,0:T(8,128)S(1)} %collective-permute-done.1.next_ref, f32[24,8,128]{2,1,0:T(8,128)S(1)} %get-tuple-element.26.coef_ref), custom_call_target="tpu_custom_call" | custom-call | tf_op jit(solution)/shard_map/pallas_call | solution.py:320
  35.3 3.8 %shard_map.37 = (f32[34,32,48,128]{3,2,1,0:T(8,128)S(1)}, f32[4,8,2048]{2,1,0:T(8,128)S(1)}) custom-call(f32[34,32,48,128]{3,2,1,0:T(8,128)S(1)} %get-tuple-element.30.vb.vb_in, f32[32,4096]{1,0:T(8,128)S(1)} %collective-permute-done.prev_ref, f32[32,4096]{1,0:T(8,128)S(1)} %collective-permute-done.1.next_ref, ...), custom_call_target="tpu_custom_call", output_to_operand_aliasing={{0}: (0, {})} | custom-call | tf_op jit(solution)/shard_map/pallas_call | solution.py:320
  39.1 0.6 collective-permute-start.9
  39.7 0.6 %collective-permute-start.3 = (f32[4,16,1024]{2,1,0:T(8,128)S(1)}, f32[4,16,1024]{2,1,0:T(8,128)S(1)}, u32[]{:S(2)}, u32[]{:S(2)}) collective-permute-start(f32[4,16,1024]{2,1,0:T(8,128)S(1)} %get-tuple-element.28), channel_id=1, source_target_pairs={{0,32},{16,48},{32,0},{48,16},{64,96},{80,112},{96,64},{112,80},{1... | collective-permute-start | bytes 786440 | tf_op jit(solution)/shard_map/ppermute | solution.py:371
  40.4 1.6 %collective-permute-start.6 = (f32[4,8,1024]{2,1,0:T(8,128)S(1)}, f32[4,8,1024]{2,1,0:T(8,128)S(1)}, u32[]{:S(2)}, u32[]{:S(2)}) collective-permute-start(f32[4,8,1024]{2,1,0:T(8,128)S(1)} %get-tuple-element.33), channel_id=1, source_target_pairs={{0,32},{16,48},{32,0},{48,16},{64,96},{80,112},{96,64},{112,80},{1... | collective-permute-start | bytes 393224 | tf_op jit(solution)/shard_map/ppermute | solution.py:371
  41.9 3.4 %shard_map.38.refs_0_ = f32[4,8,2048]{2,1,0:T(8,128)S(1)} custom-call(f32[34,32,48,128]{3,2,1,0:T(8,128)S(1)} %get-tuple-element.37.vb, f32[32,4096]{1,0:T(8,128)S(1)} %collective-permute-done.prev_ref, f32[32,4096]{1,0:T(8,128)S(1)} %collective-permute-done.1.next_ref, f32[24,8,128]{2,1,0:T(8,128)S(1)} %get-tuple-element.26.coef_ref), custom_call_target="tpu_custom_call" | custom-call | tf_op jit(solution)/shard_map/pallas_call | solution.py:320
  45.4 0.6 %collective-permute-start.10 = (f32[4,8,1024]{2,1,0:T(8,128)S(1)}, f32[4,8,1024]{2,1,0:T(8,128)S(1)}, u32[]{:S(2)}, u32[]{:S(2)}) collective-permute-start(f32[4,8,1024]{2,1,0:T(8,128)S(1)} %get-tuple-element.40), channel_id=1, source_target_pairs={{0,32},{16,48},{32,0},{48,16},{64,96},{80,112},{96,64},{112,80},{1... | collective-permute-start | bytes 393224 | tf_op jit(solution)/shard_map/ppermute | solution.py:371
  46.0 5.7 %collective-permute-done.6.refs_3_ = f32[4,8,1024]{2,1,0:T(8,128)S(1)} collective-permute-done((f32[4,8,1024]{2,1,0:T(8,128)S(1)}, f32[4,8,1024]{2,1,0:T(8,128)S(1)}, u32[]{:S(2)}, u32[]{:S(2)}) %collective-permute-start.6) | collective-permute-done | bytes 131104 | tf_op jit(solution)/shard_map/ppermute | solution.py:371
  51.8 2.7 %collective-permute-start.7 = (f32[4,24,512]{2,1,0:T(8,128)S(1)}, f32[4,24,512]{2,1,0:T(8,128)S(1)}, u32[]{:S(2)}, u32[]{:S(2)}) collective-permute-start(f32[4,24,512]{2,1,0:T(8,128)S(1)} %get-tuple-element.35), channel_id=1, source_target_pairs={{0,96},{16,112},{32,64},{48,80},{64,32},{80,48},{96,0},{112,16},{1... | collective-permute-start | bytes 589832 | tf_op jit(solution)/shard_map/ppermute | solution.py:371
  54.6 2.2 %collective-permute-start.11 = (f32[4,8,512]{2,1,0:T(8,128)S(1)}, f32[4,8,512]{2,1,0:T(8,128)S(1)}, u32[]{:S(2)}, u32[]{:S(2)}) collective-permute-start(f32[4,8,512]{2,1,0:T(8,128)S(1)} %get-tuple-element.42), channel_id=1, source_target_pairs={{0,96},{16,112},{32,64},{48,80},{64,32},{80,48},{96,0},{112,16},{1... | collective-permute-start | bytes 196616 | tf_op jit(solution)/shard_map/ppermute | solution.py:371
  56.8 3.4 %collective-permute-done.11.refs_3_ = f32[4,8,512]{2,1,0:T(8,128)S(1)} collective-permute-done((f32[4,8,512]{2,1,0:T(8,128)S(1)}, f32[4,8,512]{2,1,0:T(8,128)S(1)}, u32[]{:S(2)}, u32[]{:S(2)}) %collective-permute-start.11) | collective-permute-done | bytes 65568 | tf_op jit(solution)/shard_map/ppermute | solution.py:371
  60.2 0.7 %shard_map.41 = f32[4,32,512]{2,1,0:T(8,128)} custom-call(f32[4,24,512]{2,1,0:T(8,128)S(1)} %get-tuple-element.34.refs_0_, f32[4,24,512]{2,1,0:T(8,128)S(1)} %collective-permute-done.7.refs_1_, f32[4,8,512]{2,1,0:T(8,128)S(1)} %get-tuple-element.41.refs_2_, f32[4,8,512]{2,1,0:T(8,128)S(1)} %collective-permute-done.11.refs_3_), custom_call_target="tpu_custom_call" | custom-call | tf_op jit(solution)/shard_map/pallas_call | solution.py:320
  (15 shorter events, 0.2 us)
Async XLA Ops:
  1.3 18.5 %collective-permute-start.1 = (f32[32,4096]{1,0:T(8,128)S(1)}, f32[32,4096]{1,0:T(8,128)S(1)}, u32[]{:S(2)}, u32[]{:S(2)}) collective-permute-start(f32[32,4096]{1,0:T(8,128)S(1)} %get-tuple-element.43), channel_id=1, source_target_pairs={{0,112},{16,0},{32,16},{48,32},{64,48},{80,64},{96,80},{112,96},{1... | collective-permute-start | bytes 1572872 | tf_op jit(solution)/shard_map/ppermute | solution.py:339
  4.9 14.9 %collective-permute-start = (f32[32,4096]{1,0:T(8,128)S(1)}, f32[32,4096]{1,0:T(8,128)S(1)}, u32[]{:S(2)}, u32[]{:S(2)}) collective-permute-start(f32[32,4096]{1,0:T(8,128)S(1)} %get-tuple-element.44), channel_id=1, source_target_pairs={{0,16},{16,32},{32,48},{48,64},{64,80},{80,96},{96,112},{112,0},{1... | collective-permute-start | bytes 1572872 | tf_op jit(solution)/shard_map/ppermute | solution.py:339
  12.0 15.9 %collective-permute-start.4 = (f32[32,4096]{1,0:T(8,128)S(1)}, f32[32,4096]{1,0:T(8,128)S(1)}, u32[]{:S(2)}, u32[]{:S(2)}) collective-permute-start(f32[32,4096]{1,0:T(8,128)S(1)} %get-tuple-element.29), channel_id=1, source_target_pairs={{0,1},{1,2},{2,3},{3,4},{4,5},{5,6},{6,7},{7,8},{8,9},{9,10},{10,1... | collective-permute-start | bytes 1572872 | tf_op jit(solution)/shard_map/ppermute | solution.py:339
  13.7 21.6 %collective-permute-start.8 = (f32[32,4096]{1,0:T(8,128)S(1)}, f32[32,4096]{1,0:T(8,128)S(1)}, u32[]{:S(2)}, u32[]{:S(2)}) collective-permute-start(f32[32,4096]{1,0:T(8,128)S(1)} %get-tuple-element.36), channel_id=1, source_target_pairs={{0,15},{1,0},{2,1},{3,2},{4,3},{5,4},{6,5},{7,6},{8,7},{9,8},{10,9... | collective-permute-start | bytes 1572872 | tf_op jit(solution)/shard_map/ppermute | solution.py:339
  23.5 16.1 %collective-permute-start.2 = (f32[4,16,2048]{2,1,0:T(8,128)S(1)}, f32[4,16,2048]{2,1,0:T(8,128)S(1)}, u32[]{:S(2)}, u32[]{:S(2)}) collective-permute-start(f32[4,16,2048]{2,1,0:T(8,128)S(1)} %shard_map.31), channel_id=1, source_target_pairs={{0,16},{16,0},{32,48},{48,32},{64,80},{80,64},{96,112},{112,96},{1... | collective-permute-start | bytes 1572872 | tf_op jit(solution)/shard_map/ppermute | solution.py:371
  31.8 8.6 %collective-permute-start.5 = (f32[4,8,2048]{2,1,0:T(8,128)S(1)}, f32[4,8,2048]{2,1,0:T(8,128)S(1)}, u32[]{:S(2)}, u32[]{:S(2)}) collective-permute-start(f32[4,8,2048]{2,1,0:T(8,128)S(1)} %get-tuple-element.31), channel_id=1, source_target_pairs={{0,16},{16,0},{32,48},{48,32},{64,80},{80,64},{96,112},{112,96},{1... | collective-permute-start | bytes 786440 | tf_op jit(solution)/shard_map/ppermute | solution.py:371
  39.1 6.2 %collective-permute-start.9 = (f32[4,8,2048]{2,1,0:T(8,128)S(1)}, f32[4,8,2048]{2,1,0:T(8,128)S(1)}, u32[]{:S(2)}, u32[]{:S(2)}) collective-permute-start(f32[4,8,2048]{2,1,0:T(8,128)S(1)} %get-tuple-element.38), channel_id=1, source_target_pairs={{0,16},{16,0},{32,48},{48,32},{64,80},{80,64},{96,112},{112,96},{1... | collective-permute-start | bytes 786440 | tf_op jit(solution)/shard_map/ppermute | solution.py:371
  39.7 12.1 %collective-permute-start.3 = (f32[4,16,1024]{2,1,0:T(8,128)S(1)}, f32[4,16,1024]{2,1,0:T(8,128)S(1)}, u32[]{:S(2)}, u32[]{:S(2)}) collective-permute-start(f32[4,16,1024]{2,1,0:T(8,128)S(1)} %get-tuple-element.28), channel_id=1, source_target_pairs={{0,32},{16,48},{32,0},{48,16},{64,96},{80,112},{96,64},{112,80},{1... | collective-permute-start | bytes 786440 | tf_op jit(solution)/shard_map/ppermute | solution.py:371
  40.4 11.4 %collective-permute-start.6 = (f32[4,8,1024]{2,1,0:T(8,128)S(1)}, f32[4,8,1024]{2,1,0:T(8,128)S(1)}, u32[]{:S(2)}, u32[]{:S(2)}) collective-permute-start(f32[4,8,1024]{2,1,0:T(8,128)S(1)} %get-tuple-element.33), channel_id=1, source_target_pairs={{0,32},{16,48},{32,0},{48,16},{64,96},{80,112},{96,64},{112,80},{1... | collective-permute-start | bytes 393224 | tf_op jit(solution)/shard_map/ppermute | solution.py:371
  45.4 9.2 %collective-permute-start.10 = (f32[4,8,1024]{2,1,0:T(8,128)S(1)}, f32[4,8,1024]{2,1,0:T(8,128)S(1)}, u32[]{:S(2)}, u32[]{:S(2)}) collective-permute-start(f32[4,8,1024]{2,1,0:T(8,128)S(1)} %get-tuple-element.40), channel_id=1, source_target_pairs={{0,32},{16,48},{32,0},{48,16},{64,96},{80,112},{96,64},{112,80},{1... | collective-permute-start | bytes 393224 | tf_op jit(solution)/shard_map/ppermute | solution.py:371
  51.8 8.4 %collective-permute-start.7 = (f32[4,24,512]{2,1,0:T(8,128)S(1)}, f32[4,24,512]{2,1,0:T(8,128)S(1)}, u32[]{:S(2)}, u32[]{:S(2)}) collective-permute-start(f32[4,24,512]{2,1,0:T(8,128)S(1)} %get-tuple-element.35), channel_id=1, source_target_pairs={{0,96},{16,112},{32,64},{48,80},{64,32},{80,48},{96,0},{112,16},{1... | collective-permute-start | bytes 589832 | tf_op jit(solution)/shard_map/ppermute | solution.py:371
  54.6 5.6 %collective-permute-start.11 = (f32[4,8,512]{2,1,0:T(8,128)S(1)}, f32[4,8,512]{2,1,0:T(8,128)S(1)}, u32[]{:S(2)}, u32[]{:S(2)}) collective-permute-start(f32[4,8,512]{2,1,0:T(8,128)S(1)} %get-tuple-element.42), channel_id=1, source_target_pairs={{0,96},{16,112},{32,64},{48,80},{64,32},{80,48},{96,0},{112,16},{1... | collective-permute-start | bytes 196616 | tf_op jit(solution)/shard_map/ppermute | solution.py:371

commit v4 on v3

--- a/solution.py
+++ b/solution.py
@@ -17,8 +17,7 @@
 TO_Y = 4.0 / 3.0
 TO_X = 20.0 / 9.0
 AMBIENT = 0.25 / 0.27
-AHEAD = 10
-SPLIT = 20
+AHEAD = 16
 VMEM = pl.BlockSpec(memory_space=pltpu.VMEM)
 ANY = pl.BlockSpec(memory_space=pl.ANY)
 HBM = pl.BlockSpec(memory_space=pltpu.HBM)
@@ -117,11 +116,21 @@
         early_ref[k, :, tile_lanes(c)] = value
 
 
-def stage_kernel(volume_ref, palette_ref, vb, coef_ref, early_ref, top_ref, bottom_ref, palette, sem, palette_sem, *, scale):
+def edge_kernel(volume_ref, *refs):
+    *outs, sem = refs
+    planes, rows, _ = volume_ref.shape
+    sources = [volume_ref.at[:, 0, :], volume_ref.at[:, rows - 1, :], volume_ref.at[0], volume_ref.at[planes - 1]]
+    copies = [pltpu.make_async_copy(source, out, sem.at[i]) for i, (source, out) in enumerate(zip(sources, outs))]
+    for copy in copies:
+        copy.start()
+    for copy in copies:
+        copy.wait()
+
+
+def stage_kernel(volume_ref, palette_ref, vb, coef_ref, early_ref, palette, sem, palette_sem, *, scale):
     planes, rows, columns = volume_ref.shape
     tiles = columns // LANES
     bumps = palette_ref.shape[1]
-    flat = vb.reshape(tiles + 2, planes * STAGED, LANES)
 
     def copy(c):
         return pltpu.make_async_copy(
@@ -142,15 +151,13 @@
             coef_ref[k * bumps + j] = jnp.full((SUBLANES, LANES), weight, jnp.float32)
 
     def arrive(c):
-        copy(c).wait()
+        @pl.when(c < tiles)
+        def _():
+            copy(c).wait()
 
         @pl.when(c + AHEAD < tiles)
         def _():
             copy(c + AHEAD).start()
-
-        for z in range(0, planes, 8):
-            for out, row in ((top_ref, BELOW), (bottom_ref, BELOW + rows - 1)):
-                out[z : z + 8, tile_lanes(c)] = flat[c + 1, pl.ds(z * STAGED + row, 8, stride=STAGED), :]
 
     arrive(0)
 
@@ -161,39 +168,18 @@
             march_early(vb, coef_ref, early_ref, c, planes, scale)
         return 0
 
-    lax.fori_loop(0, SPLIT // 2, body, 0)
-
-    def rest(c, _):
-        arrive(c)
-        return 0
-
-    lax.fori_loop(SPLIT + 1, tiles, rest, 0)
-
-
-def early_kernel(vb, coef_ref, early_ref, *, scale, planes):
-    tiles = vb.shape[0] - 2
-
-    def body(i, _):
-        for c in (2 * i, 2 * i + 1):
-            march_early(vb, coef_ref, early_ref, c, planes, scale)
-        return 0
-
-    lax.fori_loop(SPLIT // 2, tiles // 2, body, 0)
-
-
-def place_of(block):
-    chip = block // 2
-    return 2 * ((chip ^ (chip // 2)) % 2) + chip // 2
-
-
-def half_tiles(m, tiles, parity, unroll):
+    lax.fori_loop(0, tiles // 2, body, 0)
+
+
+def group_of(chip):
+    return (chip ^ (chip // 2)) % 2
+
+
+def tile_at(place, tiles, parity):
     per_block = tiles // 8
-    out = []
-    for i in range(unroll):
-        at = m * unroll + i
-        block = 2 * (at // per_block) + parity
-        out.append((block * per_block + at % per_block, place_of(block) * per_block + at % per_block))
-    return out
+    position = place // per_block
+    chip = jnp.where(position < 2, 3 * position, position - 1)
+    return (2 * chip + parity) * per_block + place % per_block
 
 
 def depth_ends(prev_ref, next_ref, index, groups):
@@ -207,43 +193,45 @@
     return ends
 
 
-def middle_kernel(vb, prev_ref, next_ref, first_ref, second_ref, coef_ref, out_ref, *, scale, planes, depth, groups, send):
+def middle_kernel(vb, prev_ref, next_ref, early_ref, coef_ref, out_ref, *, scale, planes, depth, groups, send):
     tiles = vb.shape[0] - 2
     index = lax.axis_index(depth)
     ends = depth_ends(prev_ref, next_ref, index, groups)
     parity = (index + send) % 2
 
     def body(m, _):
-        for c, place in half_tiles(m, tiles, parity, 2):
+        for place in (2 * m, 2 * m + 1):
+            c = tile_at(place, tiles, parity)
             moments, passed = march(vb, c, 2, planes, scale, ends(c, 2))
             for k, value in enumerate(contracted(coef_ref, moments) + [passed]):
                 out_ref[k, 8:16, tile_lanes(place)] = value
-            early = [
-                jnp.where(c < SPLIT, first_ref[k, :, tile_lanes(c)], second_ref[k, :, tile_lanes(c)]) for k in range(4)
-            ]
-            moments = march_ends(vb, c, 1, planes, scale, ends(c, 1), early[3])
+            passed = early_ref[3, :, tile_lanes(c)]
+            moments = march_ends(vb, c, 1, planes, scale, ends(c, 1), passed)
             for k, color in enumerate(contracted(coef_ref, moments)):
-                out_ref[k, 0:8, tile_lanes(place)] = early[k] + color
-            out_ref[3, 0:8, tile_lanes(place)] = early[3]
+                out_ref[k, 0:8, tile_lanes(place)] = early_ref[k, :, tile_lanes(c)] + color
+            out_ref[3, 0:8, tile_lanes(place)] = passed
         return 0
 
     lax.fori_loop(0, tiles // 4, body, 0)
 
 
-def outer_tiles(vb, prev_ref, next_ref, coef_ref, out_ref, *, scale, planes, depth, groups, send, group):
+def outer_tiles(vb, prev_ref, next_ref, coef_ref, out_ref, *, scale, planes, depth, groups, part, group):
     tiles = vb.shape[0] - 2
     index = lax.axis_index(depth)
     ends = depth_ends(prev_ref, next_ref, index, groups)
-    parity = (index + send) % 2
+    parity = (index + (part == 0)) % 2
+    mine = group_of(index // 2)
+    first = {0: 0, 1: (1 - mine) * (tiles // 4), 2: mine * (tiles // 4)}[part]
 
     def body(m, _):
-        for c, place in half_tiles(m, tiles, parity, 2):
+        for at in (2 * m, 2 * m + 1):
+            c = tile_at(first + at, tiles, parity)
             moments, passed = march(vb, c, group, planes, scale, ends(c, group))
             for k, value in enumerate(contracted(coef_ref, moments) + [passed]):
-                out_ref[k, :, tile_lanes(place)] = value
+                out_ref[k, :, tile_lanes(at)] = value
         return 0
 
-    lax.fori_loop(0, tiles // 4, body, 0)
+    lax.fori_loop(0, out_ref.shape[2] // (2 * LANES), body, 0)
 
 
 def outer_kernel(vb_in, prev_ref, next_ref, edge_ref, behind_ref, coef_ref, vb, out_ref, *, row, stacks, group, **kwargs):
@@ -260,11 +248,7 @@
         return 0
 
     lax.fori_loop(0, tiles, place, 0)
-    outer_tiles(vb, prev_ref, next_ref, coef_ref, out_ref, send=1, group=group, **kwargs)
-
-
-def outer_rest_kernel(vb, prev_ref, next_ref, coef_ref, out_ref, **kwargs):
-    outer_tiles(vb, prev_ref, next_ref, coef_ref, out_ref, send=0, **kwargs)
+    outer_tiles(vb, prev_ref, next_ref, coef_ref, out_ref, part=0, group=group, **kwargs)
 
 
 def blend(front, back, lanes):
@@ -279,7 +263,7 @@
     chip = index // 2
     width = keep_ref.shape[2]
     if step == 0:
-        in_front, half = index % 2 == 0, (chip ^ (chip // 2)) % 2
+        in_front, half = index % 2 == 0, group_of(chip)
     else:
         in_front, half = chip % 2 == 0, chip // 2
     keep_lanes = pl.ds(pl.multiple_of(half * width, width), width)
@@ -296,6 +280,22 @@
                     for k, value in enumerate(blend(front, back, lanes)):
                         out_ref[k, row : row + count, :] = value
                 row += count
+
+
+def fold_kernel(mine_ref, theirs_ref, out_ref, *, depth, send):
+    index = lax.axis_index(depth)
+    width = out_ref.shape[2]
+    group = group_of(index // 2)
+    group = 1 - group if send else group
+    lanes = pl.ds(pl.multiple_of(group * width, width), width)
+    mine, theirs = mine_ref, theirs_ref.at[:, :, lanes]
+    for mine_first in (True, False):
+
+        @pl.when((index % 2 == 0) == mine_first)
+        def _():
+            front, back = (mine, theirs) if mine_first else (theirs, mine)
+            for k, value in enumerate(blend(front, back, slice(None))):
+                out_ref[k] = value
 
 
 def final_kernel(*refs, spans, depth):
@@ -338,17 +338,26 @@
     def ring(value, axis, count, step):
         return lax.ppermute(value, axis, [(i, (i + step) % count) for i in range(count)])
 
-    before = ring(volume[-1], "depth", groups, 1)
-    after = ring(volume[0], "depth", groups, -1)
     staged = vmem_shape(tiles + 2, planes, STAGED, LANES)
     strip = vmem_shape(4, SUBLANES, columns)
-    edge = vmem_shape(planes, columns)
     to_hbm = lambda value: pltpu.with_memory_space_constraint(value, pltpu.HBM)
-    vb, coef, first, top, bottom = call(
+    volume = to_hbm(volume)
+    low, high, front, back = call(
+        edge_kernel,
+        (vmem_shape(planes, columns),) * 2 + (vmem_shape(rows, columns),) * 2,
+        [HBM],
+        (volume,),
+        scratch=[pltpu.SemaphoreType.DMA((4,))],
+    )
+    above = in_vmem(ring(high, "row", stacks, 1))
+    below = in_vmem(ring(low, "row", stacks, -1))
+    before = in_vmem(ring(back, "depth", groups, 1))
+    after = in_vmem(ring(front, "depth", groups, -1))
+    vb, coef, early = call(
         stage_kernel,
-        (staged, vmem_shape(palette.size, SUBLANES, LANES), strip, edge, edge),
+        (staged, vmem_shape(palette.size, SUBLANES, LANES), strip),
         [HBM, HBM],
-        (to_hbm(volume), to_hbm(palette)),
+        (volume, to_hbm(palette)),
         scratch=[
             pltpu.SMEM(palette.shape, jnp.float32),
             pltpu.SemaphoreType.DMA((tiles,)),
@@ -356,34 +365,28 @@
         ],
         scale=scale,
     )
-    above = in_vmem(ring(bottom, "row", stacks, 1))
-    below = in_vmem(ring(top, "row", stacks, -1))
-    common = dict(scale=scale, planes=planes)
     coef = in_vmem(coef)
-    second = call(early_kernel, strip, [VMEM, VMEM], (in_vmem(vb), coef), **common)
-    common.update(depth="depth", groups=groups)
-    before, after = in_vmem(before), in_vmem(after)
-    half = lambda count: vmem_shape(4, count, columns // 2)
+    common = dict(scale=scale, planes=planes, depth="depth", groups=groups)
     pairs = lambda other: [(i, other(i)) for i in range(groups)]
     partners = [pairs(lambda i: i ^ 1), pairs(lambda i: i ^ 2), pairs(lambda i: groups - 2 - i // 2 * 2 + i % 2)]
 
     def swap(value, step):
-        return lax.ppermute(value, "depth", partners[step])
+        return in_vmem(lax.ppermute(value, "depth", partners[step]))
 
     def middle(send):
         return call(
             middle_kernel,
-            half(16),
-            [VMEM] * 6,
-            (in_vmem(vb), before, after, in_vmem(first), in_vmem(second), coef),
+            vmem_shape(4, 16, columns // 2),
+            [VMEM] * 5,
+            (in_vmem(vb), before, after, in_vmem(early), coef),
             send=send,
             **common,
         )
 
-    def outer(vb, edge, behind, group):
+    def outer_first(vb, edge, behind, group):
         return call(
             outer_kernel,
-            (staged, half(8)),
+            (staged, vmem_shape(4, 8, columns // 2)),
             [VMEM] * 4 + [ANY, VMEM],
             (in_vmem(vb), before, after, edge, behind, coef),
             aliases={0: 0},
@@ -393,8 +396,19 @@
             **common,
         )
 
-    def outer_rest(vb, group):
-        return call(outer_rest_kernel, half(8), [VMEM] * 4, (in_vmem(vb), before, after, coef), group=group, **common)
+    def outer(vb, group, part):
+        return call(
+            outer_tiles,
+            vmem_shape(4, 8, columns // 4),
+            [VMEM] * 4,
+            (in_vmem(vb), before, after, coef),
+            group=group,
+            part=part,
+            **common,
+        )
+
+    def fold(mine, theirs, send):
+        return call(fold_kernel, vmem_shape(*mine.shape), [VMEM] * 2, (in_vmem(mine), theirs), depth="depth", send=send)
 
     def merged(given, step):
         channels, _, width = given[0].shape
@@ -404,23 +418,20 @@
         )
 
     arrived0 = swap(middle(1), 0)
-    kept0 = middle(0)
-    behind = kept0
-    kept0, send = merged([kept0, arrived0], 0)
+    behind = middle(0)
+    kept0, send = merged([behind, arrived0], 0)
     arrived0 = swap(send, 1)
-    vb, send = outer(vb, above, behind, 0)
-    arrived1 = swap(send, 0)
-    kept1 = outer_rest(vb, 0)
-    behind = kept1
-    kept1, send = merged([kept1, arrived1], 0)
-    arrived1 = swap(send, 1)
-    vb, send = outer(vb, below, behind, 3)
-    arrived2 = swap(send, 0)
+    vb, send = outer_first(vb, above, behind, 0)
+    partner1 = swap(send, 0)
+    behind = outer(vb, 0, 1)
+    arrived1 = swap(fold(behind, partner1, 1), 1)
+    vb, send = outer_first(vb, below, behind, 3)
+    partner2 = swap(send, 0)
+    arrived2 = swap(fold(outer(vb, 3, 1), partner2, 1), 1)
+    kept1 = fold(outer(vb, 0, 2), partner1, 0)
     kept01, send = merged([kept0, arrived0, kept1, arrived1], 1)
     arrived01 = swap(send, 2)
-    kept2 = outer_rest(vb, 3)
-    kept2, send = merged([kept2, arrived2], 0)
-    arrived2 = swap(send, 1)
+    kept2 = fold(outer(vb, 3, 2), partner2, 0)
     kept2, send = merged([kept2, arrived2], 1)
     arrived2 = swap(send, 2)
     return call(

time: 61.1 us -> 59.2 us (0.969)
  starting transfers between devices: 17.5 us -> 15.5 us
  local copies, waits for them, and re-layouts: 1.27 us -> 0 us
  waiting for transfers between devices: 9.71 us -> 10.6 us
    ppermute x8, starting transfers between devices: 8.52 us -> 6.58 us  [swap(): return in_vmem(lax.ppermute(value, 'depth', partners[step]))]
    ppermute x8, waiting for transfers between devices: 9.1 us -> 10.6 us  [swap(): return in_vmem(lax.ppermute(value, 'depth', partners[step]))]
    squeeze x1 -> x0, local copies, waits for them, and re-layouts: 1.27 us -> none  [on_device(): after = ring(volume[0], 'depth', groups, -1)]
    pallas_call x14 -> x18, Pallas kernels: 32.2 us -> 32.7 us  [call(): pl.pallas_call(functools.partial(body, **kwargs), out_shape=out_shape, in...]
  transfers between devices with their start and end apart: 12 -> 12, of which waited for: 3 -> 2; matrix products, arithmetic and copies ran while one was open for 0% -> 0% of each run, Pallas kernels for 52% -> 51%
where the time goes in v4:
time: 59.2 us; the launch traced here: 59.1 us
  Pallas kernels  32.7 us (55%)
  starting transfers between devices  15.5 us (26%)
  waiting for transfers between devices  10.6 us (18%)
    pallas_call x18, Pallas kernels, call(): pl.pallas_call(functools.partial(body, **kwargs), out_shape=out_shape, in...  32.7 us
    ppermute x8, waiting for transfers between devices, swap(): return in_vmem(lax.ppermute(value, 'depth', partners[step]))  10.6 us
    ppermute x4, starting transfers between devices, ring(): lax.ppermute(value, axis, [(i, (i + step) % count) for i in range(count)])  8.97 us
    ppermute x8, starting transfers between devices, swap(): return in_vmem(lax.ppermute(value, 'depth', partners[step]))  6.58 us
  transfers between devices with their start and end apart: 12, of which 2 were waited for; matrix products, arithmetic and copies ran while one was open for 0% of the time, Pallas kernels for 51%

profile of v4, /device:TPU:0, one launch (start us, length us, event | category | flops | bytes accessed | tf_op | source)
XLA Modules:
  0.0 59.1 jit_solution(8031957540640914839)
XLA Ops:
  0.0 1.6 %shard_map.29 = (f32[32,4096]{1,0:T(8,128)S(1)}, f32[32,4096]{1,0:T(8,128)S(1)}, f32[32,4096]{1,0:T(8,128)S(1)}, f32[32,4096]{1,0:T(8,128)S(1)}) custom-call(f32[32,32,4096]{2,1,0:T(8,128)} %volume_ref.3), custom_call_target="tpu_custom_call" | custom-call | tf_op jit(solution)/shard_map/pallas_call | solution.py:320
  1.6 3.6 %collective-permute-start.1 = (f32[32,4096]{1,0:T(8,128)S(1)}, f32[32,4096]{1,0:T(8,128)S(1)}, u32[]{:S(2)}, u32[]{:S(2)}) collective-permute-start(f32[32,4096]{1,0:T(8,128)S(1)} %get-tuple-element.24), channel_id=1, source_target_pairs={{0,112},{16,0},{32,16},{48,32},{64,48},{80,64},{96,80},{112,96},{1... | collective-permute-start | bytes 1572872 | tf_op jit(solution)/shard_map/ppermute | solution.py:339
  5.2 1.6 %collective-permute-start.4 = (f32[32,4096]{1,0:T(8,128)S(1)}, f32[32,4096]{1,0:T(8,128)S(1)}, u32[]{:S(2)}, u32[]{:S(2)}) collective-permute-start(f32[32,4096]{1,0:T(8,128)S(1)} %get-tuple-element.29), channel_id=1, source_target_pairs={{0,1},{1,2},{2,3},{3,4},{4,5},{5,6},{6,7},{7,8},{8,9},{9,10},{10,1... | collective-permute-start | bytes 1572872 | tf_op jit(solution)/shard_map/ppermute | solution.py:339
  6.8 3.8 %collective-permute-start.5 = (f32[32,4096]{1,0:T(8,128)S(1)}, f32[32,4096]{1,0:T(8,128)S(1)}, u32[]{:S(2)}, u32[]{:S(2)}) collective-permute-start(f32[32,4096]{1,0:T(8,128)S(1)} %get-tuple-element.31), channel_id=1, source_target_pairs={{0,15},{1,0},{2,1},{3,2},{4,3},{5,4},{6,5},{7,6},{8,7},{9,8},{10,9... | collective-permute-start | bytes 1572872 | tf_op jit(solution)/shard_map/ppermute | solution.py:339
  10.6 8.2 %shard_map.28 = (f32[34,32,48,128]{3,2,1,0:T(8,128)S(1)}, f32[24,8,128]{2,1,0:T(8,128)S(1)}, f32[4,8,4096]{2,1,0:T(8,128)S(1)}) custom-call(f32[32,32,4096]{2,1,0:T(8,128)} %volume_ref.3, f32[3,8]{1,0:T(4,128)} %palette_ref.1), custom_call_target="tpu_custom_call" | custom-call | tf_op jit(solution)/shard_map/pallas_call | solution.py:320
  18.8 3.7 %shard_map.31 = f32[4,16,2048]{2,1,0:T(8,128)S(1)} custom-call(f32[34,32,48,128]{3,2,1,0:T(8,128)S(1)} %get-tuple-element.22.vb.vb_in, f32[32,4096]{1,0:T(8,128)S(1)} %collective-permute-done.prev_ref, f32[32,4096]{1,0:T(8,128)S(1)} %collective-permute-done.1.next_ref, f32[4,8,4096]{2,1,0:T(8,128)S(1)} %get-tuple-element.25.early_ref, ...), custom_call_target="tpu_custom_call" | custom-call | tf_op jit(solution)/shard_map/pallas_call | solution.py:320
  22.6 0.1 collective-permute-start.2
  22.6 3.7 %shard_map.30.refs_0_.behind_ref = f32[4,16,2048]{2,1,0:T(8,128)S(1)} custom-call(f32[34,32,48,128]{3,2,1,0:T(8,128)S(1)} %get-tuple-element.22.vb.vb_in, f32[32,4096]{1,0:T(8,128)S(1)} %collective-permute-done.prev_ref, f32[32,4096]{1,0:T(8,128)S(1)} %collective-permute-done.1.next_ref, f32[4,8,4096]{2,1,0:T(8,128)S(1)} %get-tuple-element.25.early_ref, ...), custom_call_target="tpu_custom_call" | custom-call | tf_op jit(solution)/shard_map/pallas_call | solution.py:320
  26.4 3.8 %shard_map.33 = (f32[34,32,48,128]{3,2,1,0:T(8,128)S(1)}, f32[4,8,2048]{2,1,0:T(8,128)S(1)}) custom-call(f32[34,32,48,128]{3,2,1,0:T(8,128)S(1)} %get-tuple-element.22.vb.vb_in, f32[32,4096]{1,0:T(8,128)S(1)} %collective-permute-done.prev_ref, f32[32,4096]{1,0:T(8,128)S(1)} %collective-permute-done.1.next_ref, ...), custom_call_target="tpu_custom_call", output_to_operand_aliasing={{0}: (0, {})} | custom-call | tf_op jit(solution)/shard_map/pallas_call | solution.py:320
  30.2 0.5 collective-permute-start.6
  30.7 1.7 %shard_map.34.behind_ref.mine_ref = f32[4,8,1024]{2,1,0:T(8,128)S(1)} custom-call(f32[34,32,48,128]{3,2,1,0:T(8,128)S(1)} %get-tuple-element.30.vb.vb_in, f32[32,4096]{1,0:T(8,128)S(1)} %collective-permute-done.prev_ref, f32[32,4096]{1,0:T(8,128)S(1)} %collective-permute-done.1.next_ref, f32[24,8,128]{2,1,0:T(8,128)S(1)} %get-tuple-element.26.coef_ref), custom_call_target="tpu_custom_call" | custom-call | tf_op jit(solution)/shard_map/pallas_call | solution.py:320
  32.4 3.8 %shard_map.35 = (f32[34,32,48,128]{3,2,1,0:T(8,128)S(1)}, f32[4,8,2048]{2,1,0:T(8,128)S(1)}) custom-call(f32[34,32,48,128]{3,2,1,0:T(8,128)S(1)} %get-tuple-element.30.vb.vb_in, f32[32,4096]{1,0:T(8,128)S(1)} %collective-permute-done.prev_ref, f32[32,4096]{1,0:T(8,128)S(1)} %collective-permute-done.1.next_ref, ...), custom_call_target="tpu_custom_call", output_to_operand_aliasing={{0}: (0, {})} | custom-call | tf_op jit(solution)/shard_map/pallas_call | solution.py:320
  36.3 0.1 collective-permute-start.9
  36.5 0.2 collective-permute-start.3
  36.7 1.9 %collective-permute-start.7 = (f32[4,8,1024]{2,1,0:T(8,128)S(1)}, f32[4,8,1024]{2,1,0:T(8,128)S(1)}, u32[]{:S(2)}, u32[]{:S(2)}) collective-permute-start(f32[4,8,1024]{2,1,0:T(8,128)S(1)} %shard_map.38), channel_id=1, source_target_pairs={{0,32},{16,48},{32,0},{48,16},{64,96},{80,112},{96,64},{112,80},{1... | collective-permute-start | bytes 393224 | tf_op jit(solution)/shard_map/ppermute | solution.py:374
  38.7 1.7 %shard_map.42.mine_ref = f32[4,8,1024]{2,1,0:T(8,128)S(1)} custom-call(f32[34,32,48,128]{3,2,1,0:T(8,128)S(1)} %get-tuple-element.32.vb, f32[32,4096]{1,0:T(8,128)S(1)} %collective-permute-done.prev_ref, f32[32,4096]{1,0:T(8,128)S(1)} %collective-permute-done.1.next_ref, f32[24,8,128]{2,1,0:T(8,128)S(1)} %get-tuple-element.26.coef_ref), custom_call_target="tpu_custom_call" | custom-call | tf_op jit(solution)/shard_map/pallas_call | solution.py:320
  40.4 1.7 %shard_map.36.mine_ref = f32[4,8,1024]{2,1,0:T(8,128)S(1)} custom-call(f32[34,32,48,128]{3,2,1,0:T(8,128)S(1)} %get-tuple-element.32.vb, f32[32,4096]{1,0:T(8,128)S(1)} %collective-permute-done.prev_ref, f32[32,4096]{1,0:T(8,128)S(1)} %collective-permute-done.1.next_ref, f32[24,8,128]{2,1,0:T(8,128)S(1)} %get-tuple-element.26.coef_ref), custom_call_target="tpu_custom_call" | custom-call | tf_op jit(solution)/shard_map/pallas_call | solution.py:320
  42.2 0.2 collective-permute-start.10
  42.5 6.1 %collective-permute-done.7.refs_3_ = f32[4,8,1024]{2,1,0:T(8,128)S(1)} collective-permute-done((f32[4,8,1024]{2,1,0:T(8,128)S(1)}, f32[4,8,1024]{2,1,0:T(8,128)S(1)}, u32[]{:S(2)}, u32[]{:S(2)}) %collective-permute-start.7) | collective-permute-done | bytes 131104 | tf_op jit(solution)/shard_map/ppermute | solution.py:374
  48.6 2.4 %collective-permute-start.8 = (f32[4,24,512]{2,1,0:T(8,128)S(1)}, f32[4,24,512]{2,1,0:T(8,128)S(1)}, u32[]{:S(2)}, u32[]{:S(2)}) collective-permute-start(f32[4,24,512]{2,1,0:T(8,128)S(1)} %get-tuple-element.35), channel_id=1, source_target_pairs={{0,96},{16,112},{32,64},{48,80},{64,32},{80,48},{96,0},{112,16},{1... | collective-permute-start | bytes 589832 | tf_op jit(solution)/shard_map/ppermute | solution.py:374
  50.9 1.7 %shard_map.40.mine_ref = f32[4,8,1024]{2,1,0:T(8,128)S(1)} custom-call(f32[34,32,48,128]{3,2,1,0:T(8,128)S(1)} %get-tuple-element.32.vb, f32[32,4096]{1,0:T(8,128)S(1)} %collective-permute-done.prev_ref, f32[32,4096]{1,0:T(8,128)S(1)} %collective-permute-done.1.next_ref, f32[24,8,128]{2,1,0:T(8,128)S(1)} %get-tuple-element.26.coef_ref), custom_call_target="tpu_custom_call" | custom-call | tf_op jit(solution)/shard_map/pallas_call | solution.py:320
  52.8 1.0 %collective-permute-start.11 = (f32[4,8,512]{2,1,0:T(8,128)S(1)}, f32[4,8,512]{2,1,0:T(8,128)S(1)}, u32[]{:S(2)}, u32[]{:S(2)}) collective-permute-start(f32[4,8,512]{2,1,0:T(8,128)S(1)} %get-tuple-element.38), channel_id=1, source_target_pairs={{0,96},{16,112},{32,64},{48,80},{64,32},{80,48},{96,0},{112,16},{1... | collective-permute-start | bytes 196616 | tf_op jit(solution)/shard_map/ppermute | solution.py:374
  53.8 4.5 %collective-permute-done.11.refs_3_ = f32[4,8,512]{2,1,0:T(8,128)S(1)} collective-permute-done((f32[4,8,512]{2,1,0:T(8,128)S(1)}, f32[4,8,512]{2,1,0:T(8,128)S(1)}, u32[]{:S(2)}, u32[]{:S(2)}) %collective-permute-start.11) | collective-permute-done | bytes 65568 | tf_op jit(solution)/shard_map/ppermute | solution.py:374
  58.3 0.7 %shard_map.45 = f32[4,32,512]{2,1,0:T(8,128)} custom-call(f32[4,24,512]{2,1,0:T(8,128)S(1)} %get-tuple-element.34.refs_0_, f32[4,24,512]{2,1,0:T(8,128)S(1)} %collective-permute-done.8.refs_1_, f32[4,8,512]{2,1,0:T(8,128)S(1)} %get-tuple-element.37.refs_2_, f32[4,8,512]{2,1,0:T(8,128)S(1)} %collective-permute-done.11.refs_3_), custom_call_target="tpu_custom_call" | custom-call | tf_op jit(solution)/shard_map/pallas_call | solution.py:320
  (18 shorter events, 0.3 us)
Async XLA Ops:
  1.6 17.2 %collective-permute-start = (f32[32,4096]{1,0:T(8,128)S(1)}, f32[32,4096]{1,0:T(8,128)S(1)}, u32[]{:S(2)}, u32[]{:S(2)}) collective-permute-start(f32[32,4096]{1,0:T(8,128)S(1)} %get-tuple-element.23), channel_id=1, source_target_pairs={{0,16},{16,32},{32,48},{48,64},{64,80},{80,96},{96,112},{112,0},{1... | collective-permute-start | bytes 1572872 | tf_op jit(solution)/shard_map/ppermute | solution.py:339
  1.6 17.2 %collective-permute-start.1 = (f32[32,4096]{1,0:T(8,128)S(1)}, f32[32,4096]{1,0:T(8,128)S(1)}, u32[]{:S(2)}, u32[]{:S(2)}) collective-permute-start(f32[32,4096]{1,0:T(8,128)S(1)} %get-tuple-element.24), channel_id=1, source_target_pairs={{0,112},{16,0},{32,16},{48,32},{64,48},{80,64},{96,80},{112,96},{1... | collective-permute-start | bytes 1572872 | tf_op jit(solution)/shard_map/ppermute | solution.py:339
  5.2 21.1 %collective-permute-start.4 = (f32[32,4096]{1,0:T(8,128)S(1)}, f32[32,4096]{1,0:T(8,128)S(1)}, u32[]{:S(2)}, u32[]{:S(2)}) collective-permute-start(f32[32,4096]{1,0:T(8,128)S(1)} %get-tuple-element.29), channel_id=1, source_target_pairs={{0,1},{1,2},{2,3},{3,4},{4,5},{5,6},{6,7},{7,8},{8,9},{9,10},{10,1... | collective-permute-start | bytes 1572872 | tf_op jit(solution)/shard_map/ppermute | solution.py:339
  6.8 25.6 %collective-permute-start.5 = (f32[32,4096]{1,0:T(8,128)S(1)}, f32[32,4096]{1,0:T(8,128)S(1)}, u32[]{:S(2)}, u32[]{:S(2)}) collective-permute-start(f32[32,4096]{1,0:T(8,128)S(1)} %get-tuple-element.31), channel_id=1, source_target_pairs={{0,15},{1,0},{2,1},{3,2},{4,3},{5,4},{6,5},{7,6},{8,7},{9,8},{10,9... | collective-permute-start | bytes 1572872 | tf_op jit(solution)/shard_map/ppermute | solution.py:339
  22.6 13.9 %collective-permute-start.2 = (f32[4,16,2048]{2,1,0:T(8,128)S(1)}, f32[4,16,2048]{2,1,0:T(8,128)S(1)}, u32[]{:S(2)}, u32[]{:S(2)}) collective-permute-start(f32[4,16,2048]{2,1,0:T(8,128)S(1)} %shard_map.31), channel_id=1, source_target_pairs={{0,16},{16,0},{32,48},{48,32},{64,80},{80,64},{96,112},{112,96},{1... | collective-permute-start | bytes 1572872 | tf_op jit(solution)/shard_map/ppermute | solution.py:374
  30.2 6.5 %collective-permute-start.6 = (f32[4,8,2048]{2,1,0:T(8,128)S(1)}, f32[4,8,2048]{2,1,0:T(8,128)S(1)}, u32[]{:S(2)}, u32[]{:S(2)}) collective-permute-start(f32[4,8,2048]{2,1,0:T(8,128)S(1)} %get-tuple-element.33), channel_id=1, source_target_pairs={{0,16},{16,0},{32,48},{48,32},{64,80},{80,64},{96,112},{112,96},{1... | collective-permute-start | bytes 786440 | tf_op jit(solution)/shard_map/ppermute | solution.py:374
  36.3 5.9 %collective-permute-start.9 = (f32[4,8,2048]{2,1,0:T(8,128)S(1)}, f32[4,8,2048]{2,1,0:T(8,128)S(1)}, u32[]{:S(2)}, u32[]{:S(2)}) collective-permute-start(f32[4,8,2048]{2,1,0:T(8,128)S(1)} %get-tuple-element.36), channel_id=1, source_target_pairs={{0,16},{16,0},{32,48},{48,32},{64,80},{80,64},{96,112},{112,96},{1... | collective-permute-start | bytes 786440 | tf_op jit(solution)/shard_map/ppermute | solution.py:374
  36.5 12.1 %collective-permute-start.3 = (f32[4,16,1024]{2,1,0:T(8,128)S(1)}, f32[4,16,1024]{2,1,0:T(8,128)S(1)}, u32[]{:S(2)}, u32[]{:S(2)}) collective-permute-start(f32[4,16,1024]{2,1,0:T(8,128)S(1)} %get-tuple-element.28), channel_id=1, source_target_pairs={{0,32},{16,48},{32,0},{48,16},{64,96},{80,112},{96,64},{112,80},{1... | collective-permute-start | bytes 786440 | tf_op jit(solution)/shard_map/ppermute | solution.py:374
  36.7 11.8 %collective-permute-start.7 = (f32[4,8,1024]{2,1,0:T(8,128)S(1)}, f32[4,8,1024]{2,1,0:T(8,128)S(1)}, u32[]{:S(2)}, u32[]{:S(2)}) collective-permute-start(f32[4,8,1024]{2,1,0:T(8,128)S(1)} %shard_map.38), channel_id=1, source_target_pairs={{0,32},{16,48},{32,0},{48,16},{64,96},{80,112},{96,64},{112,80},{1... | collective-permute-start | bytes 393224 | tf_op jit(solution)/shard_map/ppermute | solution.py:374
  42.2 10.5 %collective-permute-start.10 = (f32[4,8,1024]{2,1,0:T(8,128)S(1)}, f32[4,8,1024]{2,1,0:T(8,128)S(1)}, u32[]{:S(2)}, u32[]{:S(2)}) collective-permute-start(f32[4,8,1024]{2,1,0:T(8,128)S(1)} %shard_map.43), channel_id=1, source_target_pairs={{0,32},{16,48},{32,0},{48,16},{64,96},{80,112},{96,64},{112,80},{1... | collective-permute-start | bytes 393224 | tf_op jit(solution)/shard_map/ppermute | solution.py:374
  48.6 9.7 %collective-permute-start.8 = (f32[4,24,512]{2,1,0:T(8,128)S(1)}, f32[4,24,512]{2,1,0:T(8,128)S(1)}, u32[]{:S(2)}, u32[]{:S(2)}) collective-permute-start(f32[4,24,512]{2,1,0:T(8,128)S(1)} %get-tuple-element.35), channel_id=1, source_target_pairs={{0,96},{16,112},{32,64},{48,80},{64,32},{80,48},{96,0},{112,16},{1... | collective-permute-start | bytes 589832 | tf_op jit(solution)/shard_map/ppermute | solution.py:374
  52.8 5.6 %collective-permute-start.11 = (f32[4,8,512]{2,1,0:T(8,128)S(1)}, f32[4,8,512]{2,1,0:T(8,128)S(1)}, u32[]{:S(2)}, u32[]{:S(2)}) collective-permute-start(f32[4,8,512]{2,1,0:T(8,128)S(1)} %get-tuple-element.38), channel_id=1, source_target_pairs={{0,96},{16,112},{32,64},{48,80},{64,32},{80,48},{96,0},{112,16},{1... | collective-permute-start | bytes 196616 | tf_op jit(solution)/shard_map/ppermute | solution.py:374

commit v5 on v4

--- a/solution.py
+++ b/solution.py
@@ -193,35 +193,45 @@
     return ends
 
 
-def middle_kernel(vb, prev_ref, next_ref, early_ref, coef_ref, out_ref, *, scale, planes, depth, groups, send):
+def first_place(index, tiles, part):
+    mine = group_of(index // 2)
+    half = index // 4 if part == 3 else 1 - index // 4
+    quarter = tiles // 4
+    first = {0: 0, 1: (1 - mine) * quarter}.get(part, mine * quarter + half * (quarter // 2))
+    return first, (index + (part == 0)) % 2
+
+
+def width_of(columns, part):
+    return columns // (2, 4, 8, 8)[part]
+
+
+def middle_kernel(vb, prev_ref, next_ref, early_ref, coef_ref, out_ref, *, scale, planes, depth, groups, part):
     tiles = vb.shape[0] - 2
     index = lax.axis_index(depth)
     ends = depth_ends(prev_ref, next_ref, index, groups)
-    parity = (index + send) % 2
+    first, parity = first_place(index, tiles, part)
 
     def body(m, _):
-        for place in (2 * m, 2 * m + 1):
-            c = tile_at(place, tiles, parity)
+        for at in (2 * m, 2 * m + 1):
+            c = tile_at(first + at, tiles, parity)
             moments, passed = march(vb, c, 2, planes, scale, ends(c, 2))
             for k, value in enumerate(contracted(coef_ref, moments) + [passed]):
-                out_ref[k, 8:16, tile_lanes(place)] = value
+                out_ref[k, 8:16, tile_lanes(at)] = value
             passed = early_ref[3, :, tile_lanes(c)]
             moments = march_ends(vb, c, 1, planes, scale, ends(c, 1), passed)
             for k, color in enumerate(contracted(coef_ref, moments)):
-                out_ref[k, 0:8, tile_lanes(place)] = early_ref[k, :, tile_lanes(c)] + color
-            out_ref[3, 0:8, tile_lanes(place)] = passed
+                out_ref[k, 0:8, tile_lanes(at)] = early_ref[k, :, tile_lanes(c)] + color
+            out_ref[3, 0:8, tile_lanes(at)] = passed
         return 0
 
-    lax.fori_loop(0, tiles // 4, body, 0)
+    lax.fori_loop(0, out_ref.shape[2] // (2 * LANES), body, 0)
 
 
 def outer_tiles(vb, prev_ref, next_ref, coef_ref, out_ref, *, scale, planes, depth, groups, part, group):
     tiles = vb.shape[0] - 2
     index = lax.axis_index(depth)
     ends = depth_ends(prev_ref, next_ref, index, groups)
-    parity = (index + (part == 0)) % 2
-    mine = group_of(index // 2)
-    first = {0: 0, 1: (1 - mine) * (tiles // 4), 2: mine * (tiles // 4)}[part]
+    first, parity = first_place(index, tiles, part)
 
     def body(m, _):
         for at in (2 * m, 2 * m + 1):
@@ -257,37 +267,10 @@
     return out + [passed * back[3, :, lanes]]
 
 
-def merge_kernel(*refs, depth, step):
-    *given, keep_ref, send_ref = refs
-    index = lax.axis_index(depth)
-    chip = index // 2
-    width = keep_ref.shape[2]
-    if step == 0:
-        in_front, half = index % 2 == 0, group_of(chip)
-    else:
-        in_front, half = chip % 2 == 0, chip // 2
-    keep_lanes = pl.ds(pl.multiple_of(half * width, width), width)
-    send_lanes = pl.ds(pl.multiple_of((1 - half) * width, width), width)
-    for mine_first in (True, False):
-
-        @pl.when(in_front == mine_first)
-        def _():
-            row = 0
-            for mine_ref, theirs_ref in zip(given[::2], given[1::2]):
-                count = mine_ref.shape[1]
-                front, back = (mine_ref, theirs_ref) if mine_first else (theirs_ref, mine_ref)
-                for out_ref, lanes in ((send_ref, send_lanes), (keep_ref, keep_lanes)):
-                    for k, value in enumerate(blend(front, back, lanes)):
-                        out_ref[k, row : row + count, :] = value
-                row += count
-
-
-def fold_kernel(mine_ref, theirs_ref, out_ref, *, depth, send):
+def fold_kernel(mine_ref, theirs_ref, out_ref, *, depth):
     index = lax.axis_index(depth)
     width = out_ref.shape[2]
-    group = group_of(index // 2)
-    group = 1 - group if send else group
-    lanes = pl.ds(pl.multiple_of(group * width, width), width)
+    lanes = pl.ds(pl.multiple_of((1 - group_of(index // 2)) * width, width), width)
     mine, theirs = mine_ref, theirs_ref.at[:, :, lanes]
     for mine_first in (True, False):
 
@@ -298,20 +281,47 @@
                 out_ref[k] = value
 
 
-def final_kernel(*refs, spans, depth):
-    out_ref = refs[-1]
+def block_kernel(*refs, depth, part):
+    *given, out_ref = refs
+    index = lax.axis_index(depth)
+    chip = index // 2
+    width = out_ref.shape[2]
+    half = chip // 2 if part == 3 else 1 - chip // 2
+    lanes = lambda block: pl.ds(pl.multiple_of(block * width, width), width)
+    row = 0
+    for mine_ref, core_ref, chip_ref in zip(given[::3], given[1::3], given[2::3]):
+        rows = pl.ds(row, mine_ref.shape[1])
+        out = out_ref.at[:, rows, :]
+        core, beside = core_ref.at[:, :, lanes(2 * group_of(chip) + half)], chip_ref.at[:, :, lanes(half)]
+        for theirs, mine, at in ((core, mine_ref, index), (beside, out, chip)):
+            for mine_first in (True, False):
+
+                @pl.when((at % 2 == 0) == mine_first)
+                def _():
+                    front, back = (mine, theirs) if mine_first else (theirs, mine)
+                    for k, value in enumerate(blend(front, back, slice(None))):
+                        out[k] = value
+
+        row += mine_ref.shape[1]
+
+
+def final_kernel(mine_ref, *refs, spans, depth):
+    *given, out_ref = refs
     chip = lax.axis_index(depth) // 2
     for mine_first in (True, False):
 
         @pl.when((chip < 2) == mine_first)
         def _():
-            for i, parts in enumerate(spans):
-                front, back = (refs[2 * i], refs[2 * i + 1]) if mine_first else (refs[2 * i + 1], refs[2 * i])
+            first = 0
+            for theirs, parts in zip(given, spans):
+                mine = mine_ref.at[:, pl.ds(first, theirs.shape[1]), :]
+                front, back = (mine, theirs) if mine_first else (theirs, mine)
                 values = blend(front, back, slice(None))
                 values[3] = 1.0 - values[3]
                 for at, row, count in parts:
                     for k, value in enumerate(values):
                         out_ref[k, row : row + count, :] = value[at : at + count]
+                first += theirs.shape[1]
 
 
 def call(body, out_shape, in_specs, args, scratch=(), aliases=None, limit=4, **kwargs):
@@ -373,14 +383,16 @@
     def swap(value, step):
         return in_vmem(lax.ppermute(value, "depth", partners[step]))
 
-    def middle(send):
-        return call(
-            middle_kernel,
-            vmem_shape(4, 16, columns // 2),
-            [VMEM] * 5,
-            (in_vmem(vb), before, after, in_vmem(early), coef),
-            send=send,
-            **common,
+    def middle(part, vb):
+        return in_vmem(
+            call(
+                middle_kernel,
+                vmem_shape(4, 16, width_of(columns, part)),
+                [VMEM] * 5,
+                (in_vmem(vb), before, after, in_vmem(early), coef),
+                part=part,
+                **common,
+            )
         )
 
     def outer_first(vb, edge, behind, group):
@@ -397,48 +409,46 @@
         )
 
     def outer(vb, group, part):
+        return in_vmem(
+            call(
+                outer_tiles,
+                vmem_shape(4, 8, width_of(columns, part)),
+                [VMEM] * 4,
+                (in_vmem(vb), before, after, coef),
+                group=group,
+                part=part,
+                **common,
+            )
+        )
+
+    def fold(mine, theirs):
+        return call(fold_kernel, vmem_shape(*mine.shape), [VMEM] * 2, (mine, theirs), depth="depth")
+
+    def blocks(given, part):
+        count = sum(value.shape[1] for value in given[::3])
         return call(
-            outer_tiles,
-            vmem_shape(4, 8, columns // 4),
-            [VMEM] * 4,
-            (in_vmem(vb), before, after, coef),
-            group=group,
-            part=part,
-            **common,
+            block_kernel, vmem_shape(4, count, columns // groups), [VMEM] * len(given), given, depth="depth", part=part
         )
 
-    def fold(mine, theirs, send):
-        return call(fold_kernel, vmem_shape(*mine.shape), [VMEM] * 2, (in_vmem(mine), theirs), depth="depth", send=send)
-
-    def merged(given, step):
-        channels, _, width = given[0].shape
-        shape = (vmem_shape(channels, sum(value.shape[1] for value in given[::2]), width // 2),) * 2
-        return call(
-            merge_kernel, shape, [VMEM] * len(given), [in_vmem(value) for value in given], depth="depth", step=step
-        )
-
-    arrived0 = swap(middle(1), 0)
-    behind = middle(0)
-    kept0, send = merged([behind, arrived0], 0)
-    arrived0 = swap(send, 1)
+    core0 = swap(middle(0, vb), 0)
+    behind = middle(1, vb)
+    chip0 = swap(fold(behind, core0), 1)
     vb, send = outer_first(vb, above, behind, 0)
-    partner1 = swap(send, 0)
+    core1 = swap(send, 0)
     behind = outer(vb, 0, 1)
-    arrived1 = swap(fold(behind, partner1, 1), 1)
+    chip1 = swap(fold(behind, core1), 1)
     vb, send = outer_first(vb, below, behind, 3)
-    partner2 = swap(send, 0)
-    arrived2 = swap(fold(outer(vb, 3, 1), partner2, 1), 1)
-    kept1 = fold(outer(vb, 0, 2), partner1, 0)
-    kept01, send = merged([kept0, arrived0, kept1, arrived1], 1)
-    arrived01 = swap(send, 2)
-    kept2 = fold(outer(vb, 3, 2), partner2, 0)
-    kept2, send = merged([kept2, arrived2], 1)
-    arrived2 = swap(send, 2)
+    core2 = swap(send, 0)
+    chip2 = swap(fold(outer(vb, 3, 1), core2), 1)
+    far01 = swap(blocks([middle(2, vb), core0, chip0, outer(vb, 0, 2), core1, chip1], 2), 2)
+    middle_mine = middle(3, vb)
+    far2 = swap(blocks([outer(vb, 3, 2), core2, chip2], 2), 2)
+    mine = [middle_mine, core0, chip0, outer(vb, 0, 3), core1, chip1, outer(vb, 3, 3), core2, chip2]
     return call(
         final_kernel,
         jax.ShapeDtypeStruct((4, rows, columns // groups), jnp.float32),
-        [VMEM] * 4,
-        [in_vmem(value) for value in (kept01, arrived01, kept2, arrived2)],
+        [VMEM] * 3,
+        (in_vmem(blocks(mine, 3)), far01, far2),
         spans=(((0, 8, 16), (16, 0, 8)), ((0, 24, 8),)),
         depth="depth",
     )

time: 59.2 us -> 56.5 us (0.954)
  waiting for transfers between devices: 10.6 us -> 7.43 us
    ppermute x8, waiting for transfers between devices: 10.6 us -> 7.42 us  [swap(): return in_vmem(lax.ppermute(value, 'depth', partners[step]))]
    pallas_call x18 -> x21, Pallas kernels: 32.7 us -> 32.9 us  [call(): pl.pallas_call(functools.partial(body, **kwargs), out_shape=out_shape, in...]
  transfers between devices with their start and end apart: 12 -> 12, of which waited for: 2 -> 2; matrix products, arithmetic and copies ran while one was open for 0% -> 0% of each run, Pallas kernels for 51% -> 54%
where the time goes in v5:
time: 56.5 us; the launch traced here: 56.3 us
  Pallas kernels  32.9 us (58%)
  starting transfers between devices  15.8 us (28%)
  waiting for transfers between devices  7.43 us (13%)
    pallas_call x21, Pallas kernels, call(): pl.pallas_call(functools.partial(body, **kwargs), out_shape=out_shape, in...  32.9 us
    ppermute x4, starting transfers between devices, ring(): lax.ppermute(value, axis, [(i, (i + step) % count) for i in range(count)])  8.97 us
    ppermute x8, waiting for transfers between devices, swap(): return in_vmem(lax.ppermute(value, 'depth', partners[step]))  7.42 us
    ppermute x8, starting transfers between devices, swap(): return in_vmem(lax.ppermute(value, 'depth', partners[step]))  6.84 us
  transfers between devices with their start and end apart: 12, of which 2 were waited for; matrix products, arithmetic and copies ran while one was open for 0% of the time, Pallas kernels for 54%

profile of v5, /device:TPU:0, one launch (start us, length us, event | category | flops | bytes accessed | tf_op | source)
XLA Modules:
  0.0 56.3 jit_solution(539709355529035983)
XLA Ops:
  0.0 1.6 %shard_map.29 = (f32[32,4096]{1,0:T(8,128)S(1)}, f32[32,4096]{1,0:T(8,128)S(1)}, f32[32,4096]{1,0:T(8,128)S(1)}, f32[32,4096]{1,0:T(8,128)S(1)}) custom-call(f32[32,32,4096]{2,1,0:T(8,128)} %volume_ref.3), custom_call_target="tpu_custom_call" | custom-call | tf_op jit(solution)/shard_map/pallas_call | solution.py:330
  1.6 3.6 %collective-permute-start.1 = (f32[32,4096]{1,0:T(8,128)S(1)}, f32[32,4096]{1,0:T(8,128)S(1)}, u32[]{:S(2)}, u32[]{:S(2)}) collective-permute-start(f32[32,4096]{1,0:T(8,128)S(1)} %get-tuple-element.18), channel_id=1, source_target_pairs={{0,112},{16,0},{32,16},{48,32},{64,48},{80,64},{96,80},{112,96},{1... | collective-permute-start | bytes 1572872 | tf_op jit(solution)/shard_map/ppermute | solution.py:349
  5.2 1.6 %collective-permute-start.2 = (f32[32,4096]{1,0:T(8,128)S(1)}, f32[32,4096]{1,0:T(8,128)S(1)}, u32[]{:S(2)}, u32[]{:S(2)}) collective-permute-start(f32[32,4096]{1,0:T(8,128)S(1)} %get-tuple-element.19), channel_id=1, source_target_pairs={{0,1},{1,2},{2,3},{3,4},{4,5},{5,6},{6,7},{7,8},{8,9},{9,10},{10,1... | collective-permute-start | bytes 1572872 | tf_op jit(solution)/shard_map/ppermute | solution.py:349
  6.8 3.8 %collective-permute-start.3 = (f32[32,4096]{1,0:T(8,128)S(1)}, f32[32,4096]{1,0:T(8,128)S(1)}, u32[]{:S(2)}, u32[]{:S(2)}) collective-permute-start(f32[32,4096]{1,0:T(8,128)S(1)} %get-tuple-element.23), channel_id=1, source_target_pairs={{0,15},{1,0},{2,1},{3,2},{4,3},{5,4},{6,5},{7,6},{8,7},{9,8},{10,9... | collective-permute-start | bytes 1572872 | tf_op jit(solution)/shard_map/ppermute | solution.py:349
  10.6 8.2 %shard_map.28 = (f32[34,32,48,128]{3,2,1,0:T(8,128)S(1)}, f32[24,8,128]{2,1,0:T(8,128)S(1)}, f32[4,8,4096]{2,1,0:T(8,128)S(1)}) custom-call(f32[32,32,4096]{2,1,0:T(8,128)} %volume_ref.3, f32[3,8]{1,0:T(4,128)} %palette_ref.1), custom_call_target="tpu_custom_call" | custom-call | tf_op jit(solution)/shard_map/pallas_call | solution.py:330
  18.8 3.7 %shard_map.35 = f32[4,16,2048]{2,1,0:T(8,128)S(1)} custom-call(f32[34,32,48,128]{3,2,1,0:T(8,128)S(1)} %get-tuple-element.16.vb.vb_in, f32[32,4096]{1,0:T(8,128)S(1)} %collective-permute-done.prev_ref, f32[32,4096]{1,0:T(8,128)S(1)} %collective-permute-done.1.next_ref, f32[4,8,4096]{2,1,0:T(8,128)S(1)} %get-tuple-element.20.early_ref, ...), custom_call_target="tpu_custom_call" | custom-call | tf_op jit(solution)/shard_map/pallas_call | solution.py:330
  22.6 1.9 %shard_map.30.behind_ref.mine_ref = f32[4,16,1024]{2,1,0:T(8,128)S(1)} custom-call(f32[34,32,48,128]{3,2,1,0:T(8,128)S(1)} %get-tuple-element.16.vb.vb_in, f32[32,4096]{1,0:T(8,128)S(1)} %collective-permute-done.prev_ref, f32[32,4096]{1,0:T(8,128)S(1)} %collective-permute-done.1.next_ref, f32[4,8,4096]{2,1,0:T(8,128)S(1)} %get-tuple-element.20.early_ref, ...), custom_call_target="tpu_custom_call" | custom-call | tf_op jit(solution)/shard_map/pallas_call | solution.py:330
  24.5 3.8 %shard_map.31 = (f32[34,32,48,128]{3,2,1,0:T(8,128)S(1)}, f32[4,8,2048]{2,1,0:T(8,128)S(1)}) custom-call(f32[34,32,48,128]{3,2,1,0:T(8,128)S(1)} %get-tuple-element.16.vb.vb_in, f32[32,4096]{1,0:T(8,128)S(1)} %collective-permute-done.prev_ref, f32[32,4096]{1,0:T(8,128)S(1)} %collective-permute-done.1.next_ref, ...), custom_call_target="tpu_custom_call", output_to_operand_aliasing={{0}: (0, {})} | custom-call | tf_op jit(solution)/shard_map/pallas_call | solution.py:330
  28.4 0.5 collective-permute-start.6
  28.9 1.7 %shard_map.32.behind_ref.mine_ref = f32[4,8,1024]{2,1,0:T(8,128)S(1)} custom-call(f32[34,32,48,128]{3,2,1,0:T(8,128)S(1)} %get-tuple-element.22.vb.vb_in, f32[32,4096]{1,0:T(8,128)S(1)} %collective-permute-done.prev_ref, f32[32,4096]{1,0:T(8,128)S(1)} %collective-permute-done.1.next_ref, f32[24,8,128]{2,1,0:T(8,128)S(1)} %get-tuple-element.21.coef_ref), custom_call_target="tpu_custom_call" | custom-call | tf_op jit(solution)/shard_map/pallas_call | solution.py:330
  30.6 3.8 %shard_map.33 = (f32[34,32,48,128]{3,2,1,0:T(8,128)S(1)}, f32[4,8,2048]{2,1,0:T(8,128)S(1)}) custom-call(f32[34,32,48,128]{3,2,1,0:T(8,128)S(1)} %get-tuple-element.22.vb.vb_in, f32[32,4096]{1,0:T(8,128)S(1)} %collective-permute-done.prev_ref, f32[32,4096]{1,0:T(8,128)S(1)} %collective-permute-done.1.next_ref, ...), custom_call_target="tpu_custom_call", output_to_operand_aliasing={{0}: (0, {})} | custom-call | tf_op jit(solution)/shard_map/pallas_call | solution.py:330
  34.9 1.9 %collective-permute-start.7 = (f32[4,8,1024]{2,1,0:T(8,128)S(1)}, f32[4,8,1024]{2,1,0:T(8,128)S(1)}, u32[]{:S(2)}, u32[]{:S(2)}) collective-permute-start(f32[4,8,1024]{2,1,0:T(8,128)S(1)} %shard_map.38), channel_id=1, source_target_pairs={{0,32},{16,48},{32,0},{48,16},{64,96},{80,112},{96,64},{112,80},{1... | collective-permute-start | bytes 393224 | tf_op jit(solution)/shard_map/ppermute | solution.py:384
  36.8 0.8 %shard_map.44.refs_3_ = f32[4,8,512]{2,1,0:T(8,128)S(1)} custom-call(f32[34,32,48,128]{3,2,1,0:T(8,128)S(1)} %get-tuple-element.24.vb, f32[32,4096]{1,0:T(8,128)S(1)} %collective-permute-done.prev_ref, f32[32,4096]{1,0:T(8,128)S(1)} %collective-permute-done.1.next_ref, f32[24,8,128]{2,1,0:T(8,128)S(1)} %get-tuple-element.21.coef_ref), custom_call_target="tpu_custom_call" | custom-call | tf_op jit(solution)/shard_map/pallas_call | solution.py:330
  37.7 1.0 %shard_map.43.refs_0_ = f32[4,16,512]{2,1,0:T(8,128)S(1)} custom-call(f32[34,32,48,128]{3,2,1,0:T(8,128)S(1)} %get-tuple-element.24.vb, f32[32,4096]{1,0:T(8,128)S(1)} %collective-permute-done.prev_ref, f32[32,4096]{1,0:T(8,128)S(1)} %collective-permute-done.1.next_ref, f32[4,8,4096]{2,1,0:T(8,128)S(1)} %get-tuple-element.20.early_ref, ...), custom_call_target="tpu_custom_call" | custom-call | tf_op jit(solution)/shard_map/pallas_call | solution.py:330
  38.6 1.7 %shard_map.40.mine_ref = f32[4,8,1024]{2,1,0:T(8,128)S(1)} custom-call(f32[34,32,48,128]{3,2,1,0:T(8,128)S(1)} %get-tuple-element.24.vb, f32[32,4096]{1,0:T(8,128)S(1)} %collective-permute-done.prev_ref, f32[32,4096]{1,0:T(8,128)S(1)} %collective-permute-done.1.next_ref, f32[24,8,128]{2,1,0:T(8,128)S(1)} %get-tuple-element.21.coef_ref), custom_call_target="tpu_custom_call" | custom-call | tf_op jit(solution)/shard_map/pallas_call | solution.py:330
  40.7 6.0 %collective-permute-done.7.refs_5_ = f32[4,8,1024]{2,1,0:T(8,128)S(1)} collective-permute-done((f32[4,8,1024]{2,1,0:T(8,128)S(1)}, f32[4,8,1024]{2,1,0:T(8,128)S(1)}, u32[]{:S(2)}, u32[]{:S(2)}) %collective-permute-start.7) | collective-permute-done | bytes 131104 | tf_op jit(solution)/shard_map/ppermute | solution.py:384
  46.8 2.4 %collective-permute-start.10 = (f32[4,24,512]{2,1,0:T(8,128)S(1)}, f32[4,24,512]{2,1,0:T(8,128)S(1)}, u32[]{:S(2)}, u32[]{:S(2)}) collective-permute-start(f32[4,24,512]{2,1,0:T(8,128)S(1)} %shard_map.45), channel_id=1, source_target_pairs={{0,96},{16,112},{32,64},{48,80},{64,32},{80,48},{96,0},{112,16},{1... | collective-permute-start | bytes 589832 | tf_op jit(solution)/shard_map/ppermute | solution.py:384
  49.1 0.8 %shard_map.46.refs_0_ = f32[4,8,512]{2,1,0:T(8,128)S(1)} custom-call(f32[34,32,48,128]{3,2,1,0:T(8,128)S(1)} %get-tuple-element.24.vb, f32[32,4096]{1,0:T(8,128)S(1)} %collective-permute-done.prev_ref, f32[32,4096]{1,0:T(8,128)S(1)} %collective-permute-done.1.next_ref, f32[24,8,128]{2,1,0:T(8,128)S(1)} %get-tuple-element.21.coef_ref), custom_call_target="tpu_custom_call" | custom-call | tf_op jit(solution)/shard_map/pallas_call | solution.py:330
  50.0 1.3 %collective-permute-start.11 = (f32[4,8,512]{2,1,0:T(8,128)S(1)}, f32[4,8,512]{2,1,0:T(8,128)S(1)}, u32[]{:S(2)}, u32[]{:S(2)}) collective-permute-start(f32[4,8,512]{2,1,0:T(8,128)S(1)} %shard_map.47), channel_id=1, source_target_pairs={{0,96},{16,112},{32,64},{48,80},{64,32},{80,48},{96,0},{112,16},{1... | collective-permute-start | bytes 196616 | tf_op jit(solution)/shard_map/ppermute | solution.py:384
  51.4 0.8 %shard_map.39.refs_6_ = f32[4,8,512]{2,1,0:T(8,128)S(1)} custom-call(f32[34,32,48,128]{3,2,1,0:T(8,128)S(1)} %get-tuple-element.24.vb, f32[32,4096]{1,0:T(8,128)S(1)} %collective-permute-done.prev_ref, f32[32,4096]{1,0:T(8,128)S(1)} %collective-permute-done.1.next_ref, f32[24,8,128]{2,1,0:T(8,128)S(1)} %get-tuple-element.21.coef_ref), custom_call_target="tpu_custom_call" | custom-call | tf_op jit(solution)/shard_map/pallas_call | solution.py:330
  52.2 0.9 %shard_map.37.refs_3_ = f32[4,8,512]{2,1,0:T(8,128)S(1)} custom-call(f32[34,32,48,128]{3,2,1,0:T(8,128)S(1)} %get-tuple-element.24.vb, f32[32,4096]{1,0:T(8,128)S(1)} %collective-permute-done.prev_ref, f32[32,4096]{1,0:T(8,128)S(1)} %collective-permute-done.1.next_ref, f32[24,8,128]{2,1,0:T(8,128)S(1)} %get-tuple-element.21.coef_ref), custom_call_target="tpu_custom_call" | custom-call | tf_op jit(solution)/shard_map/pallas_call | solution.py:330
  53.1 1.0 %shard_map.34.refs_0_ = f32[4,16,512]{2,1,0:T(8,128)S(1)} custom-call(f32[34,32,48,128]{3,2,1,0:T(8,128)S(1)} %get-tuple-element.24.vb, f32[32,4096]{1,0:T(8,128)S(1)} %collective-permute-done.prev_ref, f32[32,4096]{1,0:T(8,128)S(1)} %collective-permute-done.1.next_ref, f32[4,8,4096]{2,1,0:T(8,128)S(1)} %get-tuple-element.20.early_ref, ...), custom_call_target="tpu_custom_call" | custom-call | tf_op jit(solution)/shard_map/pallas_call | solution.py:330
  54.2 1.4 %collective-permute-done.11.refs_1_ = f32[4,8,512]{2,1,0:T(8,128)S(1)} collective-permute-done((f32[4,8,512]{2,1,0:T(8,128)S(1)}, f32[4,8,512]{2,1,0:T(8,128)S(1)}, u32[]{:S(2)}, u32[]{:S(2)}) %collective-permute-start.11) | collective-permute-done | bytes 65568 | tf_op jit(solution)/shard_map/ppermute | solution.py:384
  55.6 0.7 %shard_map.48 = f32[4,32,512]{2,1,0:T(8,128)} custom-call(f32[4,32,512]{2,1,0:T(8,128)S(1)} %shard_map.42.mine_ref, f32[4,24,512]{2,1,0:T(8,128)S(1)} %collective-permute-done.10.refs_0_, f32[4,8,512]{2,1,0:T(8,128)S(1)} %collective-permute-done.11.refs_1_), custom_call_target="tpu_custom_call" | custom-call | tf_op jit(solution)/shard_map/pallas_call | solution.py:330
  (21 shorter events, 1.1 us)
Async XLA Ops:
  1.6 17.2 %collective-permute-start = (f32[32,4096]{1,0:T(8,128)S(1)}, f32[32,4096]{1,0:T(8,128)S(1)}, u32[]{:S(2)}, u32[]{:S(2)}) collective-permute-start(f32[32,4096]{1,0:T(8,128)S(1)} %get-tuple-element.17), channel_id=1, source_target_pairs={{0,16},{16,32},{32,48},{48,64},{64,80},{80,96},{96,112},{112,0},{1... | collective-permute-start | bytes 1572872 | tf_op jit(solution)/shard_map/ppermute | solution.py:349
  1.6 17.2 %collective-permute-start.1 = (f32[32,4096]{1,0:T(8,128)S(1)}, f32[32,4096]{1,0:T(8,128)S(1)}, u32[]{:S(2)}, u32[]{:S(2)}) collective-permute-start(f32[32,4096]{1,0:T(8,128)S(1)} %get-tuple-element.18), channel_id=1, source_target_pairs={{0,112},{16,0},{32,16},{48,32},{64,48},{80,64},{96,80},{112,96},{1... | collective-permute-start | bytes 1572872 | tf_op jit(solution)/shard_map/ppermute | solution.py:349
  5.2 19.3 %collective-permute-start.2 = (f32[32,4096]{1,0:T(8,128)S(1)}, f32[32,4096]{1,0:T(8,128)S(1)}, u32[]{:S(2)}, u32[]{:S(2)}) collective-permute-start(f32[32,4096]{1,0:T(8,128)S(1)} %get-tuple-element.19), channel_id=1, source_target_pairs={{0,1},{1,2},{2,3},{3,4},{4,5},{5,6},{6,7},{7,8},{8,9},{9,10},{10,1... | collective-permute-start | bytes 1572872 | tf_op jit(solution)/shard_map/ppermute | solution.py:349
  6.8 23.8 %collective-permute-start.3 = (f32[32,4096]{1,0:T(8,128)S(1)}, f32[32,4096]{1,0:T(8,128)S(1)}, u32[]{:S(2)}, u32[]{:S(2)}) collective-permute-start(f32[32,4096]{1,0:T(8,128)S(1)} %get-tuple-element.23), channel_id=1, source_target_pairs={{0,15},{1,0},{2,1},{3,2},{4,3},{5,4},{6,5},{7,6},{8,7},{9,8},{10,9... | collective-permute-start | bytes 1572872 | tf_op jit(solution)/shard_map/ppermute | solution.py:349
  22.6 12.0 %collective-permute-start.4 = (f32[4,16,2048]{2,1,0:T(8,128)S(1)}, f32[4,16,2048]{2,1,0:T(8,128)S(1)}, u32[]{:S(2)}, u32[]{:S(2)}) collective-permute-start(f32[4,16,2048]{2,1,0:T(8,128)S(1)} %shard_map.35), channel_id=1, source_target_pairs={{0,16},{16,0},{32,48},{48,32},{64,80},{80,64},{96,112},{112,96},{1... | collective-permute-start | bytes 1572872 | tf_op jit(solution)/shard_map/ppermute | solution.py:384
  28.4 6.5 %collective-permute-start.6 = (f32[4,8,2048]{2,1,0:T(8,128)S(1)}, f32[4,8,2048]{2,1,0:T(8,128)S(1)}, u32[]{:S(2)}, u32[]{:S(2)}) collective-permute-start(f32[4,8,2048]{2,1,0:T(8,128)S(1)} %get-tuple-element.25), channel_id=1, source_target_pairs={{0,16},{16,0},{32,48},{48,32},{64,80},{80,64},{96,112},{112,96},{1... | collective-permute-start | bytes 786440 | tf_op jit(solution)/shard_map/ppermute | solution.py:384
  34.4 6.0 %collective-permute-start.8 = (f32[4,8,2048]{2,1,0:T(8,128)S(1)}, f32[4,8,2048]{2,1,0:T(8,128)S(1)}, u32[]{:S(2)}, u32[]{:S(2)}) collective-permute-start(f32[4,8,2048]{2,1,0:T(8,128)S(1)} %get-tuple-element.26), channel_id=1, source_target_pairs={{0,16},{16,0},{32,48},{48,32},{64,80},{80,64},{96,112},{112,96},{1... | collective-permute-start | bytes 786440 | tf_op jit(solution)/shard_map/ppermute | solution.py:384
  34.6 12.1 %collective-permute-start.5 = (f32[4,16,1024]{2,1,0:T(8,128)S(1)}, f32[4,16,1024]{2,1,0:T(8,128)S(1)}, u32[]{:S(2)}, u32[]{:S(2)}) collective-permute-start(f32[4,16,1024]{2,1,0:T(8,128)S(1)} %shard_map.36), channel_id=1, source_target_pairs={{0,32},{16,48},{32,0},{48,16},{64,96},{80,112},{96,64},{112,80},{1... | collective-permute-start | bytes 786440 | tf_op jit(solution)/shard_map/ppermute | solution.py:384
  34.9 11.8 %collective-permute-start.7 = (f32[4,8,1024]{2,1,0:T(8,128)S(1)}, f32[4,8,1024]{2,1,0:T(8,128)S(1)}, u32[]{:S(2)}, u32[]{:S(2)}) collective-permute-start(f32[4,8,1024]{2,1,0:T(8,128)S(1)} %shard_map.38), channel_id=1, source_target_pairs={{0,32},{16,48},{32,0},{48,16},{64,96},{80,112},{96,64},{112,80},{1... | collective-permute-start | bytes 393224 | tf_op jit(solution)/shard_map/ppermute | solution.py:384
  40.4 9.5 %collective-permute-start.9 = (f32[4,8,1024]{2,1,0:T(8,128)S(1)}, f32[4,8,1024]{2,1,0:T(8,128)S(1)}, u32[]{:S(2)}, u32[]{:S(2)}) collective-permute-start(f32[4,8,1024]{2,1,0:T(8,128)S(1)} %shard_map.41), channel_id=1, source_target_pairs={{0,32},{16,48},{32,0},{48,16},{64,96},{80,112},{96,64},{112,80},{1... | collective-permute-start | bytes 393224 | tf_op jit(solution)/shard_map/ppermute | solution.py:384
  46.8 8.8 %collective-permute-start.10 = (f32[4,24,512]{2,1,0:T(8,128)S(1)}, f32[4,24,512]{2,1,0:T(8,128)S(1)}, u32[]{:S(2)}, u32[]{:S(2)}) collective-permute-start(f32[4,24,512]{2,1,0:T(8,128)S(1)} %shard_map.45), channel_id=1, source_target_pairs={{0,96},{16,112},{32,64},{48,80},{64,32},{80,48},{96,0},{112,16},{1... | collective-permute-start | bytes 589832 | tf_op jit(solution)/shard_map/ppermute | solution.py:384
  50.0 5.6 %collective-permute-start.11 = (f32[4,8,512]{2,1,0:T(8,128)S(1)}, f32[4,8,512]{2,1,0:T(8,128)S(1)}, u32[]{:S(2)}, u32[]{:S(2)}) collective-permute-start(f32[4,8,512]{2,1,0:T(8,128)S(1)} %shard_map.47), channel_id=1, source_target_pairs={{0,96},{16,112},{32,64},{48,80},{64,32},{80,48},{96,0},{112,16},{1... | collective-permute-start | bytes 196616 | tf_op jit(solution)/shard_map/ppermute | solution.py:384
